TPU v7x, 128 devices: a whole 4x4x4 slice. The times are simulated.
128 devices in a mesh: rows: 16 (over x, z_hi, core), cols: 8 (over y, z_lo).
Axes of the slice: x: 4, y: 4, z: 4 (z_hi: 2, z_lo: 2; z = z_hi * 2 + z_lo), core: 2. Of those that a mesh axis runs over, the one named last changes fastest.
Arguments:
- values: float32 [256, 64, 32, 128], P(None, 'rows', 'cols'), may hold values from -6 to 6
- offsets: float32 [2, 64, 32, 128], P(None, 'rows', 'cols'), may hold values from 0 to 1
- nugget: float32 [64, 32, 128], P('rows', 'cols'), may hold values from 0.8 to 2.5
- neighbours: int32 [64, 32, 256], P('rows', 'cols'), may hold values from 0 to 262143, as said below
- length_scale: float32 [1], replicated, may hold values from 2.5 to 5
- target_tile: int32 [65536, 1], P(('rows', 'cols')), may hold values from 0 to 15; in each aligned block of 512 rows (0 to 511, 512 to 1023, ...) at most 64 rows name the same one
- target_spots: float32 [2, 65536], P(None, ('rows', 'cols')), may hold values from 0 to 1
Outputs:
- whitened: float32 [64, 32, 128, 256], P('rows', 'cols')
- cluster_terms: float32 [64, 32], P('rows', 'cols')
- predictions: float32 [65536, 256], P(('rows', 'cols'))
Inputs may be any that keep to these rules, and one draw needn't show every extreme that they name: `neighbours`: each cluster's 256 entries are distinct points of other clusters whose two grid coordinates each differ from the cluster's own by at most 2. `target_tile`: at most 64 of the 512 targets of one device name the same tile, and in every draw some tile is named exactly 64 times by the targets of some device.
All inputs are finite; a program needn't handle non-finite values.
Results may differ from a plain program's by a relative error of at most 0.0052.
Values may be sent and summed in bfloat16 or wider, within the bound.
No kernel may reach another device: no remote copies, remote signals or barrier semaphores. Data moves between devices by JAX's collectives and lax.ppermute only.
A program may use at most 256 MiB of HBM per device.

v0:
```python
import math

import jax
import jax.numpy as jnp

from jax import lax
from jax.experimental import pallas as pl
from jax.experimental.pallas import tpu as pltpu
from jax.sharding import PartitionSpec as P

F32 = jnp.float32
BF = jnp.bfloat16
NN = (((1,), (0,)), ((), ()))
NT = (((1,), (1,)), ((), ()))
TN = (((0,), (0,)), ((), ()))


def split(x):
    hi = x.astype(BF)
    return hi, (x - hi.astype(F32)).astype(BF)


def dot(a, b, dims):
    return lax.dot_general(a, b, dims, preferred_element_type=F32)


def mm_nt(a, b):
    ah, al = split(a)
    bh, bl = split(b)
    return dot(jnp.concatenate([ah, ah, al], 1), jnp.concatenate([bh, bl, bh], 1), NT)


def mm_nn(a, b):
    ah, al = split(a)
    bh, bl = split(b)
    return dot(jnp.concatenate([ah, ah, al], 1), jnp.concatenate([bh, bl, bh], 0), NN)


def lane_take(x, idx):
    return jnp.take_along_axis(x, idx, axis=1, mode="promise_in_bounds")


def recip(p):
    r = pl.reciprocal(p, approx=True)
    return r * (2.0 - p * r)


def leaf_factor(leaf, lane, sub):
    base = lane & 96
    col = lane & 31
    x = [list(p) for p in leaf]
    ones = jnp.ones((8, 128), F32)
    piv = [[[ones, jnp.zeros((8, 128), F32), ones] for _ in range(4)] for _ in range(4)]

    def spread_row(t, s):
        return jnp.broadcast_to(t[s : s + 1, :], (8, 128))

    for j in range(0, 32, 2):
        v0, s0 = divmod(j, 8)
        first, second = base + j, base + j + 1
        unit0 = jnp.where(col == j, 1.0, 0.0)
        unit1 = jnp.where(col == j + 1, 1.0, 0.0)
        below = sub > s0 + 1
        here = (sub == s0) | (sub == s0 + 1)
        for p in range(4):
            c0 = [lane_take(x[p][v], first) for v in range(v0, 4)]
            c1 = [lane_take(x[p][v], second) for v in range(v0, 4)]
            a, b, d = spread_row(c0[0], s0), spread_row(c0[0], s0 + 1), spread_row(c1[0], s0 + 1)
            r = recip(a * d - b * b)
            r0 = spread_row(x[p][v0], s0) + unit0
            r1 = spread_row(x[p][v0], s0 + 1) + unit1
            w0 = d * r0 - b * r1
            w1 = a * r1 - b * r0
            for i, new in enumerate((a, b, d)):
                piv[p][v0][i] = jnp.where(here, new, piv[p][v0][i])
            for v in range(v0, 4):
                if v == v0 and s0 == 6:
                    continue
                t = c0[v - v0] * w0 + c1[v - v0] * w1
                if v == v0:
                    t = jnp.where(below, t, 0.0)
                x[p][v] = x[p][v] - t * r
    odd = (sub & 1) == 1
    out = []
    for p in range(4):
        o = []
        for v in range(4):
            a, b, d = piv[p][v]
            f = jnp.where(odd, b * recip(a), 0.0)
            e = jnp.where(odd, d - b * f, a)
            q = lax.rsqrt(e)
            q = q * (1.5 - 0.5 * e * q * q)
            r_i = sub + 8 * v
            n = jnp.where(col < (r_i & 30), x[p][v], jnp.where(col == r_i, 1.0, 0.0))
            o.append(q * (n - f * pltpu.roll(n, 1, axis=0)))
        out.append(o)
    return out


def inv_chol(xw, wp, count):
    lane8 = lax.broadcasted_iota(jnp.int32, (8, 128), 1)
    sub8 = lax.broadcasted_iota(jnp.int32, (8, 128), 0)
    lane = lax.broadcasted_iota(jnp.int32, (32, 128), 1)
    subl = lax.broadcasted_iota(jnp.int32, (32, 128), 0)
    for k in range(4):
        lo = 32 * k
        for base in range(0, count, 16):
            leaf = []
            for p in range(4):
                tiles = []
                for v in range(4):
                    acc = None
                    for g in range(4):
                        t = xw[base + 4 * p + g, lo + 8 * v : lo + 8 * v + 8, :]
                        t = pltpu.roll(t, (32 * (g - k)) % 128, axis=1) if g != k else t
                        acc = t if acc is None else jnp.where(lane8 // 32 == g, t, acc)
                    tiles.append(acc)
                leaf.append(tiles)
            inv = leaf_factor(leaf, lane8, sub8)
            for p in range(4):
                for v in range(4):
                    wp[p, 8 * v : 8 * v + 8, :] = inv[p][v]

            def apply(q, _):
                cs = [base + 8 * q + e for e in range(8)]
                xs = [xw[c] for c in cs]
                ws = [wp[2 * q], wp[2 * q + 1]]
                ts = []
                for e in range(8):
                    g = e % 4
                    gi = 32 * g + (lane8 & 31)
                    w = ws[e // 4]
                    wr = jnp.concatenate(
                        [lane_take(w[8 * v : 8 * v + 8], gi) for v in range(4)], 0
                    )
                    wh = wr.astype(BF).astype(F32)
                    lhs = jnp.where(lane < 64, wh, wr - wh).astype(BF)
                    r = xs[e][lo : lo + 32, :]
                    r = jnp.where(lane // 32 == k, jnp.where((lane & 31) == subl, 1.0, 0.0), r)
                    rh, rl = split(r)
                    ts.append(dot(lhs, jnp.concatenate([rh, rl, rh, rl], 0), NN))
                if k < 3:
                    n = 96 - lo
                    ln = lax.broadcasted_iota(jnp.int32, (n, 128), 1)
                    ls = []
                    for e in range(8):
                        g = e % 4
                        w = ws[e // 4]
                        w = pltpu.roll(w, (32 * (k - g)) % 128, axis=1) if g != k else w
                        w = jnp.where(lane // 32 == k, w, 0.0)
                        wh, wl = split(w)
                        wh = jnp.concatenate([wh] * 4, 0)
                        wl = jnp.concatenate([wl] * 4, 0)
                        xh, xl = split(xs[e][lo + 32 :, :])
                        ls.append(
                            dot(
                                jnp.concatenate([xh, xl, xh], 1),
                                jnp.concatenate([wh, wh, wl], 1),
                                NT,
                            )
                        )
                    us = []
                    for e in range(8):
                        lh = ls[e].astype(BF).astype(F32)
                        lhs = jnp.where(ln < 64, lh, ls[e] - lh).astype(BF)
                        th, tl = split(ts[e])
                        us.append(dot(lhs, jnp.concatenate([th, tl, th, tl], 0), NN))
                for e in range(8):
                    c = cs[e]
                    xw[c, lo : lo + 32, :] = jnp.where(lane < lo + 32, ts[e], 0.0)
                    if k < 3:
                        rest = xs[e][lo + 32 :, :]
                        xw[c, lo + 32 :, :] = jnp.where(ln // 32 == k, 0.0, rest) - us[e]
                return 0

            lax.fori_loop(0, 2, apply, 0)


def window(first, nb, c):
    ci, cj = c // 4, c % 4
    idx = nb[ci, pl.ds(cj, 1), :]
    gx = idx >> 12
    gy = (idx >> 7) & 31
    w = (gx - (first[0] + ci) + 2) * 5 + (gy - (first[1] + cj) + 2)
    return ci, cj, w, idx & 127


def first_kernel(first, length, nb, geo, xw, cc, tt, wp, mid):
    count = 16
    lane8 = lax.broadcasted_iota(jnp.int32, (8, 128), 1)
    sub8 = lax.broadcasted_iota(jnp.int32, (8, 128), 0)
    scale = math.sqrt(3.0) / length[0]
    eye = (
        lax.broadcasted_iota(jnp.int32, (128, 128), 0)
        == lax.broadcasted_iota(jnp.int32, (128, 128), 1)
    )

    def covariance(c, _):
        ci, cj, w, member = window(first, nb, c)
        parts = []
        for h in range(2):
            wb = jnp.broadcast_to(w[:, 128 * h : 128 * h + 128], (8, 128))
            mb = jnp.broadcast_to(member[:, 128 * h : 128 * h + 128], (8, 128))
            acc = jnp.zeros((8, 128), F32)
            for wi in range(5):
                for wj in range(5):
                    if wi == 2 and wj == 2:
                        continue
                    shift = jnp.where(
                        sub8 == 0, float(wi - 2), jnp.where(sub8 == 1, float(wj - 2), 0.0)
                    )
                    t = lane_take(geo[ci + wi, cj + wj], mb) + shift
                    acc = jnp.where(wb == wi * 5 + wj, t, acc)
            parts.append(acc)
        parts.append(geo[ci + 2, cj + 2])
        pts = jnp.concatenate(parts, 1)
        cols = jnp.transpose(pts * scale)
        rows = pts * scale

        def block(a, b):
            dx = cols[128 * a : 128 * a + 128, 0:1] - rows[0:1, 128 * b : 128 * b + 128]
            dy = cols[128 * a : 128 * a + 128, 1:2] - rows[1:2, 128 * b : 128 * b + 128]
            s2 = dx * dx + dy * dy
            s = s2 * lax.rsqrt(jnp.maximum(s2, 1e-30))
            k = (1.0 + s) * jnp.exp(-s)
            if a == b:
                k = k + jnp.where(eye, pts[2:3, 128 * b : 128 * b + 128], 0.0)
            return k

        xw[c] = block(0, 0)
        cc[c, :128, :] = block(1, 0)
        cc[c, 128:, :] = block(2, 0)
        mid[c] = block(1, 1)
        tt[c, :, :128] = block(2, 1)
        tt[c, :, 128:] = block(2, 2)
        return 0

    lax.fori_loop(0, count, covariance, 0)
    inv_chol(xw, wp, count)

    def level1(q, _):
        cs = [4 * q + e for e in range(4)]
        w1 = [xw[c] for c in cs]
        p = [mm_nt(cc[c], w) for c, w in zip(cs, w1)]
        u = [mm_nt(a, a) for a in p]
        v = [mm_nn(a, w) for a, w in zip(p, w1)]
        for e, c in enumerate(cs):
            cc[c] = v[e]
            xw[c] = mid[c] - u[e][:128, :128]
            tt[c] = tt[c] - u[e][128:, :]
        return 0

    lax.fori_loop(0, count // 4, level1, 0)

def rest_kernel(x_in, cc, tt, g_out, w3_out, xw, wp, l32s):
    count = 16
    xw[...] = x_in[...]

    def level2(q, _):
        cs = [4 * q + e for e in range(4)]
        w2 = [xw[c] for c in cs]
        l32 = [mm_nt(tt[c, :, :128], w) for c, w in zip(cs, w2)]
        u = [mm_nt(a, a) for a in l32]
        v = [mm_nn(a, w) for a, w in zip(l32, w2)]
        for e, c in enumerate(cs):
            l32s[c] = v[e]
            xw[c] = tt[c, :, 128:] - u[e]
        return 0

    def level(b, _):
        inv_chol(xw, wp, count)

        @pl.when(b == 0)
        def _():
            lax.fori_loop(0, count // 4, level2, 0)

        return 0

    lax.fori_loop(0, 2, level, 0)

    def last(q, _):
        cs = [4 * q + e for e in range(4)]
        w3 = [xw[c] for c in cs]
        q2 = [l32s[c] for c in cs]
        q1 = [cc[c, 128:, :] - mm_nn(b, cc[c, :128, :]) for c, b in zip(cs, q2)]
        gb = [
            mm_nn(w, jnp.concatenate([a, b], 1)).astype(BF)
            for w, a, b in zip(w3, q1, q2)
        ]
        for e, c in enumerate(cs):
            w3_out[c] = w3[e]
            g_out[c] = gb[e]
        return 0

    lax.fori_loop(0, count // 4, last, 0)


VM = pl.BlockSpec(memory_space=pltpu.VMEM)
SM = pl.BlockSpec(memory_space=pltpu.SMEM)


def factor_first(first, length, nb, geo):
    return pl.pallas_call(
        first_kernel,
        out_shape=(
            jax.ShapeDtypeStruct((16, 128, 128), F32),
            jax.ShapeDtypeStruct((16, 256, 128), F32),
            jax.ShapeDtypeStruct((16, 128, 256), F32),
        ),
        in_specs=[SM, SM, VM, VM],
        out_specs=(VM, VM, VM),
        scratch_shapes=[pltpu.VMEM((4, 32, 128), F32), pltpu.VMEM((16, 128, 128), F32)],
        compiler_params=pltpu.CompilerParams(vmem_limit_bytes=20 << 20),
        name="factor_first",
    )(first, length, nb, geo)


def factor_rest(x, c, t):
    return pl.pallas_call(
        rest_kernel,
        out_shape=(
            jax.ShapeDtypeStruct((16, 128, 256), BF),
            jax.ShapeDtypeStruct((16, 128, 128), F32),
        ),
        in_specs=[VM, VM, VM],
        out_specs=(VM, VM),
        scratch_shapes=[
            pltpu.VMEM((16, 128, 128), F32),
            pltpu.VMEM((4, 32, 128), F32),
            pltpu.VMEM((16, 128, 128), F32),
        ],
        compiler_params=pltpu.CompilerParams(vmem_limit_bytes=20 << 20),
        name="factor_rest",
    )(x, c, t)


def whiten_kernel(base, first, nb, north, mid, south, g, w3, own, white, weights, term, tab):
    step = pl.program_id(0) + base

    @pl.when(step == base)
    def _():
        tab[0:2] = north[...]
        tab[2:6] = mid[...]
        tab[6:8] = south[...]

    ci, cj, w, member = window(first, nb, step)
    start = pl.multiple_of(cj * 128, 128)
    acc = mm_nt(w3[0], own[0])
    gf = g[0].astype(F32)
    point = lax.broadcasted_iota(jnp.int32, (128, 256), 0)
    pick = jnp.where(point == jnp.broadcast_to(member, (128, 256)), 1.0, 0.0).astype(BF)
    for wi in range(5):
        lhs = jnp.concatenate(
            [jnp.where(w == wi * 5 + wj, gf, 0.0).astype(BF) for wj in range(5)], 0
        )
        gs = dot(lhs, pick, NT).astype(BF)
        gs = jnp.concatenate([gs[128 * wj : 128 * wj + 128, :] for wj in range(5)], 1)
        acc = acc - dot(gs, tab[ci + wi, :, pl.ds(start, 640)], NT)
    white[0] = acc
    weights[...] = acc.astype(BF)
    eye = (
        lax.broadcasted_iota(jnp.int32, (128, 128), 0)
        == lax.broadcasted_iota(jnp.int32, (128, 128), 1)
    )
    diag = jnp.sum(jnp.where(eye, w3[0], 0.0), axis=0, keepdims=True)
    total = 0.5 * jnp.sum(acc * acc) - 256.0 * jnp.sum(jnp.log(diag))
    term[...] = jnp.full((1, 8, 128), -total / 32768.0 - 0.5 * math.log(2.0 * math.pi), F32)


def whiten(first, nb, pieces, g, w3, own, base, white=None):
    def whole(a):
        nd = a.ndim
        return pl.BlockSpec(a.shape, lambda s: (0,) * nd, pipeline_mode=pl.Buffered(1))

    if white is None:
        kernel = lambda *refs: whiten_kernel(base, *refs)
    else:
        kernel = lambda *refs: whiten_kernel(base, *refs[:8], *refs[9:])
    extra = [] if white is None else [white]
    return pl.pallas_call(
        kernel,
        grid=(8,),
        out_shape=(
            jax.ShapeDtypeStruct((16, 128, 256), F32),
            jax.ShapeDtypeStruct((1024, 256), BF),
            jax.ShapeDtypeStruct((8, 8, 128), F32),
        ),
        in_specs=[SM, whole(nb)]
        + [whole(p) for p in pieces]
        + [
            pl.BlockSpec((1, 128, 256), lambda s: (s + base, 0, 0)),
            pl.BlockSpec((1, 128, 128), lambda s: (s + base, 0, 0)),
            pl.BlockSpec((1, 256, 128), lambda s: ((s + base) // 4, 0, (s + base) % 4)),
        ]
        + [pl.BlockSpec(memory_space=pl.ANY) for _ in extra],
        out_specs=(
            pl.BlockSpec((1, 128, 256), lambda s: (s + base, 0, 0)),
            pl.BlockSpec((128, 256), lambda s: (s, 0)),
            pl.BlockSpec((1, 8, 128), lambda s: (s, 0, 0)),
        ),
        input_output_aliases={} if white is None else {8: 0},
        scratch_shapes=[pltpu.VMEM((8, 256, 1024), BF)],
        compiler_params=pltpu.CompilerParams(vmem_limit_bytes=24 << 20),
        name="whiten",
    )(first, nb, *pieces, g, w3, own, *extra)


LN2 = math.log(2.0)
TB = 1024


def pieces3(x):
    a = x.astype(BF).astype(F32)
    r = x - a
    b = r.astype(BF).astype(F32)
    return a, b, r - b


def cross_kernel(scale, tgt, pts, wa, wb, acc_in, out, rhs, total):
    def form(x, y, left):
        q = x * x + y * y
        qs = pieces3(q)
        ones = jnp.ones_like(x)
        xs, ys = pieces3(x), pieces3(y)
        m = -2.0 if left else 1.0
        rows = []
        for a, b in ((0, 0), (0, 1), (1, 0), (0, 2), (1, 1), (2, 0)):
            k = a if left else b
            rows += [xs[k] * m, ys[k] * m]
        rows += (list(qs) + [ones] * 3) if left else ([ones] * 3 + list(qs))
        rows += [jnp.zeros_like(x)] * 14
        return jnp.concatenate(rows, 0).astype(BF)

    @pl.when(pl.program_id(0) == 0)
    def _():
        rhs[...] = form(pts[0:1, :] * scale[0], pts[1:2, :] * scale[0], False)

    lhs = form(tgt[0, 0:1, :] * scale[0], tgt[0, 1:2, :] * scale[0], True)
    total[...] = acc_in[...] if acc_in is not None else jnp.zeros((TB, 256), F32)

    def chunk(b, _):
        acc = total[...]
        for w in (wa, wb):
            at = b * 256 + (1024 if w is wb else 0)
            s2 = jnp.maximum(dot(lhs, rhs[:, pl.ds(pl.multiple_of(at, 256), 256)], TN), 1e-30)
            s = s2 * lax.rsqrt(s2)
            k = (1.0 + s * LN2) * jnp.exp2(-s)
            acc = acc + dot(k.astype(BF), w[pl.ds(pl.multiple_of(b * 256, 256), 256), :], NN)
        total[...] = acc
        return 0

    lax.fori_loop(0, 4, chunk, 0)
    out[...] = total[...].astype(out.dtype)


def cross(scale, tgt, pts, w, dtype, acc=None, skip=0, name="cross"):
    n = tgt.shape[0]
    kernel = cross_kernel
    if acc is None:
        kernel = lambda s, t, p, a, b, o, r, m: cross_kernel(s, t, p, a, b, None, o, r, m)
    return pl.pallas_call(
        kernel,
        grid=(n,),
        out_shape=jax.ShapeDtypeStruct((n * TB, 256), dtype),
        in_specs=[
            pl.BlockSpec(memory_space=pltpu.SMEM),
            pl.BlockSpec((1, 2, TB), lambda s: (s, 0, 0)),
            pl.BlockSpec((2, 2048), lambda s: (0, 0)),
            pl.BlockSpec((1024, 256), lambda s: (0, 0)),
            pl.BlockSpec((1024, 256), lambda s: (0, 0)),
        ]
        + ([] if acc is None else [pl.BlockSpec((TB, 256), lambda s: (skip + s, 0))]),
        out_specs=pl.BlockSpec((TB, 256), lambda s: (s, 0)),
        scratch_shapes=[pltpu.VMEM((32, 2048), BF), pltpu.VMEM((TB, 256), F32)],
        compiler_params=pltpu.CompilerParams(vmem_limit_bytes=24 << 20),
        name=name,
    )(scale, tgt, pts, *w, *([] if acc is None else [acc]))


def sides(low, high, axis):
    count = lax.axis_size(axis)
    forward = [(i, i + 1) for i in range(count - 1)]
    backward = [(b, a) for a, b in forward]
    return lax.ppermute(high, axis, forward), lax.ppermute(low, axis, backward)


def body(values, offsets, nugget, neighbours, length_scale, target_tile, target_spots):
    row = lax.axis_index("rows")
    col = lax.axis_index("cols")
    length = length_scale[0]
    first = jnp.stack([row * 4, col * 4]).astype(jnp.int32)

    geo = jnp.concatenate(
        [offsets.transpose(1, 2, 0, 3), nugget[:, :, None, :], jnp.zeros((4, 4, 5, 128), F32)], 2
    )
    w, e = sides(geo[:, :2], geo[:, 2:], "cols")
    geo = jnp.concatenate([w, geo, e], 1)
    n, s = sides(geo[:2], geo[2:], "rows")
    geo = jnp.concatenate([n, geo, s], 0)

    own = values.transpose(1, 0, 2, 3).reshape(4, 256, 512)
    mid = own.astype(BF)
    w, e = sides(mid[:, :, :256], mid[:, :, 256:], "cols")

    tile_ids = target_tile[:, 0]
    one_hot = (tile_ids[:, None] == jnp.arange(16, dtype=jnp.int32)[None, :]).astype(jnp.int32)
    rank = jnp.sum((jnp.cumsum(one_hot, axis=0) - 1) * one_hot, axis=1)
    slot = tile_ids * 64 + rank
    send_x = jnp.zeros((1024,), F32).at[slot].set(target_spots[0])
    send_y = jnp.zeros((1024,), F32).at[slot].set(target_spots[1])
    outgoing = jnp.concatenate([send_x.reshape(16, 64), send_y.reshape(16, 64)], axis=1)
    everyone = jnp.broadcast_to(outgoing[:, None, :], (16, 8, 128)).reshape(128, 1, 128)
    spots = lax.all_to_all(everyone, ("rows", "cols"), split_axis=0, concat_axis=0, tiled=True)
    spots = spots.reshape(16, 8, 2, 64).transpose(1, 2, 0, 3).reshape(4, 2, 2, 1024)
    band, half = col // 2, col % 2
    spots = lax.dynamic_index_in_dim(spots, half, 1, keepdims=False)
    spots = jnp.take(spots, (band + jnp.array([2, 1, 3, 0], jnp.int32)) % 4, axis=0)
    mid_y = (band * 8 + 4).astype(F32)
    tgt = jnp.stack([spots[:, 0] * 4.0 - 2.0, spots[:, 1] * 32.0 - mid_y], 1)
    tgt = tgt.reshape(4, 2, 1024 // TB, TB).transpose(0, 2, 1, 3).reshape(-1, 2, TB)
    px = offsets[0] + (jnp.arange(4, dtype=F32) - 2.0)[:, None, None]
    py = offsets[1] + (jnp.arange(4, dtype=F32) - 4.0 + 4.0 * half.astype(F32))[None, :, None]
    pts = jnp.stack([px.reshape(-1), py.reshape(-1)])
    partner = [(c, c ^ 1) for c in range(8)]
    pts2 = lax.ppermute(pts, "cols", partner)

    state = factor_first(first, length_scale, neighbours, geo)
    mid = jnp.concatenate([w, mid, e], 2)
    *state, mid = lax.optimization_barrier((*state, mid))
    n, s = sides(mid[:2], mid[2:], "rows")
    around = [n, mid, s]
    g, w3 = factor_rest(*state)
    white, w_a, term_a = whiten(first, neighbours, around, g, w3, own, 0)
    far_a = lax.ppermute(w_a, "cols", partner)
    white, w_b, term_b = whiten(first, neighbours, around, g, w3, own, 8, white)
    far_b = lax.ppermute(w_b, "cols", partner)
    term = jnp.concatenate([term_a[:, 0, 0], term_b[:, 0, 0]])

    scale = jnp.stack([math.sqrt(3.0) / LN2 / length])
    near = cross(scale, tgt, pts, (w_a, w_b), F32, name="cross_near")
    per = 1024 // TB
    parts = []
    for i, k in enumerate((2, 1, 3)):
        part = cross(
            scale, tgt[per * i : per * i + per], pts2, (far_a, far_b), BF, near, per * i, "cross_far"
        )
        parts.append(lax.ppermute(part, "cols", [(c, (c + 2 * k) % 8) for c in range(8)]))
    here = cross(scale, tgt[3 * per :], pts2, (far_a, far_b), F32, near, 3 * per, "cross_here")
    predicted = here + (parts[0].astype(F32) + parts[1].astype(F32) + parts[2].astype(F32))
    predicted = (predicted * (1.0 / 128.0)).astype(BF)
    returned = lax.all_to_all(
        predicted.reshape(16, 64, 256), "rows", split_axis=0, concat_axis=0, tiled=True
    )
    predictions = returned.reshape(-1, 256)[slot].astype(F32)
    return (white.reshape(4, 4, 128, 256), term.reshape(4, 4), predictions)


def solution(mesh):
    return jax.shard_map(
        body,
        mesh=mesh,
        in_specs=(
            P(None, "rows", "cols", None),
            P(None, "rows", "cols", None),
            P("rows", "cols", None),
            P("rows", "cols", None),
            P(),
            P(("rows", "cols"), None),
            P(None, ("rows", "cols")),
        ),
        out_specs=(P("rows", "cols", None, None), P("rows", "cols"), P(("rows", "cols"), None)),
        check_vma=False,
    )
```

profile of v0, /device:TPU:1, one launch (start us, length us, event | category | flops | bytes accessed | tf_op | source)
XLA Modules:
  0.0 228.2 jit_solution(16204330680006420790)
XLA Ops:
  0.6 0.7 copy.31
  1.4 0.7 pad_maximum_fusion.3
  2.1 4.4 %collective-permute-start = (f32[4,2,8,128]{3,2,1,0:T(8,128)S(1)}, f32[4,2,8,128]{3,2,1,0:T(8,128)S(1)}, u32[]{:S(2)}, u32[]{:S(2)}) collective-permute-start(f32[4,2,8,128]{3,2,1,0:T(8,128)S(1)} %get-tuple-element.41), channel_id=1, source_target_pairs={{0,1},{1,2},{2,3},{3,4},{4,5},{5,6},{6,7},{8,9},{9,10},{10,11},{11... | collective-permute-start | bytes 98312 | tf_op jit(solution)/shard_map/ppermute | solution.py:484
  6.5 1.3 collective-permute-start.1
  7.8 2.5 %reshape.156 = f32[4,256,512]{2,0,1:T(4,128)S(1)} reshape(f32[4,256,4,128]{3,2,0,1:T(4,128)} %bitcast.44) | data formatting | bytes 4194304 | tf_op jit(solution)/shard_map/reshape | solution.py:501
  10.9 1.0 fusion.15
  12.0 4.0 %collective-permute-start.4 = (bf16[4,256,256]{2,1,0:T(8,128)(2,1)}, bf16[4,256,256]{2,1,0:T(8,128)(2,1)S(1)}, u32[]{:S(2)}, u32[]{:S(2)}) collective-permute-start(bf16[4,256,256]{2,1,0:T(8,128)(2,1)} %get-tuple-element.37), channel_id=1, source_target_pairs={{0,1},{1,2},{2,3},{3,4},{4,5},{5,6},{6,7},{8,9},{9,10},{10,11},{11... | collective-permute-start | bytes 1572872 | tf_op jit(solution)/shard_map/ppermute | solution.py:484
  16.0 1.3 collective-permute-start.5
  17.3 1.2 reduce-window.6
  18.8 2.4 %scatter_custom_fusion = f32[1024]{0:T(1024)S(1)} fusion(s32[512]{0:T(512)S(1)} %bitcast.59, f32[512]{0:T(512)S(1)} %bitcast.64, f32[]{:T(128)} %constant.85.clone.1), kind=kCustom, calls=%fused_computation.50 | custom fusion | bytes 4100 | tf_op jit(solution)/shard_map/scatter | solution.py:509
  21.4 2.4 %scatter_custom_fusion.1 = f32[1024]{0:T(1024)S(1)} fusion(s32[512]{0:T(512)S(1)} %bitcast.60, f32[512]{0:T(512)S(1)} %bitcast.63, f32[]{:T(128)} %constant.85.clone.1), kind=kCustom, calls=%fused_computation.48 | custom fusion | bytes 4100 | tf_op jit(solution)/shard_map/scatter | solution.py:510
  24.6 13.8 %all-to-all-start = ((f32[128,1,128]{2,1,0:T(1,128)}), f32[128,1,128]{2,1,0:T(1,128)S(1)}, u32[]{:S(2)}, u32[]{:S(2)}) async-start(f32[128,1,128]{2,1,0:T(1,128)} %bitcast.13), calls=%async_computation | async-start | bytes 131072 | tf_op jit(solution)/shard_map/all_to_all | solution.py:513
  39.2 5.4 %collective-permute-start.2 = (f32[2,8,8,128]{3,2,1,0:T(8,128)S(1)}, f32[2,8,8,128]{3,2,1,0:T(8,128)S(1)}, u32[]{:S(2)}, u32[]{:S(2)}) collective-permute-start(f32[2,8,8,128]{3,2,1,0:T(8,128)S(1)} %get-tuple-element.39), channel_id=1, source_target_pairs={{0,8},{8,16},{16,24},{24,32},{32,40},{40,48},{48,56},{56,64},{64,7... | collective-permute-start | bytes 196616 | tf_op jit(solution)/shard_map/ppermute | solution.py:484
  44.6 1.9 collective-permute-start.3
  46.7 5.1 %collective-permute-done.3 = f32[2,8,8,128]{3,2,1,0:T(8,128)S(1)} collective-permute-done((f32[2,8,8,128]{3,2,1,0:T(8,128)S(1)}, f32[2,8,8,128]{3,2,1,0:T(8,128)S(1)}, u32[]{:S(2)}, u32[]{:S(2)}) %collective-permute-start.3) | collective-permute-done | bytes 65568 | tf_op jit(solution)/shard_map/ppermute | solution.py:484
  51.8 24.3 %factor_first.1 = (f32[16,128,128]{2,1,0:T(8,128)S(1)}, f32[16,256,128]{2,1,0:T(8,128)S(1)}, f32[16,128,256]{2,1,0:T(8,128)S(1)}) custom-call(s32[2]{0:T(128)S(1)} %pad_add_fusion.first.refs_0_, f32[1]{0:T(128)S(6)} %copy.33.length, s32[4,4,256]{2,1,0:T(4,128)S(1)} %copy-done.7, f32[8,8,8,128]{3,2,1,0:T(8,128)S(1)} %pad_maximum_fusion.1.geo), custom_call_target="tpu_custom_call" | custom-call | tf_op jit(solution)/shard_map/factor_first/pallas_call | solution.py:303
  76.1 1.3 copy-done.1
  77.4 1.3 copy-done.3
  78.7 1.0 copy-done.5
  79.7 0.8 copy-done.10
  80.5 1.5 pad_maximum_fusion.refs_3_
  82.0 1.5 fusion.14
  83.5 1.9 collective-permute-start.6
  85.4 2.5 %collective-permute-start.7 = (bf16[2,256,1024]{2,1,0:T(8,128)(2,1)}, bf16[2,256,1024]{2,1,0:T(8,128)(2,1)}, u32[]{:S(2)}, u32[]{:S(2)}) collective-permute-start(bf16[2,256,1024]{2,1,0:T(8,128)(2,1)} %get-tuple-element.35), channel_id=1, source_target_pairs={{8,0},{16,8},{24,16},{32,24},{40,32},{48,40},{56,48},{64,56},{72,6... | collective-permute-start | bytes 3145736 | tf_op jit(solution)/shard_map/ppermute | solution.py:484
  88.2 0.6 collective-permute-start.8
  88.8 2.0 copy.25.refs_7_
  91.4 0.8 reduce.9
  93.1 1.6 copy-done.2
  94.7 1.6 copy-done.4
  96.3 1.2 copy-done.6
  97.5 27.3 %factor_rest.1 = (bf16[16,128,256]{2,1,0:T(8,128)(2,1)S(1)}, f32[16,128,128]{2,1,0:T(8,128)S(1)}) custom-call(f32[16,128,128]{2,1,0:T(8,128)S(1)} %copy-done.6, f32[16,256,128]{2,1,0:T(8,128)S(1)} %copy-done.2, f32[16,128,256]{2,1,0:T(8,128)S(1)} %copy-done.4), custom_call_target="tpu_custom_call" | custom-call | tf_op jit(solution)/shard_map/factor_rest/pallas_call | solution.py:319
  124.9 13.2 %whiten.2 = (f32[16,128,256]{2,1,0:T(8,128)}, bf16[1024,256]{1,0:T(8,128)(2,1)S(1)}, f32[8,8,128]{2,1,0:T(8,128)S(1)}) custom-call(s32[2]{0:T(128)S(1)} %pad_add_fusion.first.refs_0_, s32[4,4,256]{2,1,0:T(4,128)S(1)} %copy-done.7, bf16[2,256,1024]{2,1,0:T(8,128)(2,1)S(1)} %collective-permute-done.6.refs_2_, ...), custom_call_target="tpu_custom_call" | custom-call | tf_op jit(solution)/shard_map/whiten/pallas_call | solution.py:380
  138.2 13.2 %whiten.3 = (f32[16,128,256]{2,1,0:T(8,128)}, bf16[1024,256]{1,0:T(8,128)(2,1)S(1)}, f32[8,8,128]{2,1,0:T(8,128)S(1)}) custom-call(s32[2]{0:T(128)S(1)} %pad_add_fusion.first.refs_0_, s32[4,4,256]{2,1,0:T(4,128)S(1)} %copy-done.7, bf16[2,256,1024]{2,1,0:T(8,128)(2,1)S(1)} %collective-permute-done.6.refs_2_, ...), custom_call_target="tpu_custom_call", output_to_operand_aliasing={{0}: (8, {})} | custom-call | tf_op jit(solution)/shard_map/whiten/pallas_call | solution.py:380
  151.4 0.9 collective-permute-start.10
  153.1 16.3 %cross_near.1.acc_in = f32[4096,256]{1,0:T(8,128)S(1)} custom-call(f32[1]{0:T(128)S(6)} %div.12.s.scale, f32[4,2,1024]{2,1,0:T(2,128)S(1)} %pad_maximum_fusion.4.t, f32[2,2048]{1,0:T(2,128)S(1)} %pad_maximum_fusion.5.p, bf16[1024,256]{1,0:T(8,128)(2,1)S(1)} %get-tuple-element.31.a, bf16[1024,256]{1,0:T(8,128)(2,1)S(1)} %get-tuple-element.32.b), custom_call_target="tpu_custom_call" | custom-call | tf_op jit(solution)/shard_map/cross_near/pallas_call | solution.py:461
  169.3 7.1 %collective-permute-done.9.wa = bf16[1024,256]{1,0:T(8,128)(2,1)S(1)} collective-permute-done((bf16[1024,256]{1,0:T(8,128)(2,1)S(1)}, bf16[1024,256]{1,0:T(8,128)(2,1)S(1)}, u32[]{:S(2)}, u32[]{:S(2)}) %collective-permute-start.9) | collective-permute-done | bytes 524320 | tf_op jit(solution)/shard_map/ppermute | solution.py:534
  176.4 4.1 %cross_far.3 = bf16[1024,256]{1,0:T(8,128)(2,1)S(1)} custom-call(f32[1]{0:T(128)S(6)} %div.12.s.scale, f32[1,2,1024]{2,1,0:T(2,128)S(1)} %get-tuple-element.43.tgt, f32[2,2048]{1,0:T(2,128)S(1)} %collective-permute-done.8.pts, bf16[1024,256]{1,0:T(8,128)(2,1)S(1)} %collective-permute-done.9.wa, bf16[1024,256]{1,0:T(8,128)(2,1)S(1)} %collective-permute-done.10.wb, ...), custom_call_target="tpu_custom_call" | custom-call | tf_op jit(solution)/shard_map/cross_far/pallas_call | solution.py:461
  180.5 2.9 %collective-permute-start.11 = (bf16[1024,256]{1,0:T(8,128)(2,1)S(1)}, bf16[1024,256]{1,0:T(8,128)(2,1)S(1)}, u32[]{:S(2)}, u32[]{:S(2)}) collective-permute-start(bf16[1024,256]{1,0:T(8,128)(2,1)S(1)} %cross_far.3), channel_id=1, source_target_pairs={{0,4},{1,5},{2,6},{3,7},{4,0},{5,1},{6,2},{7,3},{8,12},{9,13},{10,... | collective-permute-start | bytes 1572872 | tf_op jit(solution)/shard_map/ppermute | solution.py:547
  183.4 4.1 %cross_far.4 = bf16[1024,256]{1,0:T(8,128)(2,1)S(1)} custom-call(f32[1]{0:T(128)S(6)} %div.12.s.scale, f32[1,2,1024]{2,1,0:T(2,128)S(1)} %get-tuple-element.45.tgt, f32[2,2048]{1,0:T(2,128)S(1)} %collective-permute-done.8.pts, bf16[1024,256]{1,0:T(8,128)(2,1)S(1)} %collective-permute-done.9.wa, bf16[1024,256]{1,0:T(8,128)(2,1)S(1)} %collective-permute-done.10.wb, ...), custom_call_target="tpu_custom_call" | custom-call | tf_op jit(solution)/shard_map/cross_far/pallas_call | solution.py:461
  187.9 4.1 %cross_far.5 = bf16[1024,256]{1,0:T(8,128)(2,1)S(1)} custom-call(f32[1]{0:T(128)S(6)} %div.12.s.scale, f32[1,2,1024]{2,1,0:T(2,128)S(1)} %get-tuple-element.46.tgt, f32[2,2048]{1,0:T(2,128)S(1)} %collective-permute-done.8.pts, bf16[1024,256]{1,0:T(8,128)(2,1)S(1)} %collective-permute-done.9.wa, bf16[1024,256]{1,0:T(8,128)(2,1)S(1)} %collective-permute-done.10.wb, ...), custom_call_target="tpu_custom_call" | custom-call | tf_op jit(solution)/shard_map/cross_far/pallas_call | solution.py:461
  192.0 2.4 %collective-permute-start.13 = (bf16[1024,256]{1,0:T(8,128)(2,1)S(1)}, bf16[1024,256]{1,0:T(8,128)(2,1)S(1)}, u32[]{:S(2)}, u32[]{:S(2)}) collective-permute-start(bf16[1024,256]{1,0:T(8,128)(2,1)S(1)} %cross_far.5), channel_id=1, source_target_pairs={{0,6},{1,7},{2,0},{3,1},{4,2},{5,3},{6,4},{7,5},{8,14},{9,15},{10,... | collective-permute-start | bytes 1572872 | tf_op jit(solution)/shard_map/ppermute | solution.py:547
  194.4 4.1 %cross_here.1 = f32[1024,256]{1,0:T(8,128)S(1)} custom-call(f32[1]{0:T(128)S(6)} %div.12.s.scale, f32[1,2,1024]{2,1,0:T(2,128)S(1)} %get-tuple-element.44.tgt, f32[2,2048]{1,0:T(2,128)S(1)} %collective-permute-done.8.pts, bf16[1024,256]{1,0:T(8,128)(2,1)S(1)} %collective-permute-done.9.wa, bf16[1024,256]{1,0:T(8,128)(2,1)S(1)} %collective-permute-done.10.wb, ...), custom_call_target="tpu_custom_call" | custom-call | tf_op jit(solution)/shard_map/cross_here/pallas_call | solution.py:461
  198.5 8.6 %collective-permute-done.12 = bf16[1024,256]{1,0:T(8,128)(2,1)S(1)} collective-permute-done((bf16[1024,256]{1,0:T(8,128)(2,1)S(1)}, bf16[1024,256]{1,0:T(8,128)(2,1)S(1)}, u32[]{:S(2)}, u32[]{:S(2)}) %collective-permute-start.12) | collective-permute-done | bytes 524320 | tf_op jit(solution)/shard_map/ppermute | solution.py:547
  207.2 1.1 multiply_convert_fusion
  208.2 6.0 %all-to-all-start.1 = ((bf16[16,64,256]{2,1,0:T(8,128)(2,1)}), bf16[16,64,256]{2,1,0:T(8,128)(2,1)S(1)}, u32[]{:S(2)}, u32[]{:S(2)}) async-start(bf16[16,64,256]{2,1,0:T(8,128)(2,1)} %bitcast.20), calls=%async_computation.1 | async-start | bytes 1048576 | tf_op jit(solution)/shard_map/all_to_all | solution.py:551
  215.3 10.1 %all-to-all-done.1 = bf16[16,64,256]{2,1,0:T(8,128)(2,1)S(1)} async-done(((bf16[16,64,256]{2,1,0:T(8,128)(2,1)}), bf16[16,64,256]{2,1,0:T(8,128)(2,1)S(1)}, u32[]{:S(2)}, u32[]{:S(2)}) %all-to-all-start.1) | async-done | bytes 524320 | tf_op jit(solution)/shard_map/all_to_all | solution.py:551
  225.4 1.9 gather_fusion.1
  227.4 0.8 convert_element_type.37
  (83 shorter events, 5.9 us)
Async XLA Ops:
  2.1 37.0 %collective-permute-start = (f32[4,2,8,128]{3,2,1,0:T(8,128)S(1)}, f32[4,2,8,128]{3,2,1,0:T(8,128)S(1)}, u32[]{:S(2)}, u32[]{:S(2)}) collective-permute-start(f32[4,2,8,128]{3,2,1,0:T(8,128)S(1)} %get-tuple-element.41), channel_id=1, source_target_pairs={{0,1},{1,2},{2,3},{3,4},{4,5},{5,6},{6,7},{8,9},{9,10},{10,11},{11... | collective-permute-start | bytes 98312 | tf_op jit(solution)/shard_map/ppermute | solution.py:484
  6.5 32.6 %collective-permute-start.1 = (f32[4,2,8,128]{3,2,1,0:T(8,128)S(1)}, f32[4,2,8,128]{3,2,1,0:T(8,128)S(1)}, u32[]{:S(2)}, u32[]{:S(2)}) collective-permute-start(f32[4,2,8,128]{3,2,1,0:T(8,128)S(1)} %get-tuple-element.42), channel_id=1, source_target_pairs={{1,0},{2,1},{3,2},{4,3},{5,4},{6,5},{7,6},{9,8},{10,9},{11,10},{12... | collective-permute-start | bytes 98312 | tf_op jit(solution)/shard_map/ppermute | solution.py:484
  10.3 1.7 copy-start.8
  10.3 7.0 %copy-start.13 = (s32[512,1]{0,1:T(1,128)S(1)}, s32[512,1]{0,1:T(1,128)}, u32[]{:S(2)}) copy-start(s32[512,1]{0,1:T(1,128)} %param.13) | copy-start | bytes 6148
  10.3 8.5 %copy-start.14 = (f32[2,512]{1,0:T(2,128)S(1)}, f32[2,512]{1,0:T(2,128)}, u32[]{:S(2)}) copy-start(f32[2,512]{1,0:T(2,128)} %param.14) | copy-start | bytes 12292
  10.9 28.3 %copy-start.11 = (f32[4,4,128]{2,1,0:T(4,128)S(1)}, f32[4,4,128]{2,1,0:T(4,128)}, u32[]{:S(2)}) copy-start(f32[4,4,128]{2,1,0:T(4,128)} %param.10) | copy-start | bytes 24580
  10.9 40.9 %copy-start.7 = (s32[4,4,256]{2,1,0:T(4,128)S(1)}, s32[4,4,256]{2,1,0:T(4,128)}, u32[]{:S(2)}) copy-start(s32[4,4,256]{2,1,0:T(4,128)} %refs_1_.3) | copy-start | bytes 49156
  12.0 67.7 %collective-permute-start.4 = (bf16[4,256,256]{2,1,0:T(8,128)(2,1)}, bf16[4,256,256]{2,1,0:T(8,128)(2,1)S(1)}, u32[]{:S(2)}, u32[]{:S(2)}) collective-permute-start(bf16[4,256,256]{2,1,0:T(8,128)(2,1)} %get-tuple-element.37), channel_id=1, source_target_pairs={{0,1},{1,2},{2,3},{3,4},{4,5},{5,6},{6,7},{8,9},{9,10},{10,11},{11... | collective-permute-start | bytes 1572872 | tf_op jit(solution)/shard_map/ppermute | solution.py:484
  16.0 64.5 %collective-permute-start.5 = (bf16[4,256,256]{2,1,0:T(8,128)(2,1)}, bf16[4,256,256]{2,1,0:T(8,128)(2,1)}, u32[]{:S(2)}, u32[]{:S(2)}) collective-permute-start(bf16[4,256,256]{2,1,0:T(8,128)(2,1)} %get-tuple-element.38), channel_id=1, source_target_pairs={{1,0},{2,1},{3,2},{4,3},{5,4},{6,5},{7,6},{9,8},{10,9},{11,10},{12... | collective-permute-start | bytes 1572872 | tf_op jit(solution)/shard_map/ppermute | solution.py:484
  24.6 66.3 %all-to-all-start = ((f32[128,1,128]{2,1,0:T(1,128)}), f32[128,1,128]{2,1,0:T(1,128)S(1)}, u32[]{:S(2)}, u32[]{:S(2)}) async-start(f32[128,1,128]{2,1,0:T(1,128)} %bitcast.13), calls=%async_computation | async-start | bytes 131072 | tf_op jit(solution)/shard_map/all_to_all | solution.py:513
  39.2 7.5 %collective-permute-start.2 = (f32[2,8,8,128]{3,2,1,0:T(8,128)S(1)}, f32[2,8,8,128]{3,2,1,0:T(8,128)S(1)}, u32[]{:S(2)}, u32[]{:S(2)}) collective-permute-start(f32[2,8,8,128]{3,2,1,0:T(8,128)S(1)} %get-tuple-element.39), channel_id=1, source_target_pairs={{0,8},{8,16},{16,24},{24,32},{32,40},{40,48},{48,56},{56,64},{64,7... | collective-permute-start | bytes 196616 | tf_op jit(solution)/shard_map/ppermute | solution.py:484
  44.6 7.1 %collective-permute-start.3 = (f32[2,8,8,128]{3,2,1,0:T(8,128)S(1)}, f32[2,8,8,128]{3,2,1,0:T(8,128)S(1)}, u32[]{:S(2)}, u32[]{:S(2)}) collective-permute-start(f32[2,8,8,128]{3,2,1,0:T(8,128)S(1)} %get-tuple-element.40), channel_id=1, source_target_pairs={{8,0},{16,8},{24,16},{32,24},{40,32},{48,40},{56,48},{64,56},{72,6... | collective-permute-start | bytes 196616 | tf_op jit(solution)/shard_map/ppermute | solution.py:484
  76.1 1.3 copy-start.1
  77.4 1.3 copy-start.3
  78.7 1.0 copy-start.5
  79.7 0.8 copy-start.10
  82.0 6.0 %copy-start.12 = (f32[2,4,4,128]{3,2,1,0:T(4,128)S(1)}, f32[2,4,4,128]{3,2,1,0:T(4,128)}, u32[]{:S(2)}) copy-start(f32[2,4,4,128]{3,2,1,0:T(4,128)} %param.9) | copy-start | bytes 49156
  82.0 6.8 %copy-start.9 = (f32[4,256,512]{2,0,1:T(4,128)S(1)}, f32[4,256,512]{2,0,1:T(4,128)}, u32[]{:S(2)}) copy-start(f32[4,256,512]{2,0,1:T(4,128)} %copy-done.8) | copy-start | bytes 6291460
  83.5 41.4 %collective-permute-start.6 = (bf16[2,256,1024]{2,1,0:T(8,128)(2,1)}, bf16[2,256,1024]{2,1,0:T(8,128)(2,1)S(1)}, u32[]{:S(2)}, u32[]{:S(2)}) collective-permute-start(bf16[2,256,1024]{2,1,0:T(8,128)(2,1)} %get-tuple-element.36), channel_id=1, source_target_pairs={{0,8},{8,16},{16,24},{24,32},{32,40},{40,48},{48,56},{56,64},{64,7... | collective-permute-start | bytes 3145736 | tf_op jit(solution)/shard_map/ppermute | solution.py:484
  85.4 39.5 %collective-permute-start.7 = (bf16[2,256,1024]{2,1,0:T(8,128)(2,1)}, bf16[2,256,1024]{2,1,0:T(8,128)(2,1)}, u32[]{:S(2)}, u32[]{:S(2)}) collective-permute-start(bf16[2,256,1024]{2,1,0:T(8,128)(2,1)} %get-tuple-element.35), channel_id=1, source_target_pairs={{8,0},{16,8},{24,16},{32,24},{40,32},{48,40},{56,48},{64,56},{72,6... | collective-permute-start | bytes 3145736 | tf_op jit(solution)/shard_map/ppermute | solution.py:484
  88.2 2.7 %copy-start.15 = (s32[4]{0:T(128)S(1)}, s32[4]{0:T(128)}, u32[]{:S(2)}) copy-start(s32[4]{0:T(128)} %constant.101.clone) | copy-start | bytes 52
  88.2 81.1 %collective-permute-start.8 = (f32[2,2048]{1,0:T(2,128)S(1)}, f32[2,2048]{1,0:T(2,128)S(1)}, u32[]{:S(2)}, u32[]{:S(2)}) collective-permute-start(f32[2,2048]{1,0:T(2,128)S(1)} %pad_maximum_fusion.5.p), channel_id=1, source_target_pairs={{0,1},{1,0},{2,3},{3,2},{4,5},{5,4},{6,7},{7,6},{8,9},{9,8},{10,11... | collective-permute-start | bytes 49160 | tf_op jit(solution)/shard_map/ppermute | solution.py:525
  93.1 1.6 copy-start.2
  94.7 1.6 copy-start.4
  96.3 1.2 copy-start.6
  97.5 27.4 %copy-start = (f32[4,256,512]{2,1,0:T(8,128)S(1)}, f32[4,256,512]{2,1,0:T(8,128)}, u32[]{:S(2)}) copy-start(f32[4,256,512]{2,1,0:T(8,128)} %copy.25.refs_7_) | copy-start | bytes 6291460
  151.4 18.0 %collective-permute-start.10 = (bf16[1024,256]{1,0:T(8,128)(2,1)S(1)}, bf16[1024,256]{1,0:T(8,128)(2,1)S(1)}, u32[]{:S(2)}, u32[]{:S(2)}) collective-permute-start(bf16[1024,256]{1,0:T(8,128)(2,1)S(1)} %get-tuple-element.32.b), channel_id=1, source_target_pairs={{0,1},{1,0},{2,3},{3,2},{4,5},{5,4},{6,7},{7,6},{8,9},{9,8},{10,11... | collective-permute-start | bytes 1572872 | tf_op jit(solution)/shard_map/ppermute | solution.py:536
  152.3 24.2 %collective-permute-start.9 = (bf16[1024,256]{1,0:T(8,128)(2,1)S(1)}, bf16[1024,256]{1,0:T(8,128)(2,1)S(1)}, u32[]{:S(2)}, u32[]{:S(2)}) collective-permute-start(bf16[1024,256]{1,0:T(8,128)(2,1)S(1)} %get-tuple-element.31.a), channel_id=1, source_target_pairs={{0,1},{1,0},{2,3},{3,2},{4,5},{5,4},{6,7},{7,6},{8,9},{9,8},{10,11... | collective-permute-start | bytes 1572872 | tf_op jit(solution)/shard_map/ppermute | solution.py:534
  180.5 18.0 %collective-permute-start.11 = (bf16[1024,256]{1,0:T(8,128)(2,1)S(1)}, bf16[1024,256]{1,0:T(8,128)(2,1)S(1)}, u32[]{:S(2)}, u32[]{:S(2)}) collective-permute-start(bf16[1024,256]{1,0:T(8,128)(2,1)S(1)} %cross_far.3), channel_id=1, source_target_pairs={{0,4},{1,5},{2,6},{3,7},{4,0},{5,1},{6,2},{7,3},{8,12},{9,13},{10,... | collective-permute-start | bytes 1572872 | tf_op jit(solution)/shard_map/ppermute | solution.py:547
  187.5 19.7 %collective-permute-start.12 = (bf16[1024,256]{1,0:T(8,128)(2,1)S(1)}, bf16[1024,256]{1,0:T(8,128)(2,1)S(1)}, u32[]{:S(2)}, u32[]{:S(2)}) collective-permute-start(bf16[1024,256]{1,0:T(8,128)(2,1)S(1)} %cross_far.4), channel_id=1, source_target_pairs={{0,2},{1,3},{2,4},{3,5},{4,6},{5,7},{6,0},{7,1},{8,10},{9,11},{10,... | collective-permute-start | bytes 1572872 | tf_op jit(solution)/shard_map/ppermute | solution.py:547
  192.0 15.2 %collective-permute-start.13 = (bf16[1024,256]{1,0:T(8,128)(2,1)S(1)}, bf16[1024,256]{1,0:T(8,128)(2,1)S(1)}, u32[]{:S(2)}, u32[]{:S(2)}) collective-permute-start(bf16[1024,256]{1,0:T(8,128)(2,1)S(1)} %cross_far.5), channel_id=1, source_target_pairs={{0,6},{1,7},{2,0},{3,1},{4,2},{5,3},{6,4},{7,5},{8,14},{9,15},{10,... | collective-permute-start | bytes 1572872 | tf_op jit(solution)/shard_map/ppermute | solution.py:547
  208.2 17.2 %all-to-all-start.1 = ((bf16[16,64,256]{2,1,0:T(8,128)(2,1)}), bf16[16,64,256]{2,1,0:T(8,128)(2,1)S(1)}, u32[]{:S(2)}, u32[]{:S(2)}) async-start(bf16[16,64,256]{2,1,0:T(8,128)(2,1)} %bitcast.20), calls=%async_computation.1 | async-start | bytes 1048576 | tf_op jit(solution)/shard_map/all_to_all | solution.py:551
where the time goes:
time: 229 us; the launch traced here: 228 us
  Pallas kernels  111 us (48%)
  starting transfers between devices  50.4 us (22%)
  waiting for transfers between devices  30.9 us (13%)
  local copies, waits for them, and re-layouts  27 us (12%)
  other arithmetic  7.29 us (3%)
    pallas_call x5, Pallas kernels, cross(): pl.pallas_call(kernel, grid=(n,), out_shape=jax.ShapeDtypeStruct((n * TB,...  32.6 us
    pallas_call x1, Pallas kernels, factor_rest(): pl.pallas_call(rest_kernel, out_shape=(jax.ShapeDtypeStruct((16, 128, 256...  27.3 us
    pallas_call x2, Pallas kernels, whiten(): pl.pallas_call(kernel, grid=(8,), out_shape=(jax.ShapeDtypeStruct((16, 12...  26.4 us
    pallas_call x1, Pallas kernels, factor_first(): pl.pallas_call(first_kernel, out_shape=(jax.ShapeDtypeStruct((16, 128, 12...  24.3 us
    ppermute x4, starting transfers between devices, sides(): lax.ppermute(high, axis, forward)  15.7 us
    all_to_all x1, starting transfers between devices, body(): lax.all_to_all(everyone, ('rows', 'cols'), split_axis=0, concat_axis=0, t...  13.8 us
    all_to_all x1, waiting for transfers between devices, body(): lax.all_to_all(predicted.reshape(16, 64, 256), 'rows', split_axis=0, conc...  10.1 us
    unnamed x33, local copies, waits for them, and re-layouts  9.57 us
  transfers between devices with their start and end apart: 16, of which 4 were waited for; matrix products, arithmetic and copies ran while one was open for 9% of the time, Pallas kernels for 47%

commit v1 on v0

--- a/solution.py
+++ b/solution.py
@@ -185,7 +185,7 @@
     return ci, cj, w, idx & 127
 
 
-def first_kernel(first, length, nb, geo, xw, cc, tt, wp, mid):
+def factor_kernel(first, length, nb, geo, g_out, w3_out, xw, wp, mid, cc, tt, l32s):
     count = 16
     lane8 = lax.broadcasted_iota(jnp.int32, (8, 128), 1)
     sub8 = lax.broadcasted_iota(jnp.int32, (8, 128), 0)
@@ -236,8 +236,6 @@
         return 0
 
     lax.fori_loop(0, count, covariance, 0)
-    inv_chol(xw, wp, count)
-
     def level1(q, _):
         cs = [4 * q + e for e in range(4)]
         w1 = [xw[c] for c in cs]
@@ -250,12 +248,6 @@
             tt[c] = tt[c] - u[e][128:, :]
         return 0
 
-    lax.fori_loop(0, count // 4, level1, 0)
-
-def rest_kernel(x_in, cc, tt, g_out, w3_out, xw, wp, l32s):
-    count = 16
-    xw[...] = x_in[...]
-
     def level2(q, _):
         cs = [4 * q + e for e in range(4)]
         w2 = [xw[c] for c in cs]
@@ -272,11 +264,15 @@
 
         @pl.when(b == 0)
         def _():
+            lax.fori_loop(0, count // 4, level1, 0)
+
+        @pl.when(b == 1)
+        def _():
             lax.fori_loop(0, count // 4, level2, 0)
 
         return 0
 
-    lax.fori_loop(0, 2, level, 0)
+    lax.fori_loop(0, 3, level, 0)
 
     def last(q, _):
         cs = [4 * q + e for e in range(4)]
@@ -299,114 +295,108 @@
 SM = pl.BlockSpec(memory_space=pltpu.SMEM)
 
 
-def factor_first(first, length, nb, geo):
+def factor(first, length, nb, geo):
     return pl.pallas_call(
-        first_kernel,
-        out_shape=(
-            jax.ShapeDtypeStruct((16, 128, 128), F32),
-            jax.ShapeDtypeStruct((16, 256, 128), F32),
-            jax.ShapeDtypeStruct((16, 128, 256), F32),
-        ),
-        in_specs=[SM, SM, VM, VM],
-        out_specs=(VM, VM, VM),
-        scratch_shapes=[pltpu.VMEM((4, 32, 128), F32), pltpu.VMEM((16, 128, 128), F32)],
-        compiler_params=pltpu.CompilerParams(vmem_limit_bytes=20 << 20),
-        name="factor_first",
-    )(first, length, nb, geo)
-
-
-def factor_rest(x, c, t):
-    return pl.pallas_call(
-        rest_kernel,
+        factor_kernel,
         out_shape=(
             jax.ShapeDtypeStruct((16, 128, 256), BF),
             jax.ShapeDtypeStruct((16, 128, 128), F32),
         ),
-        in_specs=[VM, VM, VM],
+        in_specs=[SM, SM, VM, VM],
         out_specs=(VM, VM),
         scratch_shapes=[
             pltpu.VMEM((16, 128, 128), F32),
             pltpu.VMEM((4, 32, 128), F32),
             pltpu.VMEM((16, 128, 128), F32),
+            pltpu.VMEM((16, 256, 128), F32),
+            pltpu.VMEM((16, 128, 256), F32),
+            pltpu.VMEM((16, 128, 128), F32),
         ],
         compiler_params=pltpu.CompilerParams(vmem_limit_bytes=20 << 20),
-        name="factor_rest",
-    )(x, c, t)
-
-
-def whiten_kernel(base, first, nb, north, mid, south, g, w3, own, white, weights, term, tab):
-    step = pl.program_id(0) + base
-
-    @pl.when(step == base)
+        name="factor",
+    )(first, length, nb, geo)
+
+
+def whiten_kernel(first, nb, north, mid, south, g, w3, own, white, weights, term, tab, acc):
+    ci = pl.program_id(0)
+
+    @pl.when(ci == 0)
     def _():
         tab[0:2] = north[...]
         tab[2:6] = mid[...]
         tab[6:8] = south[...]
 
-    ci, cj, w, member = window(first, nb, step)
-    start = pl.multiple_of(cj * 128, 128)
-    acc = mm_nt(w3[0], own[0])
-    gf = g[0].astype(F32)
     point = lax.broadcasted_iota(jnp.int32, (128, 256), 0)
-    pick = jnp.where(point == jnp.broadcast_to(member, (128, 256)), 1.0, 0.0).astype(BF)
-    for wi in range(5):
-        lhs = jnp.concatenate(
-            [jnp.where(w == wi * 5 + wj, gf, 0.0).astype(BF) for wj in range(5)], 0
-        )
-        gs = dot(lhs, pick, NT).astype(BF)
-        gs = jnp.concatenate([gs[128 * wj : 128 * wj + 128, :] for wj in range(5)], 1)
-        acc = acc - dot(gs, tab[ci + wi, :, pl.ds(start, 640)], NT)
-    white[0] = acc
-    weights[...] = acc.astype(BF)
+    near = []
+    for cj in range(4):
+        _, _, w, member = window(first, nb, 4 * ci + cj)
+        pick = jnp.where(point == jnp.broadcast_to(member, (128, 256)), 1.0, 0.0).astype(BF)
+        near.append((w, pick, g[cj].astype(F32)))
+        acc[128 * cj : 128 * cj + 128, :] = mm_nt(w3[cj], own[0, :, 128 * cj : 128 * cj + 128])
+    blank = [jnp.zeros((128, 128), BF)] * 4
+
+    def one_row(wi, _):
+        rows = []
+        for cj in range(4):
+            w, pick, gf = near[cj]
+            lhs = jnp.concatenate(
+                [jnp.where(w == wi * 5 + wj, gf, 0.0).astype(BF) for wj in range(5)], 0
+            )
+            gs = dot(lhs, pick, NT).astype(BF)
+            blocks = [gs[128 * wj : 128 * wj + 128, :] for wj in range(5)]
+            rows.append(jnp.concatenate(blank[:cj] + blocks + blank[cj + 1 :], 1))
+        acc[...] = acc[...] - dot(jnp.concatenate(rows, 0), tab[ci + wi], NT)
+        return 0
+
+    lax.fori_loop(0, 5, one_row, 0)
+    weights[...] = acc[...].astype(BF)
     eye = (
         lax.broadcasted_iota(jnp.int32, (128, 128), 0)
         == lax.broadcasted_iota(jnp.int32, (128, 128), 1)
     )
-    diag = jnp.sum(jnp.where(eye, w3[0], 0.0), axis=0, keepdims=True)
-    total = 0.5 * jnp.sum(acc * acc) - 256.0 * jnp.sum(jnp.log(diag))
-    term[...] = jnp.full((1, 8, 128), -total / 32768.0 - 0.5 * math.log(2.0 * math.pi), F32)
-
-
-def whiten(first, nb, pieces, g, w3, own, base, white=None):
+    for cj in range(4):
+        out = acc[128 * cj : 128 * cj + 128, :]
+        white[cj] = out
+        diag = jnp.sum(jnp.where(eye, w3[cj], 0.0), axis=0, keepdims=True)
+        total = 0.5 * jnp.sum(out * out) - 256.0 * jnp.sum(jnp.log(diag))
+        value = -total / 32768.0 - 0.5 * math.log(2.0 * math.pi)
+        term[0, cj : cj + 1, :] = jnp.full((1, 128), value, F32)
+
+
+def whiten(first, nb, pieces, g, w3, own):
     def whole(a):
         nd = a.ndim
         return pl.BlockSpec(a.shape, lambda s: (0,) * nd, pipeline_mode=pl.Buffered(1))
 
-    if white is None:
-        kernel = lambda *refs: whiten_kernel(base, *refs)
-    else:
-        kernel = lambda *refs: whiten_kernel(base, *refs[:8], *refs[9:])
-    extra = [] if white is None else [white]
     return pl.pallas_call(
-        kernel,
-        grid=(8,),
+        whiten_kernel,
+        grid=(4,),
         out_shape=(
             jax.ShapeDtypeStruct((16, 128, 256), F32),
-            jax.ShapeDtypeStruct((1024, 256), BF),
-            jax.ShapeDtypeStruct((8, 8, 128), F32),
+            jax.ShapeDtypeStruct((2048, 256), BF),
+            jax.ShapeDtypeStruct((4, 8, 128), F32),
         ),
         in_specs=[SM, whole(nb)]
         + [whole(p) for p in pieces]
         + [
-            pl.BlockSpec((1, 128, 256), lambda s: (s + base, 0, 0)),
-            pl.BlockSpec((1, 128, 128), lambda s: (s + base, 0, 0)),
-            pl.BlockSpec((1, 256, 128), lambda s: ((s + base) // 4, 0, (s + base) % 4)),
-        ]
-        + [pl.BlockSpec(memory_space=pl.ANY) for _ in extra],
+            pl.BlockSpec((4, 128, 256), lambda s: (s, 0, 0)),
+            pl.BlockSpec((4, 128, 128), lambda s: (s, 0, 0)),
+            pl.BlockSpec((1, 256, 512), lambda s: (s, 0, 0)),
+        ],
         out_specs=(
-            pl.BlockSpec((1, 128, 256), lambda s: (s + base, 0, 0)),
-            pl.BlockSpec((128, 256), lambda s: (s, 0)),
+            pl.BlockSpec((4, 128, 256), lambda s: (s, 0, 0)),
+            pl.BlockSpec((512, 256), lambda s: (s, 0)),
             pl.BlockSpec((1, 8, 128), lambda s: (s, 0, 0)),
         ),
-        input_output_aliases={} if white is None else {8: 0},
-        scratch_shapes=[pltpu.VMEM((8, 256, 1024), BF)],
+        scratch_shapes=[pltpu.VMEM((8, 256, 1024), BF), pltpu.VMEM((512, 256), F32)],
         compiler_params=pltpu.CompilerParams(vmem_limit_bytes=24 << 20),
         name="whiten",
-    )(first, nb, *pieces, g, w3, own, *extra)
+    )(first, nb, *pieces, g, w3, own)
 
 
 LN2 = math.log(2.0)
 TB = 1024
+FAR = 1
 
 
 def pieces3(x):
@@ -416,7 +406,7 @@
     return a, b, r - b
 
 
-def cross_kernel(scale, tgt, pts, wa, wb, acc_in, out, rhs, total):
+def cross_kernel(loops, scale, tgt, pts, w, acc_in, out, rhs, total):
     def form(x, y, left):
         q = x * x + y * y
         qs = pieces3(q)
@@ -436,28 +426,38 @@
         rhs[...] = form(pts[0:1, :] * scale[0], pts[1:2, :] * scale[0], False)
 
     lhs = form(tgt[0, 0:1, :] * scale[0], tgt[0, 1:2, :] * scale[0], True)
-    total[...] = acc_in[...] if acc_in is not None else jnp.zeros((TB, 256), F32)
-
-    def chunk(b, _):
+    def chunk(at, acc):
+        s2 = jnp.maximum(dot(lhs, rhs[:, pl.ds(at, 256)], TN), 1e-30)
+        s = s2 * lax.rsqrt(s2)
+        k = (1.0 + s * LN2) * jnp.exp2(-s)
+        return acc + dot(k.astype(BF), w[pl.ds(at, 256), :], NN)
+
+    acc = acc_in[...] if acc_in is not None else jnp.zeros((TB, 256), F32)
+    per = 8 // loops
+    if loops == 1:
+        for e in range(8):
+            acc = chunk(256 * e, acc)
+        out[...] = acc.astype(out.dtype)
+        return
+    total[...] = acc
+
+    def some(b, _):
         acc = total[...]
-        for w in (wa, wb):
-            at = b * 256 + (1024 if w is wb else 0)
-            s2 = jnp.maximum(dot(lhs, rhs[:, pl.ds(pl.multiple_of(at, 256), 256)], TN), 1e-30)
-            s = s2 * lax.rsqrt(s2)
-            k = (1.0 + s * LN2) * jnp.exp2(-s)
-            acc = acc + dot(k.astype(BF), w[pl.ds(pl.multiple_of(b * 256, 256), 256), :], NN)
+        for e in range(per):
+            acc = chunk(pl.multiple_of((b * per + e) * 256, 256), acc)
         total[...] = acc
         return 0
 
-    lax.fori_loop(0, 4, chunk, 0)
+    lax.fori_loop(0, loops, some, 0)
     out[...] = total[...].astype(out.dtype)
 
 
-def cross(scale, tgt, pts, w, dtype, acc=None, skip=0, name="cross"):
+def cross(scale, tgt, pts, w, dtype, acc=None, skip=0, name="cross", loops=1):
     n = tgt.shape[0]
-    kernel = cross_kernel
     if acc is None:
-        kernel = lambda s, t, p, a, b, o, r, m: cross_kernel(s, t, p, a, b, None, o, r, m)
+        kernel = lambda s, t, p, w, o, r, m: cross_kernel(loops, s, t, p, w, None, o, r, m)
+    else:
+        kernel = lambda *refs: cross_kernel(loops, *refs)
     return pl.pallas_call(
         kernel,
         grid=(n,),
@@ -466,15 +466,51 @@
             pl.BlockSpec(memory_space=pltpu.SMEM),
             pl.BlockSpec((1, 2, TB), lambda s: (s, 0, 0)),
             pl.BlockSpec((2, 2048), lambda s: (0, 0)),
-            pl.BlockSpec((1024, 256), lambda s: (0, 0)),
-            pl.BlockSpec((1024, 256), lambda s: (0, 0)),
+            pl.BlockSpec((2048, 256), lambda s: (0, 0)),
         ]
         + ([] if acc is None else [pl.BlockSpec((TB, 256), lambda s: (skip + s, 0))]),
         out_specs=pl.BlockSpec((TB, 256), lambda s: (s, 0)),
         scratch_shapes=[pltpu.VMEM((32, 2048), BF), pltpu.VMEM((TB, 256), F32)],
         compiler_params=pltpu.CompilerParams(vmem_limit_bytes=24 << 20),
         name=name,
-    )(scale, tgt, pts, *w, *([] if acc is None else [acc]))
+    )(scale, tgt, pts, w, *([] if acc is None else [acc]))
+
+
+def sort_kernel(tile, spots, out, slot):
+    t = tile[...]
+    named = lax.broadcasted_iota(jnp.int32, (16, 512), 0) == jnp.broadcast_to(t, (16, 512))
+    hot = jnp.where(named, 1.0, 0.0)
+    before = lax.broadcasted_iota(jnp.int32, (512, 512), 0) < lax.broadcasted_iota(
+        jnp.int32, (512, 512), 1
+    )
+    counts = dot(hot.astype(BF), jnp.where(before, 1.0, 0.0).astype(BF), NN)
+    rank = jnp.sum(counts * hot, axis=0, keepdims=True).astype(jnp.int32)
+    slot[...] = t * 64 + rank
+    at = lax.broadcasted_iota(jnp.int32, (128, 512), 0) & 63
+    place = jnp.where(at == jnp.broadcast_to(rank, (128, 512)), 1.0, 0.0).astype(BF)
+    moved = []
+    for i in range(2):
+        parts = [hot * p for p in pieces3(spots[i : i + 1, :])]
+        m = dot(jnp.concatenate(parts, 0).astype(BF), place, NT)
+        moved.append(m[:16] + m[16:32] + m[32:48])
+    lane = lax.broadcasted_iota(jnp.int32, (16, 128), 1)
+    row = jnp.where(lane < 64, moved[0], moved[1])
+    for g in range(16):
+        out[g] = jnp.broadcast_to(row[g : g + 1, :], (8, 128))
+
+
+def sort_targets(tile, spots):
+    return pl.pallas_call(
+        sort_kernel,
+        out_shape=(
+            jax.ShapeDtypeStruct((16, 8, 128), F32),
+            jax.ShapeDtypeStruct((1, 512), jnp.int32),
+        ),
+        in_specs=[VM, VM],
+        out_specs=(VM, VM),
+        compiler_params=pltpu.CompilerParams(vmem_limit_bytes=8 << 20),
+        name="sort_targets",
+    )(tile, spots)
 
 
 def sides(low, high, axis):
@@ -502,14 +538,8 @@
     mid = own.astype(BF)
     w, e = sides(mid[:, :, :256], mid[:, :, 256:], "cols")
 
-    tile_ids = target_tile[:, 0]
-    one_hot = (tile_ids[:, None] == jnp.arange(16, dtype=jnp.int32)[None, :]).astype(jnp.int32)
-    rank = jnp.sum((jnp.cumsum(one_hot, axis=0) - 1) * one_hot, axis=1)
-    slot = tile_ids * 64 + rank
-    send_x = jnp.zeros((1024,), F32).at[slot].set(target_spots[0])
-    send_y = jnp.zeros((1024,), F32).at[slot].set(target_spots[1])
-    outgoing = jnp.concatenate([send_x.reshape(16, 64), send_y.reshape(16, 64)], axis=1)
-    everyone = jnp.broadcast_to(outgoing[:, None, :], (16, 8, 128)).reshape(128, 1, 128)
+    everyone, slot = sort_targets(target_tile.reshape(1, 512), target_spots)
+    everyone = everyone.reshape(128, 1, 128)
     spots = lax.all_to_all(everyone, ("rows", "cols"), split_axis=0, concat_axis=0, tiled=True)
     spots = spots.reshape(16, 8, 2, 64).transpose(1, 2, 0, 3).reshape(4, 2, 2, 1024)
     band, half = col // 2, col % 2
@@ -524,35 +554,30 @@
     partner = [(c, c ^ 1) for c in range(8)]
     pts2 = lax.ppermute(pts, "cols", partner)
 
-    state = factor_first(first, length_scale, neighbours, geo)
+    first, w, e = lax.optimization_barrier((first, w, e))
     mid = jnp.concatenate([w, mid, e], 2)
-    *state, mid = lax.optimization_barrier((*state, mid))
     n, s = sides(mid[:2], mid[2:], "rows")
     around = [n, mid, s]
-    g, w3 = factor_rest(*state)
-    white, w_a, term_a = whiten(first, neighbours, around, g, w3, own, 0)
-    far_a = lax.ppermute(w_a, "cols", partner)
-    white, w_b, term_b = whiten(first, neighbours, around, g, w3, own, 8, white)
-    far_b = lax.ppermute(w_b, "cols", partner)
-    term = jnp.concatenate([term_a[:, 0, 0], term_b[:, 0, 0]])
-
+    g, w3 = factor(first, length_scale, neighbours, geo)
+    white, weights, term = whiten(first, neighbours, around, g, w3, own)
     scale = jnp.stack([math.sqrt(3.0) / LN2 / length])
-    near = cross(scale, tgt, pts, (w_a, w_b), F32, name="cross_near")
+    weights2 = lax.ppermute(weights, "cols", partner)
+    near = cross(scale, tgt, pts, weights, F32, name="cross_near")
     per = 1024 // TB
     parts = []
     for i, k in enumerate((2, 1, 3)):
         part = cross(
-            scale, tgt[per * i : per * i + per], pts2, (far_a, far_b), BF, near, per * i, "cross_far"
+            scale, tgt[per * i : per * i + per], pts2, weights2, BF, near, per * i, "cross_far", FAR
         )
         parts.append(lax.ppermute(part, "cols", [(c, (c + 2 * k) % 8) for c in range(8)]))
-    here = cross(scale, tgt[3 * per :], pts2, (far_a, far_b), F32, near, 3 * per, "cross_here")
+    here = cross(scale, tgt[3 * per :], pts2, weights2, F32, near, 3 * per, "cross_here", FAR)
     predicted = here + (parts[0].astype(F32) + parts[1].astype(F32) + parts[2].astype(F32))
     predicted = (predicted * (1.0 / 128.0)).astype(BF)
     returned = lax.all_to_all(
         predicted.reshape(16, 64, 256), "rows", split_axis=0, concat_axis=0, tiled=True
     )
-    predictions = returned.reshape(-1, 256)[slot].astype(F32)
-    return (white.reshape(4, 4, 128, 256), term.reshape(4, 4), predictions)
+    predictions = returned.reshape(-1, 256)[slot.reshape(512)].astype(F32)
+    return (white.reshape(4, 4, 128, 256), term[:, :4, 0], predictions)
 
 
 def solution(mesh):

time: 229 us -> 214 us (0.934)
  starting transfers between devices: 50.4 us -> 61.9 us
  local copies, waits for them, and re-layouts: 27 us -> 15.8 us
  waiting for transfers between devices: 30.9 us -> 23.7 us
  Pallas kernels: 111 us -> 105 us
  other arithmetic: 7.29 us -> 4.61 us
    ppermute x4, waiting for transfers between devices: 0.01 us -> 9.89 us  [sides(): lax.ppermute(high, axis, forward)]
    unnamed x33 -> x17, local copies, waits for them, and re-layouts: 9.57 us -> 1.64 us
    ppermute x2 -> x1, waiting for transfers between devices: 7.08 us -> 0.01 us  [body(): weights2 = lax.ppermute(weights, 'cols', partner)]
    pallas_call x5, Pallas kernels: 32.6 us -> 26.9 us  [cross(): pl.pallas_call(kernel, grid=(n,), out_shape=jax.ShapeDtypeStruct((n * TB,...]
    ppermute x4, starting transfers between devices: 15.7 us -> 21.4 us  [sides(): lax.ppermute(high, axis, forward)]
    ppermute x3, waiting for transfers between devices: 8.65 us -> 3.34 us  [body(): lax.ppermute(part, 'cols', [(c, (c + 2 * k) % 8) for c in range(8)])]
    ppermute x4, waiting for transfers between devices: 5.09 us -> 0.01 us  [sides(): lax.ppermute(low, axis, backward)]
    all_to_all x1, starting transfers between devices: 6.04 us -> 11.1 us  [body(): lax.all_to_all(predicted.reshape(16, 64, 256), 'rows', split_axis=0, conc...]
  transfers between devices with their start and end apart: 16 -> 15, of which waited for: 4 -> 5; matrix products, arithmetic and copies ran while one was open for 9% -> 5% of each run, Pallas kernels for 47% -> 48%
where the time goes in v1:
time: 214 us; the launch traced here: 213 us
  Pallas kernels  105 us (49%)
  starting transfers between devices  61.9 us (29%)
  waiting for transfers between devices  23.7 us (11%)
  local copies, waits for them, and re-layouts  15.8 us (7%)
  other arithmetic  4.61 us (2%)
    pallas_call x1, Pallas kernels, factor(): pl.pallas_call(factor_kernel, out_shape=(jax.ShapeDtypeStruct((16, 128, 2...  51.6 us
    pallas_call x5, Pallas kernels, cross(): pl.pallas_call(kernel, grid=(n,), out_shape=jax.ShapeDtypeStruct((n * TB,...  26.9 us
    pallas_call x1, Pallas kernels, whiten(): pl.pallas_call(whiten_kernel, grid=(4,), out_shape=(jax.ShapeDtypeStruct(...  25.7 us
    ppermute x4, starting transfers between devices, sides(): lax.ppermute(high, axis, forward)  21.4 us
    all_to_all x1, starting transfers between devices, body(): lax.all_to_all(everyone, ('rows', 'cols'), split_axis=0, concat_axis=0, t...  13.1 us
    all_to_all x1, starting transfers between devices, body(): lax.all_to_all(predicted.reshape(16, 64, 256), 'rows', split_axis=0, conc...  11.1 us
    all_to_all x1, waiting for transfers between devices, body(): lax.all_to_all(predicted.reshape(16, 64, 256), 'rows', split_axis=0, conc...  10.5 us
    ppermute x4, waiting for transfers between devices, sides(): lax.ppermute(high, axis, forward)  9.89 us
  transfers between devices with their start and end apart: 15, of which 5 were waited for; matrix products, arithmetic and copies ran while one was open for 5% of the time, Pallas kernels for 48%

profile of v1, /device:TPU:1, one launch (start us, length us, event | category | flops | bytes accessed | tf_op | source)
XLA Modules:
  0.0 212.9 jit_solution(4640851148037953988)
XLA Ops:
  0.6 2.5 %reshape.142 = f32[4,256,512]{2,0,1:T(4,128)S(1)} reshape(f32[4,256,4,128]{3,2,0,1:T(4,128)} %bitcast.30) | data formatting | bytes 4194304 | tf_op jit(solution)/shard_map/reshape | solution.py:537
  3.2 0.6 copy.25
  3.7 1.1 fusion.8
  4.8 5.2 %collective-permute-start = (bf16[4,256,256]{2,1,0:T(8,128)(2,1)}, bf16[4,256,256]{2,1,0:T(8,128)(2,1)}, u32[]{:S(2)}, u32[]{:S(2)}) collective-permute-start(bf16[4,256,256]{2,1,0:T(8,128)(2,1)} %get-tuple-element.28), channel_id=1, source_target_pairs={{0,1},{1,2},{2,3},{3,4},{4,5},{5,6},{6,7},{8,9},{9,10},{10,11},{11... | collective-permute-start | bytes 1572872 | tf_op jit(solution)/shard_map/ppermute | solution.py:520
  10.0 1.3 collective-permute-start.1
  11.4 4.0 %collective-permute-start.4 = (f32[4,2,8,128]{3,2,1,0:T(8,128)S(1)}, f32[4,2,8,128]{3,2,1,0:T(8,128)S(1)}, u32[]{:S(2)}, u32[]{:S(2)}) collective-permute-start(f32[4,2,8,128]{3,2,1,0:T(8,128)S(1)} %get-tuple-element.31), channel_id=1, source_target_pairs={{0,1},{1,2},{2,3},{3,4},{4,5},{5,6},{6,7},{8,9},{9,10},{10,11},{11... | collective-permute-start | bytes 98312 | tf_op jit(solution)/shard_map/ppermute | solution.py:520
  15.4 1.3 collective-permute-start.5
  16.7 1.0 sort_targets.1
  17.7 13.1 %all-to-all-start = ((f32[128,1,128]{2,1,0:T(1,128)}), f32[128,1,128]{2,1,0:T(1,128)S(1)}, u32[]{:S(2)}, u32[]{:S(2)}) async-start(f32[128,1,128]{2,1,0:T(1,128)} %bitcast.8), calls=%async_computation | async-start | bytes 131072 | tf_op jit(solution)/shard_map/all_to_all | solution.py:543
  30.8 0.1 pad_add_fusion.first
  30.9 1.2 collective-permute-done
  32.1 1.5 pad_maximum_fusion.mid
  33.6 1.6 fusion.7
  35.1 7.1 %collective-permute-start.2 = (bf16[2,256,1024]{2,1,0:T(8,128)(2,1)}, bf16[2,256,1024]{2,1,0:T(8,128)(2,1)S(1)}, u32[]{:S(2)}, u32[]{:S(2)}) collective-permute-start(bf16[2,256,1024]{2,1,0:T(8,128)(2,1)} %get-tuple-element.26), channel_id=1, source_target_pairs={{0,8},{8,16},{16,24},{24,32},{32,40},{40,48},{48,56},{56,64},{64,7... | collective-permute-start | bytes 3145736 | tf_op jit(solution)/shard_map/ppermute | solution.py:520
  42.3 1.9 collective-permute-start.3
  44.3 0.1 add.118
  44.5 0.7 fusion.9
  45.2 5.1 %collective-permute-start.6 = (f32[2,8,8,128]{3,2,1,0:T(8,128)}, f32[2,8,8,128]{3,2,1,0:T(8,128)S(1)}, u32[]{:S(2)}, u32[]{:S(2)}) collective-permute-start(f32[2,8,8,128]{3,2,1,0:T(8,128)} %get-tuple-element.29), channel_id=1, source_target_pairs={{0,8},{8,16},{16,24},{24,32},{32,40},{40,48},{48,56},{56,64},{64,7... | collective-permute-start | bytes 196616 | tf_op jit(solution)/shard_map/ppermute | solution.py:520
  50.3 1.9 collective-permute-start.7
  52.3 1.9 collective-permute-start.8
  54.1 3.6 %copy.22.own = f32[4,256,512]{2,1,0:T(8,128)} copy(f32[4,256,512]{2,0,1:T(4,128)} %copy-done.4) | data formatting | bytes 4194304 | tf_op jit(solution)/shard_map/reshape | solution.py:537
  58.4 8.7 %collective-permute-done.6 = f32[2,8,8,128]{3,2,1,0:T(8,128)S(1)} collective-permute-done((f32[2,8,8,128]{3,2,1,0:T(8,128)}, f32[2,8,8,128]{3,2,1,0:T(8,128)S(1)}, u32[]{:S(2)}, u32[]{:S(2)}) %collective-permute-start.6) | collective-permute-done | bytes 65568 | tf_op jit(solution)/shard_map/ppermute | solution.py:520
  67.2 51.6 %factor.1 = (bf16[16,128,256]{2,1,0:T(8,128)(2,1)S(1)}, f32[16,128,128]{2,1,0:T(8,128)S(1)}) custom-call(s32[2]{0:T(128)S(1)} %pad_add_fusion.first, f32[1]{0:T(128)S(6)} %copy.27.length, s32[4,4,256]{2,1,0:T(4,128)S(1)} %copy-done.1, f32[8,8,8,128]{3,2,1,0:T(8,128)S(1)} %pad_maximum_fusion.1.geo), custom_call_target="tpu_custom_call" | custom-call | tf_op jit(solution)/shard_map/factor/pallas_call | solution.py:299
  118.8 1.6 copy-done
  120.4 25.7 %whiten.1 = (f32[16,128,256]{2,1,0:T(8,128)}, bf16[2048,256]{1,0:T(8,128)(2,1)}, f32[4,8,128]{2,1,0:T(8,128)S(1)}) custom-call(s32[2]{0:T(128)S(1)} %pad_add_fusion.first, s32[4,4,256]{2,1,0:T(4,128)S(1)} %copy-done.1, bf16[2,256,1024]{2,1,0:T(8,128)(2,1)S(1)} %collective-permute-done.2.north, bf16[4,256,1024]{2,1,0:T(8,128)(2,1)S(1)} %pad_maximum_fusion.mid, ...), custom_call_target="tpu_custom_call" | custom-call | tf_op jit(solution)/shard_map/whiten/pallas_call | solution.py:371
  146.1 1.6 collective-permute-start.9
  147.7 0.5 broadcast.85
  148.2 0.8 reduce.5
  149.0 0.1 reshape.120
  149.2 0.1 reshape.121
  149.3 0.6 gather_fusion
  149.9 0.1 broadcast_select_fusion
  150.1 14.2 %cross_near.1.refs_4_ = f32[4096,256]{1,0:T(8,128)S(1)} custom-call(f32[1]{0:T(128)S(6)} %div.12.s.refs_0_, f32[4,2,1024]{2,1,0:T(2,128)S(1)} %pad_maximum_fusion.4.t, f32[2,2048]{1,0:T(2,128)S(1)} %pad_maximum_fusion.5.p, bf16[2048,256]{1,0:T(8,128)(2,1)} %get-tuple-element.21.w), custom_call_target="tpu_custom_call" | custom-call | tf_op jit(solution)/shard_map/cross_near/pallas_call | solution.py:461
  164.4 3.2 %cross_far.3 = bf16[1024,256]{1,0:T(8,128)(2,1)S(1)} custom-call(f32[1]{0:T(128)S(6)} %div.12.s.refs_0_, f32[1,2,1024]{2,1,0:T(2,128)S(1)} %get-tuple-element.33.refs_1_, f32[2,2048]{1,0:T(2,128)S(1)} %collective-permute-done.8.refs_2_, bf16[2048,256]{1,0:T(8,128)(2,1)S(1)} %collective-permute-done.9.refs_3_, f32[4096,256]{1,0:T(8,128)S(1)} %cross_near.1.refs_4_), custom_call_target="tpu_custom_call" | custom-call | tf_op jit(solution)/shard_map/cross_far/pallas_call | solution.py:461
  167.6 3.4 %collective-permute-start.10 = (bf16[1024,256]{1,0:T(8,128)(2,1)S(1)}, bf16[1024,256]{1,0:T(8,128)(2,1)S(1)}, u32[]{:S(2)}, u32[]{:S(2)}) collective-permute-start(bf16[1024,256]{1,0:T(8,128)(2,1)S(1)} %cross_far.3), channel_id=1, source_target_pairs={{0,4},{1,5},{2,6},{3,7},{4,0},{5,1},{6,2},{7,3},{8,12},{9,13},{10,... | collective-permute-start | bytes 1572872 | tf_op jit(solution)/shard_map/ppermute | solution.py:572
  170.9 3.2 %cross_far.4 = bf16[1024,256]{1,0:T(8,128)(2,1)S(1)} custom-call(f32[1]{0:T(128)S(6)} %div.12.s.refs_0_, f32[1,2,1024]{2,1,0:T(2,128)S(1)} %get-tuple-element.35.refs_1_, f32[2,2048]{1,0:T(2,128)S(1)} %collective-permute-done.8.refs_2_, bf16[2048,256]{1,0:T(8,128)(2,1)S(1)} %collective-permute-done.9.refs_3_, f32[4096,256]{1,0:T(8,128)S(1)} %cross_near.1.refs_4_), custom_call_target="tpu_custom_call" | custom-call | tf_op jit(solution)/shard_map/cross_far/pallas_call | solution.py:461
  174.1 0.5 collective-permute-start.11
  174.6 3.2 %cross_far.5 = bf16[1024,256]{1,0:T(8,128)(2,1)S(1)} custom-call(f32[1]{0:T(128)S(6)} %div.12.s.refs_0_, f32[1,2,1024]{2,1,0:T(2,128)S(1)} %get-tuple-element.36.refs_1_, f32[2,2048]{1,0:T(2,128)S(1)} %collective-permute-done.8.refs_2_, bf16[2048,256]{1,0:T(8,128)(2,1)S(1)} %collective-permute-done.9.refs_3_, f32[4096,256]{1,0:T(8,128)S(1)} %cross_near.1.refs_4_), custom_call_target="tpu_custom_call" | custom-call | tf_op jit(solution)/shard_map/cross_far/pallas_call | solution.py:461
  177.7 2.6 %collective-permute-start.12 = (bf16[1024,256]{1,0:T(8,128)(2,1)S(1)}, bf16[1024,256]{1,0:T(8,128)(2,1)S(1)}, u32[]{:S(2)}, u32[]{:S(2)}) collective-permute-start(bf16[1024,256]{1,0:T(8,128)(2,1)S(1)} %cross_far.5), channel_id=1, source_target_pairs={{0,6},{1,7},{2,0},{3,1},{4,2},{5,3},{6,4},{7,5},{8,14},{9,15},{10,... | collective-permute-start | bytes 1572872 | tf_op jit(solution)/shard_map/ppermute | solution.py:572
  180.3 3.2 %cross_here.1 = f32[1024,256]{1,0:T(8,128)S(1)} custom-call(f32[1]{0:T(128)S(6)} %div.12.s.refs_0_, f32[1,2,1024]{2,1,0:T(2,128)S(1)} %get-tuple-element.34.refs_1_, f32[2,2048]{1,0:T(2,128)S(1)} %collective-permute-done.8.refs_2_, bf16[2048,256]{1,0:T(8,128)(2,1)S(1)} %collective-permute-done.9.refs_3_, f32[4096,256]{1,0:T(8,128)S(1)} %cross_near.1.refs_4_), custom_call_target="tpu_custom_call" | custom-call | tf_op jit(solution)/shard_map/cross_here/pallas_call | solution.py:461
  183.5 0.3 collective-permute-done.11
  183.8 3.1 %collective-permute-done.12 = bf16[1024,256]{1,0:T(8,128)(2,1)S(1)} collective-permute-done((bf16[1024,256]{1,0:T(8,128)(2,1)S(1)}, bf16[1024,256]{1,0:T(8,128)(2,1)S(1)}, u32[]{:S(2)}, u32[]{:S(2)}) %collective-permute-start.12) | collective-permute-done | bytes 524320 | tf_op jit(solution)/shard_map/ppermute | solution.py:572
  186.9 1.1 multiply_convert_fusion
  187.9 11.1 %all-to-all-start.1 = ((bf16[16,64,256]{2,1,0:T(8,128)(2,1)}), bf16[16,64,256]{2,1,0:T(8,128)(2,1)S(1)}, u32[]{:S(2)}, u32[]{:S(2)}) async-start(bf16[16,64,256]{2,1,0:T(8,128)(2,1)} %bitcast.15), calls=%async_computation.1 | async-start | bytes 1048576 | tf_op jit(solution)/shard_map/all_to_all | solution.py:576
  199.0 0.7 slice_reduce_fusion
  199.7 10.5 %all-to-all-done.1 = bf16[16,64,256]{2,1,0:T(8,128)(2,1)S(1)} async-done(((bf16[16,64,256]{2,1,0:T(8,128)(2,1)}), bf16[16,64,256]{2,1,0:T(8,128)(2,1)S(1)}, u32[]{:S(2)}, u32[]{:S(2)}) %all-to-all-start.1) | async-done | bytes 524320 | tf_op jit(solution)/shard_map/all_to_all | solution.py:576
  210.1 1.9 gather_fusion.1
  212.1 0.8 convert_element_type.31
  (47 shorter events, 0.5 us)
Async XLA Ops:
  3.1 1.7 copy-start.4
  3.1 8.2 %copy-start.6 = (f32[2,4,4,128]{3,2,1,0:T(4,128)S(1)}, f32[2,4,4,128]{3,2,1,0:T(4,128)}, u32[]{:S(2)}) copy-start(f32[2,4,4,128]{3,2,1,0:T(4,128)} %param.9) | copy-start | bytes 49156
  3.1 8.2 %copy-start.5 = (f32[4,4,128]{2,1,0:T(4,128)S(1)}, f32[4,4,128]{2,1,0:T(4,128)}, u32[]{:S(2)}) copy-start(f32[4,4,128]{2,1,0:T(4,128)} %param.10) | copy-start | bytes 24580
  3.1 13.6 %copy-start.2 = (f32[2,512]{1,0:T(2,128)S(1)}, f32[2,512]{1,0:T(2,128)}, u32[]{:S(2)}) copy-start(f32[2,512]{1,0:T(2,128)} %spots.1) | copy-start | bytes 12292
  3.1 13.6 %copy-start.3 = (s32[512,1]{0,1:T(1,128)S(1)}, s32[512,1]{0,1:T(1,128)}, u32[]{:S(2)}) copy-start(s32[512,1]{0,1:T(1,128)} %param.13) | copy-start | bytes 6148
  4.8 27.3 %collective-permute-start = (bf16[4,256,256]{2,1,0:T(8,128)(2,1)}, bf16[4,256,256]{2,1,0:T(8,128)(2,1)}, u32[]{:S(2)}, u32[]{:S(2)}) collective-permute-start(bf16[4,256,256]{2,1,0:T(8,128)(2,1)} %get-tuple-element.28), channel_id=1, source_target_pairs={{0,1},{1,2},{2,3},{3,4},{4,5},{5,6},{6,7},{8,9},{9,10},{10,11},{11... | collective-permute-start | bytes 1572872 | tf_op jit(solution)/shard_map/ppermute | solution.py:520
  10.0 22.1 %collective-permute-start.1 = (bf16[4,256,256]{2,1,0:T(8,128)(2,1)}, bf16[4,256,256]{2,1,0:T(8,128)(2,1)}, u32[]{:S(2)}, u32[]{:S(2)}) collective-permute-start(bf16[4,256,256]{2,1,0:T(8,128)(2,1)} %get-tuple-element.27), channel_id=1, source_target_pairs={{1,0},{2,1},{3,2},{4,3},{5,4},{6,5},{7,6},{9,8},{10,9},{11,10},{12... | collective-permute-start | bytes 1572872 | tf_op jit(solution)/shard_map/ppermute | solution.py:520
  11.4 33.0 %collective-permute-start.4 = (f32[4,2,8,128]{3,2,1,0:T(8,128)S(1)}, f32[4,2,8,128]{3,2,1,0:T(8,128)S(1)}, u32[]{:S(2)}, u32[]{:S(2)}) collective-permute-start(f32[4,2,8,128]{3,2,1,0:T(8,128)S(1)} %get-tuple-element.31), channel_id=1, source_target_pairs={{0,1},{1,2},{2,3},{3,4},{4,5},{5,6},{6,7},{8,9},{9,10},{10,11},{11... | collective-permute-start | bytes 98312 | tf_op jit(solution)/shard_map/ppermute | solution.py:520
  15.4 29.1 %collective-permute-start.5 = (f32[4,2,8,128]{3,2,1,0:T(8,128)S(1)}, f32[4,2,8,128]{3,2,1,0:T(8,128)S(1)}, u32[]{:S(2)}, u32[]{:S(2)}) collective-permute-start(f32[4,2,8,128]{3,2,1,0:T(8,128)S(1)} %get-tuple-element.32), channel_id=1, source_target_pairs={{1,0},{2,1},{3,2},{4,3},{5,4},{6,5},{7,6},{9,8},{10,9},{11,10},{12... | collective-permute-start | bytes 98312 | tf_op jit(solution)/shard_map/ppermute | solution.py:520
  17.7 129.9 %all-to-all-start = ((f32[128,1,128]{2,1,0:T(1,128)}), f32[128,1,128]{2,1,0:T(1,128)S(1)}, u32[]{:S(2)}, u32[]{:S(2)}) async-start(f32[128,1,128]{2,1,0:T(1,128)} %bitcast.8), calls=%async_computation | async-start | bytes 131072 | tf_op jit(solution)/shard_map/all_to_all | solution.py:543
  35.1 83.6 %collective-permute-start.2 = (bf16[2,256,1024]{2,1,0:T(8,128)(2,1)}, bf16[2,256,1024]{2,1,0:T(8,128)(2,1)S(1)}, u32[]{:S(2)}, u32[]{:S(2)}) collective-permute-start(bf16[2,256,1024]{2,1,0:T(8,128)(2,1)} %get-tuple-element.26), channel_id=1, source_target_pairs={{0,8},{8,16},{16,24},{24,32},{32,40},{40,48},{48,56},{56,64},{64,7... | collective-permute-start | bytes 3145736 | tf_op jit(solution)/shard_map/ppermute | solution.py:520
  42.3 76.5 %collective-permute-start.3 = (bf16[2,256,1024]{2,1,0:T(8,128)(2,1)}, bf16[2,256,1024]{2,1,0:T(8,128)(2,1)}, u32[]{:S(2)}, u32[]{:S(2)}) collective-permute-start(bf16[2,256,1024]{2,1,0:T(8,128)(2,1)} %get-tuple-element.25), channel_id=1, source_target_pairs={{8,0},{16,8},{24,16},{32,24},{40,32},{48,40},{56,48},{64,56},{72,6... | collective-permute-start | bytes 3145736 | tf_op jit(solution)/shard_map/ppermute | solution.py:520
  45.2 22.0 %collective-permute-start.6 = (f32[2,8,8,128]{3,2,1,0:T(8,128)}, f32[2,8,8,128]{3,2,1,0:T(8,128)S(1)}, u32[]{:S(2)}, u32[]{:S(2)}) collective-permute-start(f32[2,8,8,128]{3,2,1,0:T(8,128)} %get-tuple-element.29), channel_id=1, source_target_pairs={{0,8},{8,16},{16,24},{24,32},{32,40},{40,48},{48,56},{56,64},{64,7... | collective-permute-start | bytes 196616 | tf_op jit(solution)/shard_map/ppermute | solution.py:520
  50.3 16.8 %collective-permute-start.7 = (f32[2,8,8,128]{3,2,1,0:T(8,128)}, f32[2,8,8,128]{3,2,1,0:T(8,128)S(1)}, u32[]{:S(2)}, u32[]{:S(2)}) collective-permute-start(f32[2,8,8,128]{3,2,1,0:T(8,128)} %get-tuple-element.30), channel_id=1, source_target_pairs={{8,0},{16,8},{24,16},{32,24},{40,32},{48,40},{56,48},{64,56},{72,6... | collective-permute-start | bytes 196616 | tf_op jit(solution)/shard_map/ppermute | solution.py:520
  52.2 14.9 %copy-start.1 = (s32[4,4,256]{2,1,0:T(4,128)S(1)}, s32[4,4,256]{2,1,0:T(4,128)}, u32[]{:S(2)}) copy-start(s32[4,4,256]{2,1,0:T(4,128)} %nb.3) | copy-start | bytes 49156
  52.3 112.1 %collective-permute-start.8 = (f32[2,2048]{1,0:T(2,128)S(1)}, f32[2,2048]{1,0:T(2,128)S(1)}, u32[]{:S(2)}, u32[]{:S(2)}) collective-permute-start(f32[2,2048]{1,0:T(2,128)S(1)} %pad_maximum_fusion.5.p), channel_id=1, source_target_pairs={{0,1},{1,0},{2,3},{3,2},{4,5},{5,4},{6,7},{7,6},{8,9},{9,8},{10,11... | collective-permute-start | bytes 49160 | tf_op jit(solution)/shard_map/ppermute | solution.py:555
  118.8 1.6 copy-start
  120.4 27.3 %copy-start.7 = (s32[4]{0:T(128)S(1)}, s32[4]{0:T(128)}, u32[]{:S(2)}) copy-start(s32[4]{0:T(128)} %constant.91.clone) | copy-start | bytes 52
  146.1 18.3 %collective-permute-start.9 = (bf16[2048,256]{1,0:T(8,128)(2,1)}, bf16[2048,256]{1,0:T(8,128)(2,1)S(1)}, u32[]{:S(2)}, u32[]{:S(2)}) collective-permute-start(bf16[2048,256]{1,0:T(8,128)(2,1)} %get-tuple-element.21.w), channel_id=1, source_target_pairs={{0,1},{1,0},{2,3},{3,2},{4,5},{5,4},{6,7},{7,6},{8,9},{9,8},{10,11... | collective-permute-start | bytes 3145736 | tf_op jit(solution)/shard_map/ppermute | solution.py:564
  167.6 16.0 %collective-permute-start.10 = (bf16[1024,256]{1,0:T(8,128)(2,1)S(1)}, bf16[1024,256]{1,0:T(8,128)(2,1)S(1)}, u32[]{:S(2)}, u32[]{:S(2)}) collective-permute-start(bf16[1024,256]{1,0:T(8,128)(2,1)S(1)} %cross_far.3), channel_id=1, source_target_pairs={{0,4},{1,5},{2,6},{3,7},{4,0},{5,1},{6,2},{7,3},{8,12},{9,13},{10,... | collective-permute-start | bytes 1572872 | tf_op jit(solution)/shard_map/ppermute | solution.py:572
  174.1 9.7 %collective-permute-start.11 = (bf16[1024,256]{1,0:T(8,128)(2,1)S(1)}, bf16[1024,256]{1,0:T(8,128)(2,1)S(1)}, u32[]{:S(2)}, u32[]{:S(2)}) collective-permute-start(bf16[1024,256]{1,0:T(8,128)(2,1)S(1)} %cross_far.4), channel_id=1, source_target_pairs={{0,2},{1,3},{2,4},{3,5},{4,6},{5,7},{6,0},{7,1},{8,10},{9,11},{10,... | collective-permute-start | bytes 1572872 | tf_op jit(solution)/shard_map/ppermute | solution.py:572
  177.7 9.1 %collective-permute-start.12 = (bf16[1024,256]{1,0:T(8,128)(2,1)S(1)}, bf16[1024,256]{1,0:T(8,128)(2,1)S(1)}, u32[]{:S(2)}, u32[]{:S(2)}) collective-permute-start(bf16[1024,256]{1,0:T(8,128)(2,1)S(1)} %cross_far.5), channel_id=1, source_target_pairs={{0,6},{1,7},{2,0},{3,1},{4,2},{5,3},{6,4},{7,5},{8,14},{9,15},{10,... | collective-permute-start | bytes 1572872 | tf_op jit(solution)/shard_map/ppermute | solution.py:572
  187.9 22.2 %all-to-all-start.1 = ((bf16[16,64,256]{2,1,0:T(8,128)(2,1)}), bf16[16,64,256]{2,1,0:T(8,128)(2,1)S(1)}, u32[]{:S(2)}, u32[]{:S(2)}) async-start(bf16[16,64,256]{2,1,0:T(8,128)(2,1)} %bitcast.15), calls=%async_computation.1 | async-start | bytes 1048576 | tf_op jit(solution)/shard_map/all_to_all | solution.py:576

commit v2 on v1

--- a/solution.py
+++ b/solution.py
@@ -317,7 +317,7 @@
     )(first, length, nb, geo)
 
 
-def whiten_kernel(first, nb, north, mid, south, g, w3, own, white, weights, term, tab, acc):
+def whiten_kernel(first, nb, north, mid, south, g, w3, own, white, weights, term, tab, acc, lhs):
     ci = pl.program_id(0)
 
     @pl.when(ci == 0)
@@ -325,30 +325,39 @@
         tab[0:2] = north[...]
         tab[2:6] = mid[...]
         tab[6:8] = south[...]
+        for wi in range(5):
+            for cj, q in ((0, 5), (1, 0), (2, 7), (3, 2)):
+                lhs[wi, 128 * cj : 128 * cj + 128, 128 * q : 128 * q + 128] = jnp.zeros((128, 128), BF)
 
     point = lax.broadcasted_iota(jnp.int32, (128, 256), 0)
-    near = []
     for cj in range(4):
         _, _, w, member = window(first, nb, 4 * ci + cj)
-        pick = jnp.where(point == jnp.broadcast_to(member, (128, 256)), 1.0, 0.0).astype(BF)
-        near.append((w, pick, g[cj].astype(F32)))
+        here = point == jnp.broadcast_to(member, (128, 256))
+        odd = jnp.broadcast_to(w & 1, (128, 256)) == 1
+        pick = jnp.concatenate(
+            [
+                jnp.where(here & ~odd, 1.0, 0.0).astype(BF),
+                jnp.where(here & odd, 1.0, 0.0).astype(BF),
+            ],
+            0,
+        )
+        gf = g[cj].astype(F32)
+        pair = w >> 1
+        for p in range(13):
+            s = dot(jnp.where(pair == p, gf, 0.0).astype(BF), pick, NT).astype(BF)
+            for h in range(2):
+                wi, wj = divmod(2 * p + h, 5)
+                if wi < 5:
+                    at = 128 * (cj + wj)
+                    lhs[wi, 128 * cj : 128 * cj + 128, at : at + 128] = s[:, 128 * h : 128 * h + 128]
         acc[128 * cj : 128 * cj + 128, :] = mm_nt(w3[cj], own[0, :, 128 * cj : 128 * cj + 128])
-    blank = [jnp.zeros((128, 128), BF)] * 4
-
-    def one_row(wi, _):
-        rows = []
-        for cj in range(4):
-            w, pick, gf = near[cj]
-            lhs = jnp.concatenate(
-                [jnp.where(w == wi * 5 + wj, gf, 0.0).astype(BF) for wj in range(5)], 0
-            )
-            gs = dot(lhs, pick, NT).astype(BF)
-            blocks = [gs[128 * wj : 128 * wj + 128, :] for wj in range(5)]
-            rows.append(jnp.concatenate(blank[:cj] + blocks + blank[cj + 1 :], 1))
-        acc[...] = acc[...] - dot(jnp.concatenate(rows, 0), tab[ci + wi], NT)
-        return 0
-
-    lax.fori_loop(0, 5, one_row, 0)
+
+    for wi in range(5):
+        row = tab.at[ci + wi]
+        both = dot(lhs[wi, :, 256:768], row[:, 256:768], NT)
+        left = dot(lhs[wi, :256, :256], row[:, :256], NT)
+        right = dot(lhs[wi, 256:, 768:], row[:, 768:], NT)
+        acc[...] = acc[...] - both - jnp.concatenate([left, right], 0)
     weights[...] = acc[...].astype(BF)
     eye = (
         lax.broadcasted_iota(jnp.int32, (128, 128), 0)
@@ -388,7 +397,8 @@
             pl.BlockSpec((512, 256), lambda s: (s, 0)),
             pl.BlockSpec((1, 8, 128), lambda s: (s, 0, 0)),
         ),
-        scratch_shapes=[pltpu.VMEM((8, 256, 1024), BF), pltpu.VMEM((512, 256), F32)],
+        scratch_shapes=[pltpu.VMEM((8, 256, 1024), BF), pltpu.VMEM((512, 256), F32),
+            pltpu.VMEM((5, 512, 1024), BF)],
         compiler_params=pltpu.CompilerParams(vmem_limit_bytes=24 << 20),
         name="whiten",
     )(first, nb, *pieces, g, w3, own)
@@ -529,8 +539,9 @@
     geo = jnp.concatenate(
         [offsets.transpose(1, 2, 0, 3), nugget[:, :, None, :], jnp.zeros((4, 4, 5, 128), F32)], 2
     )
-    w, e = sides(geo[:, :2], geo[:, 2:], "cols")
-    geo = jnp.concatenate([w, geo, e], 1)
+    w, e = sides(geo, geo, "cols")
+    partner_geo = jnp.where(col % 2 == 0, e, w)
+    geo = jnp.concatenate([w[:, 2:], geo, e[:, :2]], 1)
     n, s = sides(geo[:2], geo[2:], "rows")
     geo = jnp.concatenate([n, geo, s], 0)
 
@@ -552,7 +563,9 @@
     py = offsets[1] + (jnp.arange(4, dtype=F32) - 4.0 + 4.0 * half.astype(F32))[None, :, None]
     pts = jnp.stack([px.reshape(-1), py.reshape(-1)])
     partner = [(c, c ^ 1) for c in range(8)]
-    pts2 = lax.ppermute(pts, "cols", partner)
+    px = partner_geo[:, :, 0] + (jnp.arange(4, dtype=F32) - 2.0)[:, None, None]
+    py = partner_geo[:, :, 1] + (jnp.arange(4, dtype=F32) - 4.0 * half.astype(F32))[None, :, None]
+    pts2 = jnp.stack([px.reshape(-1), py.reshape(-1)])
 
     first, w, e = lax.optimization_barrier((first, w, e))
     mid = jnp.concatenate([w, mid, e], 2)
@@ -570,7 +583,7 @@
             scale, tgt[per * i : per * i + per], pts2, weights2, BF, near, per * i, "cross_far", FAR
         )
         parts.append(lax.ppermute(part, "cols", [(c, (c + 2 * k) % 8) for c in range(8)]))
-    here = cross(scale, tgt[3 * per :], pts2, weights2, F32, near, 3 * per, "cross_here", FAR)
+    here = cross(scale, tgt[3 * per :], pts2, weights2, F32, near, 3 * per, "cross_here", 2)
     predicted = here + (parts[0].astype(F32) + parts[1].astype(F32) + parts[2].astype(F32))
     predicted = (predicted * (1.0 / 128.0)).astype(BF)
     returned = lax.all_to_all(

time: 214 us -> 220 us (1.028)
  waiting for transfers between devices: 23.7 us -> 45.2 us
  Pallas kernels: 105 us -> 94.7 us
  starting transfers between devices: 61.9 us -> 55.8 us
  other arithmetic: 4.61 us -> 6.84 us
    ppermute x4, waiting for transfers between devices: 9.89 us -> 29.2 us  [sides(): lax.ppermute(high, axis, forward)]
    pallas_call x1, Pallas kernels: 25.7 us -> 16.1 us  [whiten(): pl.pallas_call(whiten_kernel, grid=(4,), out_shape=(jax.ShapeDtypeStruct(...]
    ppermute x4, starting transfers between devices: 21.4 us -> 17.6 us  [sides(): lax.ppermute(high, axis, forward)]
    ppermute x4, waiting for transfers between devices: 0.01 us -> 2.94 us  [sides(): lax.ppermute(low, axis, backward)]
  transfers between devices with their start and end apart: 15 -> 14, of which waited for: 5 -> 5; matrix products, arithmetic and copies ran while one was open for 5% -> 6% of each run, Pallas kernels for 48% -> 34%
where the time goes in v2:
time: 220 us; the launch traced here: 219 us
  Pallas kernels  94.7 us (43%)
  starting transfers between devices  55.8 us (25%)
  waiting for transfers between devices  45.2 us (21%)
  local copies, waits for them, and re-layouts  14.5 us (7%)
  other arithmetic  6.84 us (3%)
    pallas_call x1, Pallas kernels, factor(): pl.pallas_call(factor_kernel, out_shape=(jax.ShapeDtypeStruct((16, 128, 2...  51.6 us
    ppermute x4, waiting for transfers between devices, sides(): lax.ppermute(high, axis, forward)  29.2 us
    pallas_call x5, Pallas kernels, cross(): pl.pallas_call(kernel, grid=(n,), out_shape=jax.ShapeDtypeStruct((n * TB,...  26 us
    ppermute x4, starting transfers between devices, sides(): lax.ppermute(high, axis, forward)  17.6 us
    pallas_call x1, Pallas kernels, whiten(): pl.pallas_call(whiten_kernel, grid=(4,), out_shape=(jax.ShapeDtypeStruct(...  16.1 us
    all_to_all x1, starting transfers between devices, body(): lax.all_to_all(predicted.reshape(16, 64, 256), 'rows', split_axis=0, conc...  12.2 us
    all_to_all x1, starting transfers between devices, body(): lax.all_to_all(everyone, ('rows', 'cols'), split_axis=0, concat_axis=0, t...  11.3 us
    all_to_all x1, waiting for transfers between devices, body(): lax.all_to_all(predicted.reshape(16, 64, 256), 'rows', split_axis=0, conc...  10.5 us
  transfers between devices with their start and end apart: 14, of which 5 were waited for; matrix products, arithmetic and copies ran while one was open for 6% of the time, Pallas kernels for 34%

profile of v2, /device:TPU:1, one launch (start us, length us, event | category | flops | bytes accessed | tf_op | source)
XLA Modules:
  0.0 218.9 jit_solution(16444650827232128713)
XLA Ops:
  0.6 0.7 copy.26
  1.4 1.3 pad_maximum_fusion.3
  2.7 1.3 collective-permute-start.5
  4.0 5.6 %collective-permute-start.4 = (f32[4,4,8,128]{3,2,1,0:T(8,128)}, f32[4,4,8,128]{3,2,1,0:T(8,128)}, u32[]{:S(2)}, u32[]{:S(2)}) collective-permute-start(f32[4,4,8,128]{3,2,1,0:T(8,128)} %pad_maximum_fusion.3), channel_id=1, source_target_pairs={{0,1},{1,2},{2,3},{3,4},{4,5},{5,6},{6,7},{8,9},{9,10},{10,11},{11... | collective-permute-start | bytes 196616 | tf_op jit(solution)/shard_map/ppermute | solution.py:530
  9.6 0.7 copy-done.1
  10.3 0.7 copy-done.2
  11.0 1.0 sort_targets.1
  12.0 11.3 %all-to-all-start = ((f32[128,1,128]{2,1,0:T(1,128)}), f32[128,1,128]{2,1,0:T(1,128)S(1)}, u32[]{:S(2)}, u32[]{:S(2)}) async-start(f32[128,1,128]{2,1,0:T(1,128)} %bitcast.8), calls=%async_computation | async-start | bytes 131072 | tf_op jit(solution)/shard_map/all_to_all | solution.py:554
  23.4 2.5 %reshape.184 = f32[4,256,512]{2,0,1:T(4,128)S(1)} reshape(f32[4,256,4,128]{3,2,0,1:T(4,128)} %bitcast.33) | data formatting | bytes 4194304 | tf_op jit(solution)/shard_map/reshape | solution.py:548
  25.9 0.6 copy.25
  26.5 1.1 fusion.8
  27.5 1.3 collective-permute-start.1
  28.8 4.9 %collective-permute-start = (bf16[4,256,256]{2,1,0:T(8,128)(2,1)}, bf16[4,256,256]{2,1,0:T(8,128)(2,1)}, u32[]{:S(2)}, u32[]{:S(2)}) collective-permute-start(bf16[4,256,256]{2,1,0:T(8,128)(2,1)} %get-tuple-element.28), channel_id=1, source_target_pairs={{0,1},{1,2},{2,3},{3,4},{4,5},{5,6},{6,7},{8,9},{9,10},{10,11},{11... | collective-permute-start | bytes 1572872 | tf_op jit(solution)/shard_map/ppermute | solution.py:530
  33.7 2.3 %copy.22.own = f32[4,256,512]{2,1,0:T(8,128)S(1)} copy(f32[4,256,512]{2,0,1:T(4,128)} %copy-done.3) | data formatting | bytes 4194304 | tf_op jit(solution)/shard_map/reshape | solution.py:548
  36.9 0.5 broadcast.93
  37.5 0.8 reduce.5
  38.3 0.1 reshape.162
  38.6 0.6 gather_fusion
  39.3 2.9 %collective-permute-done.1 = bf16[4,256,256]{2,1,0:T(8,128)(2,1)} collective-permute-done((bf16[4,256,256]{2,1,0:T(8,128)(2,1)}, bf16[4,256,256]{2,1,0:T(8,128)(2,1)}, u32[]{:S(2)}, u32[]{:S(2)}) %collective-permute-start.1) | collective-permute-done | bytes 524320 | tf_op jit(solution)/shard_map/ppermute | solution.py:530
  42.2 12.8 %collective-permute-done = bf16[4,256,256]{2,1,0:T(8,128)(2,1)} collective-permute-done((bf16[4,256,256]{2,1,0:T(8,128)(2,1)}, bf16[4,256,256]{2,1,0:T(8,128)(2,1)}, u32[]{:S(2)}, u32[]{:S(2)}) %collective-permute-start) | collective-permute-done | bytes 524320 | tf_op jit(solution)/shard_map/ppermute | solution.py:530
  55.0 1.5 pad_maximum_fusion.mid
  56.5 0.3 fusion.7
  56.8 2.4 %collective-permute-start.3 = (bf16[2,256,1024]{2,1,0:T(8,128)(2,1)S(1)}, bf16[2,256,1024]{2,1,0:T(8,128)(2,1)S(1)}, u32[]{:S(2)}, u32[]{:S(2)}) collective-permute-start(bf16[2,256,1024]{2,1,0:T(8,128)(2,1)S(1)} %get-tuple-element.25), channel_id=1, source_target_pairs={{8,0},{16,8},{24,16},{32,24},{40,32},{48,40},{56,48},{64,56},{72,6... | collective-permute-start | bytes 3145736 | tf_op jit(solution)/shard_map/ppermute | solution.py:530
  59.2 4.7 %collective-permute-start.2 = (bf16[2,256,1024]{2,1,0:T(8,128)(2,1)S(1)}, bf16[2,256,1024]{2,1,0:T(8,128)(2,1)S(1)}, u32[]{:S(2)}, u32[]{:S(2)}) collective-permute-start(bf16[2,256,1024]{2,1,0:T(8,128)(2,1)S(1)} %get-tuple-element.26), channel_id=1, source_target_pairs={{0,8},{8,16},{16,24},{24,32},{32,40},{40,48},{48,56},{56,64},{64,7... | collective-permute-start | bytes 3145736 | tf_op jit(solution)/shard_map/ppermute | solution.py:530
  64.1 0.8 slice.85
  64.8 0.8 slice.84
  65.7 2.4 %collective-permute-start.6 = (f32[2,8,8,128]{3,2,1,0:T(8,128)S(1)}, f32[2,8,8,128]{3,2,1,0:T(8,128)S(1)}, u32[]{:S(2)}, u32[]{:S(2)}) collective-permute-start(f32[2,8,8,128]{3,2,1,0:T(8,128)S(1)} %get-tuple-element.29), channel_id=1, source_target_pairs={{0,8},{8,16},{16,24},{24,32},{32,40},{40,48},{48,56},{56,64},{64,7... | collective-permute-start | bytes 196616 | tf_op jit(solution)/shard_map/ppermute | solution.py:530
  68.1 2.1 collective-permute-start.7
  70.2 0.9 broadcast_select_fusion.1
  71.0 16.4 %collective-permute-done.6 = f32[2,8,8,128]{3,2,1,0:T(8,128)S(1)} collective-permute-done((f32[2,8,8,128]{3,2,1,0:T(8,128)S(1)}, f32[2,8,8,128]{3,2,1,0:T(8,128)S(1)}, u32[]{:S(2)}, u32[]{:S(2)}) %collective-permute-start.6) | collective-permute-done | bytes 65568 | tf_op jit(solution)/shard_map/ppermute | solution.py:530
  87.5 51.6 %factor.1 = (bf16[16,128,256]{2,1,0:T(8,128)(2,1)S(1)}, f32[16,128,128]{2,1,0:T(8,128)S(1)}) custom-call(s32[2]{0:T(128)S(1)} %pad_add_fusion.first, f32[1]{0:T(128)S(6)} %copy.27.length, s32[4,4,256]{2,1,0:T(4,128)S(1)} %copy-done, f32[8,8,8,128]{3,2,1,0:T(8,128)S(1)} %pad_maximum_fusion.1.geo), custom_call_target="tpu_custom_call" | custom-call | tf_op jit(solution)/shard_map/factor/pallas_call | solution.py:299
  139.1 16.1 %whiten.1 = (f32[16,128,256]{2,1,0:T(8,128)}, bf16[2048,256]{1,0:T(8,128)(2,1)S(1)}, f32[4,8,128]{2,1,0:T(8,128)S(1)}) custom-call(s32[2]{0:T(128)S(1)} %pad_add_fusion.first, s32[4,4,256]{2,1,0:T(4,128)S(1)} %copy-done, bf16[2,256,1024]{2,1,0:T(8,128)(2,1)S(1)} %collective-permute-done.2.north, bf16[4,256,1024]{2,1,0:T(8,128)(2,1)S(1)} %pad_maximum_fusion.mid, ...), custom_call_target="tpu_custom_call" | custom-call | tf_op jit(solution)/shard_map/whiten/pallas_call | solution.py:380
  155.2 1.6 collective-permute-start.8
  157.1 13.0 %cross_near.1.refs_4_ = f32[4096,256]{1,0:T(8,128)S(1)} custom-call(f32[1]{0:T(128)S(6)} %div.12.s.refs_0_, f32[4,2,1024]{2,1,0:T(2,128)S(1)} %pad_maximum_fusion.4.t, f32[2,2048]{1,0:T(2,128)S(1)} %pad_maximum_fusion.6.p, bf16[2048,256]{1,0:T(8,128)(2,1)S(1)} %get-tuple-element.21.w), custom_call_target="tpu_custom_call" | custom-call | tf_op jit(solution)/shard_map/cross_near/pallas_call | solution.py:471
  170.1 3.2 %cross_far.3 = bf16[1024,256]{1,0:T(8,128)(2,1)S(1)} custom-call(f32[1]{0:T(128)S(6)} %div.12.s.refs_0_, f32[1,2,1024]{2,1,0:T(2,128)S(1)} %get-tuple-element.33.refs_1_, f32[2,2048]{1,0:T(2,128)S(1)} %pad_maximum_fusion.5.refs_2_, bf16[2048,256]{1,0:T(8,128)(2,1)S(1)} %collective-permute-done.8.refs_3_, f32[4096,256]{1,0:T(8,128)S(1)} %cross_near.1.refs_4_), custom_call_target="tpu_custom_call" | custom-call | tf_op jit(solution)/shard_map/cross_far/pallas_call | solution.py:471
  173.3 2.9 %collective-permute-start.9 = (bf16[1024,256]{1,0:T(8,128)(2,1)S(1)}, bf16[1024,256]{1,0:T(8,128)(2,1)S(1)}, u32[]{:S(2)}, u32[]{:S(2)}) collective-permute-start(bf16[1024,256]{1,0:T(8,128)(2,1)S(1)} %cross_far.3), channel_id=1, source_target_pairs={{0,4},{1,5},{2,6},{3,7},{4,0},{5,1},{6,2},{7,3},{8,12},{9,13},{10,... | collective-permute-start | bytes 1572872 | tf_op jit(solution)/shard_map/ppermute | solution.py:585
  176.2 3.2 %cross_far.4 = bf16[1024,256]{1,0:T(8,128)(2,1)S(1)} custom-call(f32[1]{0:T(128)S(6)} %div.12.s.refs_0_, f32[1,2,1024]{2,1,0:T(2,128)S(1)} %get-tuple-element.35.refs_1_, f32[2,2048]{1,0:T(2,128)S(1)} %pad_maximum_fusion.5.refs_2_, bf16[2048,256]{1,0:T(8,128)(2,1)S(1)} %collective-permute-done.8.refs_3_, f32[4096,256]{1,0:T(8,128)S(1)} %cross_near.1.refs_4_), custom_call_target="tpu_custom_call" | custom-call | tf_op jit(solution)/shard_map/cross_far/pallas_call | solution.py:471
  179.3 0.3 collective-permute-start.10
  179.7 3.2 %cross_far.5 = bf16[1024,256]{1,0:T(8,128)(2,1)S(1)} custom-call(f32[1]{0:T(128)S(6)} %div.12.s.refs_0_, f32[1,2,1024]{2,1,0:T(2,128)S(1)} %get-tuple-element.36.refs_1_, f32[2,2048]{1,0:T(2,128)S(1)} %pad_maximum_fusion.5.refs_2_, bf16[2048,256]{1,0:T(8,128)(2,1)S(1)} %collective-permute-done.8.refs_3_, f32[4096,256]{1,0:T(8,128)S(1)} %cross_near.1.refs_4_), custom_call_target="tpu_custom_call" | custom-call | tf_op jit(solution)/shard_map/cross_far/pallas_call | solution.py:471
  182.9 2.7 %collective-permute-start.11 = (bf16[1024,256]{1,0:T(8,128)(2,1)S(1)}, bf16[1024,256]{1,0:T(8,128)(2,1)S(1)}, u32[]{:S(2)}, u32[]{:S(2)}) collective-permute-start(bf16[1024,256]{1,0:T(8,128)(2,1)S(1)} %cross_far.5), channel_id=1, source_target_pairs={{0,6},{1,7},{2,0},{3,1},{4,2},{5,3},{6,4},{7,5},{8,14},{9,15},{10,... | collective-permute-start | bytes 1572872 | tf_op jit(solution)/shard_map/ppermute | solution.py:585
  185.6 3.5 %cross_here.1 = f32[1024,256]{1,0:T(8,128)S(1)} custom-call(f32[1]{0:T(128)S(6)} %div.12.s.refs_0_, f32[1,2,1024]{2,1,0:T(2,128)S(1)} %get-tuple-element.34.refs_1_, f32[2,2048]{1,0:T(2,128)S(1)} %pad_maximum_fusion.5.refs_2_, bf16[2048,256]{1,0:T(8,128)(2,1)S(1)} %collective-permute-done.8.refs_3_, f32[4096,256]{1,0:T(8,128)S(1)} %cross_near.1.refs_4_), custom_call_target="tpu_custom_call" | custom-call | tf_op jit(solution)/shard_map/cross_here/pallas_call | solution.py:471
  189.1 2.6 %collective-permute-done.11 = bf16[1024,256]{1,0:T(8,128)(2,1)S(1)} collective-permute-done((bf16[1024,256]{1,0:T(8,128)(2,1)S(1)}, bf16[1024,256]{1,0:T(8,128)(2,1)S(1)}, u32[]{:S(2)}, u32[]{:S(2)}) %collective-permute-start.11) | collective-permute-done | bytes 524320 | tf_op jit(solution)/shard_map/ppermute | solution.py:585
  191.7 1.1 multiply_convert_fusion
  192.8 12.2 %all-to-all-start.1 = ((bf16[16,64,256]{2,1,0:T(8,128)(2,1)}), bf16[16,64,256]{2,1,0:T(8,128)(2,1)S(1)}, u32[]{:S(2)}, u32[]{:S(2)}) async-start(bf16[16,64,256]{2,1,0:T(8,128)(2,1)} %bitcast.18), calls=%async_computation.1 | async-start | bytes 1048576 | tf_op jit(solution)/shard_map/all_to_all | solution.py:589
  205.0 0.7 slice_reduce_fusion
  205.6 10.5 %all-to-all-done.1 = bf16[16,64,256]{2,1,0:T(8,128)(2,1)S(1)} async-done(((bf16[16,64,256]{2,1,0:T(8,128)(2,1)}), bf16[16,64,256]{2,1,0:T(8,128)(2,1)S(1)}, u32[]{:S(2)}, u32[]{:S(2)}) %all-to-all-start.1) | async-done | bytes 524320 | tf_op jit(solution)/shard_map/all_to_all | solution.py:589
  216.1 1.9 gather_fusion.1
  218.0 0.8 convert_element_type.32
  (49 shorter events, 0.9 us)
Async XLA Ops:
  2.7 61.3 %collective-permute-start.5 = (f32[4,4,8,128]{3,2,1,0:T(8,128)}, f32[4,4,8,128]{3,2,1,0:T(8,128)}, u32[]{:S(2)}, u32[]{:S(2)}) collective-permute-start(f32[4,4,8,128]{3,2,1,0:T(8,128)} %pad_maximum_fusion.3), channel_id=1, source_target_pairs={{1,0},{2,1},{3,2},{4,3},{5,4},{6,5},{7,6},{9,8},{10,9},{11,10},{12... | collective-permute-start | bytes 196616 | tf_op jit(solution)/shard_map/ppermute | solution.py:530
  4.0 60.8 %collective-permute-start.4 = (f32[4,4,8,128]{3,2,1,0:T(8,128)}, f32[4,4,8,128]{3,2,1,0:T(8,128)}, u32[]{:S(2)}, u32[]{:S(2)}) collective-permute-start(f32[4,4,8,128]{3,2,1,0:T(8,128)} %pad_maximum_fusion.3), channel_id=1, source_target_pairs={{0,1},{1,2},{2,3},{3,4},{4,5},{5,6},{6,7},{8,9},{9,10},{10,11},{11... | collective-permute-start | bytes 196616 | tf_op jit(solution)/shard_map/ppermute | solution.py:530
  9.6 0.7 copy-start.1
  10.3 0.7 copy-start.2
  12.0 24.9 %all-to-all-start = ((f32[128,1,128]{2,1,0:T(1,128)}), f32[128,1,128]{2,1,0:T(1,128)S(1)}, u32[]{:S(2)}, u32[]{:S(2)}) async-start(f32[128,1,128]{2,1,0:T(1,128)} %bitcast.8), calls=%async_computation | async-start | bytes 131072 | tf_op jit(solution)/shard_map/all_to_all | solution.py:554
  25.8 1.7 copy-start.3
  25.9 7.8 %copy-start.5 = (f32[2,4,4,128]{3,2,1,0:T(4,128)S(1)}, f32[2,4,4,128]{3,2,1,0:T(4,128)}, u32[]{:S(2)}) copy-start(f32[2,4,4,128]{3,2,1,0:T(4,128)} %param.9) | copy-start | bytes 49156
  27.5 14.7 %collective-permute-start.1 = (bf16[4,256,256]{2,1,0:T(8,128)(2,1)}, bf16[4,256,256]{2,1,0:T(8,128)(2,1)}, u32[]{:S(2)}, u32[]{:S(2)}) collective-permute-start(bf16[4,256,256]{2,1,0:T(8,128)(2,1)} %get-tuple-element.27), channel_id=1, source_target_pairs={{1,0},{2,1},{3,2},{4,3},{5,4},{6,5},{7,6},{9,8},{10,9},{11,10},{12... | collective-permute-start | bytes 1572872 | tf_op jit(solution)/shard_map/ppermute | solution.py:530
  28.8 26.2 %collective-permute-start = (bf16[4,256,256]{2,1,0:T(8,128)(2,1)}, bf16[4,256,256]{2,1,0:T(8,128)(2,1)}, u32[]{:S(2)}, u32[]{:S(2)}) collective-permute-start(bf16[4,256,256]{2,1,0:T(8,128)(2,1)} %get-tuple-element.28), channel_id=1, source_target_pairs={{0,1},{1,2},{2,3},{3,4},{4,5},{5,6},{6,7},{8,9},{9,10},{10,11},{11... | collective-permute-start | bytes 1572872 | tf_op jit(solution)/shard_map/ppermute | solution.py:530
  33.7 3.0 %copy-start.6 = (s32[4]{0:T(128)S(1)}, s32[4]{0:T(128)}, u32[]{:S(2)}) copy-start(s32[4]{0:T(128)} %constant.94.clone) | copy-start | bytes 52
  56.5 9.1 %copy-start.4 = (f32[4,4,128]{2,1,0:T(4,128)S(1)}, f32[4,4,128]{2,1,0:T(4,128)}, u32[]{:S(2)}) copy-start(f32[4,4,128]{2,1,0:T(4,128)} %param.10) | copy-start | bytes 24580
  56.5 31.0 %copy-start = (s32[4,4,256]{2,1,0:T(4,128)S(1)}, s32[4,4,256]{2,1,0:T(4,128)}, u32[]{:S(2)}) copy-start(s32[4,4,256]{2,1,0:T(4,128)} %nb.3) | copy-start | bytes 49156
  56.8 82.3 %collective-permute-start.3 = (bf16[2,256,1024]{2,1,0:T(8,128)(2,1)S(1)}, bf16[2,256,1024]{2,1,0:T(8,128)(2,1)S(1)}, u32[]{:S(2)}, u32[]{:S(2)}) collective-permute-start(bf16[2,256,1024]{2,1,0:T(8,128)(2,1)S(1)} %get-tuple-element.25), channel_id=1, source_target_pairs={{8,0},{16,8},{24,16},{32,24},{40,32},{48,40},{56,48},{64,56},{72,6... | collective-permute-start | bytes 3145736 | tf_op jit(solution)/shard_map/ppermute | solution.py:530
  59.2 79.9 %collective-permute-start.2 = (bf16[2,256,1024]{2,1,0:T(8,128)(2,1)S(1)}, bf16[2,256,1024]{2,1,0:T(8,128)(2,1)S(1)}, u32[]{:S(2)}, u32[]{:S(2)}) collective-permute-start(bf16[2,256,1024]{2,1,0:T(8,128)(2,1)S(1)} %get-tuple-element.26), channel_id=1, source_target_pairs={{0,8},{8,16},{16,24},{24,32},{32,40},{40,48},{48,56},{56,64},{64,7... | collective-permute-start | bytes 3145736 | tf_op jit(solution)/shard_map/ppermute | solution.py:530
  65.7 21.8 %collective-permute-start.6 = (f32[2,8,8,128]{3,2,1,0:T(8,128)S(1)}, f32[2,8,8,128]{3,2,1,0:T(8,128)S(1)}, u32[]{:S(2)}, u32[]{:S(2)}) collective-permute-start(f32[2,8,8,128]{3,2,1,0:T(8,128)S(1)} %get-tuple-element.29), channel_id=1, source_target_pairs={{0,8},{8,16},{16,24},{24,32},{32,40},{40,48},{48,56},{56,64},{64,7... | collective-permute-start | bytes 196616 | tf_op jit(solution)/shard_map/ppermute | solution.py:530
  68.1 19.4 %collective-permute-start.7 = (f32[2,8,8,128]{3,2,1,0:T(8,128)S(1)}, f32[2,8,8,128]{3,2,1,0:T(8,128)S(1)}, u32[]{:S(2)}, u32[]{:S(2)}) collective-permute-start(f32[2,8,8,128]{3,2,1,0:T(8,128)S(1)} %get-tuple-element.30), channel_id=1, source_target_pairs={{8,0},{16,8},{24,16},{32,24},{40,32},{48,40},{56,48},{64,56},{72,6... | collective-permute-start | bytes 196616 | tf_op jit(solution)/shard_map/ppermute | solution.py:530
  155.2 14.9 %collective-permute-start.8 = (bf16[2048,256]{1,0:T(8,128)(2,1)S(1)}, bf16[2048,256]{1,0:T(8,128)(2,1)S(1)}, u32[]{:S(2)}, u32[]{:S(2)}) collective-permute-start(bf16[2048,256]{1,0:T(8,128)(2,1)S(1)} %get-tuple-element.21.w), channel_id=1, source_target_pairs={{0,1},{1,0},{2,3},{3,2},{4,5},{5,4},{6,7},{7,6},{8,9},{9,8},{10,11... | collective-permute-start | bytes 3145736 | tf_op jit(solution)/shard_map/ppermute | solution.py:577
  173.3 15.9 %collective-permute-start.9 = (bf16[1024,256]{1,0:T(8,128)(2,1)S(1)}, bf16[1024,256]{1,0:T(8,128)(2,1)S(1)}, u32[]{:S(2)}, u32[]{:S(2)}) collective-permute-start(bf16[1024,256]{1,0:T(8,128)(2,1)S(1)} %cross_far.3), channel_id=1, source_target_pairs={{0,4},{1,5},{2,6},{3,7},{4,0},{5,1},{6,2},{7,3},{8,12},{9,13},{10,... | collective-permute-start | bytes 1572872 | tf_op jit(solution)/shard_map/ppermute | solution.py:585
  179.3 9.8 %collective-permute-start.10 = (bf16[1024,256]{1,0:T(8,128)(2,1)S(1)}, bf16[1024,256]{1,0:T(8,128)(2,1)S(1)}, u32[]{:S(2)}, u32[]{:S(2)}) collective-permute-start(bf16[1024,256]{1,0:T(8,128)(2,1)S(1)} %cross_far.4), channel_id=1, source_target_pairs={{0,2},{1,3},{2,4},{3,5},{4,6},{5,7},{6,0},{7,1},{8,10},{9,11},{10,... | collective-permute-start | bytes 1572872 | tf_op jit(solution)/shard_map/ppermute | solution.py:585
  182.9 8.9 %collective-permute-start.11 = (bf16[1024,256]{1,0:T(8,128)(2,1)S(1)}, bf16[1024,256]{1,0:T(8,128)(2,1)S(1)}, u32[]{:S(2)}, u32[]{:S(2)}) collective-permute-start(bf16[1024,256]{1,0:T(8,128)(2,1)S(1)} %cross_far.5), channel_id=1, source_target_pairs={{0,6},{1,7},{2,0},{3,1},{4,2},{5,3},{6,4},{7,5},{8,14},{9,15},{10,... | collective-permute-start | bytes 1572872 | tf_op jit(solution)/shard_map/ppermute | solution.py:585
  192.8 23.3 %all-to-all-start.1 = ((bf16[16,64,256]{2,1,0:T(8,128)(2,1)}), bf16[16,64,256]{2,1,0:T(8,128)(2,1)S(1)}, u32[]{:S(2)}, u32[]{:S(2)}) async-start(bf16[16,64,256]{2,1,0:T(8,128)(2,1)} %bitcast.18), calls=%async_computation.1 | async-start | bytes 1048576 | tf_op jit(solution)/shard_map/all_to_all | solution.py:589

commit v3 on v2

--- a/solution.py
+++ b/solution.py
@@ -542,8 +542,9 @@
     w, e = sides(geo, geo, "cols")
     partner_geo = jnp.where(col % 2 == 0, e, w)
     geo = jnp.concatenate([w[:, 2:], geo, e[:, :2]], 1)
-    n, s = sides(geo[:2], geo[2:], "rows")
-    geo = jnp.concatenate([n, geo, s], 0)
+    upper, lower = geo[:2], geo[2:]
+    target_spots, upper, lower = lax.optimization_barrier((target_spots, upper, lower))
+    north, south = sides(upper, lower, "rows")
 
     own = values.transpose(1, 0, 2, 3).reshape(4, 256, 512)
     mid = own.astype(BF)
@@ -552,6 +553,7 @@
     everyone, slot = sort_targets(target_tile.reshape(1, 512), target_spots)
     everyone = everyone.reshape(128, 1, 128)
     spots = lax.all_to_all(everyone, ("rows", "cols"), split_axis=0, concat_axis=0, tiled=True)
+    first, w, e, north, south, spots = lax.optimization_barrier((first, w, e, north, south, spots))
     spots = spots.reshape(16, 8, 2, 64).transpose(1, 2, 0, 3).reshape(4, 2, 2, 1024)
     band, half = col // 2, col % 2
     spots = lax.dynamic_index_in_dim(spots, half, 1, keepdims=False)
@@ -567,7 +569,7 @@
     py = partner_geo[:, :, 1] + (jnp.arange(4, dtype=F32) - 4.0 * half.astype(F32))[None, :, None]
     pts2 = jnp.stack([px.reshape(-1), py.reshape(-1)])
 
-    first, w, e = lax.optimization_barrier((first, w, e))
+    geo = jnp.concatenate([north, geo, south], 0)
     mid = jnp.concatenate([w, mid, e], 2)
     n, s = sides(mid[:2], mid[2:], "rows")
     around = [n, mid, s]

time: 220 us -> 209 us (0.950)
  waiting for transfers between devices: 45.2 us -> 32.2 us
  starting transfers between devices: 55.8 us -> 52.1 us
  local copies, waits for them, and re-layouts: 14.5 us -> 17.6 us
    ppermute x4, waiting for transfers between devices: 29.2 us -> 0.01 us  [sides(): lax.ppermute(high, axis, forward)]
    ppermute x3, waiting for transfers between devices: 2.57 us -> 10.5 us  [body(): lax.ppermute(part, 'cols', [(c, (c + 2 * k) % 8) for c in range(8)])]
    all_to_all x1, starting transfers between devices: 12.2 us -> 5.91 us  [body(): lax.all_to_all(predicted.reshape(16, 64, 256), 'rows', split_axis=0, conc...]
    ppermute x1, waiting for transfers between devices: 0.01 us -> 6.14 us  [body(): weights2 = lax.ppermute(weights, 'cols', partner)]
    ppermute x4, starting transfers between devices: 17.6 us -> 21.5 us  [sides(): lax.ppermute(high, axis, forward)]
    all_to_all x1, waiting for transfers between devices: 0.01 us -> 3.47 us  [body(): lax.all_to_all(everyone, ('rows', 'cols'), split_axis=0, concat_axis=0, t...]
  transfers between devices with their start and end apart: 14 -> 14, of which waited for: 5 -> 5; matrix products, arithmetic and copies ran while one was open for 6% -> 7% of each run, Pallas kernels for 34% -> 37%
where the time goes in v3:
time: 209 us; the launch traced here: 208 us
  Pallas kernels  96.5 us (46%)
  starting transfers between devices  52.1 us (25%)
  waiting for transfers between devices  32.2 us (15%)
  local copies, waits for them, and re-layouts  17.6 us (8%)
  other arithmetic  8.38 us (4%)
    pallas_call x1, Pallas kernels, factor(): pl.pallas_call(factor_kernel, out_shape=(jax.ShapeDtypeStruct((16, 128, 2...  51.6 us
    pallas_call x5, Pallas kernels, cross(): pl.pallas_call(kernel, grid=(n,), out_shape=jax.ShapeDtypeStruct((n * TB,...  27.2 us
    ppermute x4, starting transfers between devices, sides(): lax.ppermute(high, axis, forward)  21.5 us
    pallas_call x1, Pallas kernels, whiten(): pl.pallas_call(whiten_kernel, grid=(4,), out_shape=(jax.ShapeDtypeStruct(...  16.7 us
    all_to_all x1, starting transfers between devices, body(): lax.all_to_all(everyone, ('rows', 'cols'), split_axis=0, concat_axis=0, t...  11.8 us
    ppermute x3, waiting for transfers between devices, body(): lax.ppermute(part, 'cols', [(c, (c + 2 * k) % 8) for c in range(8)])  10.5 us
    all_to_all x1, waiting for transfers between devices, body(): lax.all_to_all(predicted.reshape(16, 64, 256), 'rows', split_axis=0, conc...  10.5 us
    reshape x3, local copies, waits for them, and re-layouts, body(): own = values.transpose(1, 0, 2, 3).reshape(4, 256, 512)  6.66 us
  transfers between devices with their start and end apart: 14, of which 5 were waited for; matrix products, arithmetic and copies ran while one was open for 7% of the time, Pallas kernels for 37%

profile of v3, /device:TPU:1, one launch (start us, length us, event | category | flops | bytes accessed | tf_op | source)
XLA Modules:
  0.0 208.5 jit_solution(10811144794905153040)
XLA Ops:
  0.6 0.7 copy.26
  1.4 0.7 pad_maximum_fusion.3
  2.1 1.3 collective-permute-start.3
  3.4 5.0 %collective-permute-start.2 = (f32[4,4,8,128]{3,2,1,0:T(8,128)S(1)}, f32[4,4,8,128]{3,2,1,0:T(8,128)S(1)}, u32[]{:S(2)}, u32[]{:S(2)}) collective-permute-start(f32[4,4,8,128]{3,2,1,0:T(8,128)S(1)} %pad_maximum_fusion.3), channel_id=1, source_target_pairs={{0,1},{1,2},{2,3},{3,4},{4,5},{5,6},{6,7},{8,9},{9,10},{10,11},{11... | collective-permute-start | bytes 196616 | tf_op jit(solution)/shard_map/ppermute | solution.py:530
  8.4 2.5 %reshape.184 = f32[4,256,512]{2,0,1:T(4,128)S(1)} reshape(f32[4,256,4,128]{3,2,0,1:T(4,128)} %bitcast.33) | data formatting | bytes 4194304 | tf_op jit(solution)/shard_map/reshape | solution.py:549
  10.9 1.3 copy-done.4
  12.2 0.6 copy.25
  12.9 1.3 collective-permute-start.1
  14.2 5.7 %collective-permute-start = (bf16[4,256,256]{2,1,0:T(8,128)(2,1)S(1)}, bf16[4,256,256]{2,1,0:T(8,128)(2,1)}, u32[]{:S(2)}, u32[]{:S(2)}) collective-permute-start(bf16[4,256,256]{2,1,0:T(8,128)(2,1)S(1)} %get-tuple-element.40), channel_id=1, source_target_pairs={{0,1},{1,2},{2,3},{3,4},{4,5},{5,6},{6,7},{8,9},{9,10},{10,11},{11... | collective-permute-start | bytes 1572872 | tf_op jit(solution)/shard_map/ppermute | solution.py:530
  19.9 0.5 compare_and_fusion
  20.4 0.6 pad_clamp_fusion.1
  21.0 0.5 add_add_fusion
  21.7 1.0 sort_targets.1
  22.7 11.8 %all-to-all-start = ((f32[128,1,128]{2,1,0:T(1,128)}), f32[128,1,128]{2,1,0:T(1,128)S(1)}, u32[]{:S(2)}, u32[]{:S(2)}) async-start(f32[128,1,128]{2,1,0:T(1,128)} %bitcast.7), calls=%async_computation | async-start | bytes 131072 | tf_op jit(solution)/shard_map/all_to_all | solution.py:555
  34.5 5.4 %collective-permute-start.4 = (f32[2,8,8,128]{3,2,1,0:T(8,128)S(1)}, f32[2,8,8,128]{3,2,1,0:T(8,128)}, u32[]{:S(2)}, u32[]{:S(2)}) collective-permute-start(f32[2,8,8,128]{3,2,1,0:T(8,128)S(1)} %get-tuple-element.19), channel_id=1, source_target_pairs={{0,8},{8,16},{16,24},{24,32},{32,40},{40,48},{48,56},{56,64},{64,7... | collective-permute-start | bytes 196616 | tf_op jit(solution)/shard_map/ppermute | solution.py:530
  39.9 1.9 collective-permute-start.5
  41.9 3.5 %all-to-all-done = f32[128,1,128]{2,1,0:T(1,128)S(1)} async-done(((f32[128,1,128]{2,1,0:T(1,128)}), f32[128,1,128]{2,1,0:T(1,128)S(1)}, u32[]{:S(2)}, u32[]{:S(2)}) %all-to-all-start) | async-done | bytes 65568 | tf_op jit(solution)/shard_map/all_to_all | solution.py:555
  45.4 1.6 collective-permute-done.5
  47.0 0.6 copy-done.6
  47.7 1.5 pad_maximum_fusion.mid
  49.1 1.5 fusion.7
  50.7 1.9 collective-permute-start.7
  52.6 5.3 %collective-permute-start.6 = (bf16[2,256,1024]{2,1,0:T(8,128)(2,1)}, bf16[2,256,1024]{2,1,0:T(8,128)(2,1)}, u32[]{:S(2)}, u32[]{:S(2)}) collective-permute-start(bf16[2,256,1024]{2,1,0:T(8,128)(2,1)} %get-tuple-element.38), channel_id=1, source_target_pairs={{0,8},{8,16},{16,24},{24,32},{32,40},{40,48},{48,56},{56,64},{64,7... | collective-permute-start | bytes 3145736 | tf_op jit(solution)/shard_map/ppermute | solution.py:530
  58.4 3.6 %copy.22.own = f32[4,256,512]{2,1,0:T(8,128)} copy(f32[4,256,512]{2,0,1:T(4,128)} %copy-done.4) | data formatting | bytes 4194304 | tf_op jit(solution)/shard_map/reshape | solution.py:549
  62.9 0.7 add.146
  63.6 0.9 pad_maximum_fusion.1.geo
  64.6 51.6 %factor.1 = (bf16[16,128,256]{2,1,0:T(8,128)(2,1)S(1)}, f32[16,128,128]{2,1,0:T(8,128)S(1)}) custom-call(s32[2]{0:T(128)S(1)} %pad_add_fusion.first, f32[1]{0:T(128)S(6)} %copy.27.length, s32[4,4,256]{2,1,0:T(4,128)S(1)} %copy-done.1, f32[8,8,8,128]{3,2,1,0:T(8,128)S(1)} %pad_maximum_fusion.1.geo), custom_call_target="tpu_custom_call" | custom-call | tf_op jit(solution)/shard_map/factor/pallas_call | solution.py:299
  116.2 1.6 copy-done
  117.7 16.7 %whiten.1 = (f32[16,128,256]{2,1,0:T(8,128)}, bf16[2048,256]{1,0:T(8,128)(2,1)}, f32[4,8,128]{2,1,0:T(8,128)S(1)}) custom-call(s32[2]{0:T(128)S(1)} %pad_add_fusion.first, s32[4,4,256]{2,1,0:T(4,128)S(1)} %copy-done.1, bf16[2,256,1024]{2,1,0:T(8,128)(2,1)} %collective-permute-done.6.north, bf16[4,256,1024]{2,1,0:T(8,128)(2,1)S(1)} %pad_maximum_fusion.mid, ...), custom_call_target="tpu_custom_call" | custom-call | tf_op jit(solution)/shard_map/whiten/pallas_call | solution.py:380
  134.4 0.6 collective-permute-start.8
  135.7 0.8 reduce.5
  136.8 0.7 gather_fusion
  137.7 14.2 %cross_near.1.refs_4_ = f32[4096,256]{1,0:T(8,128)S(1)} custom-call(f32[1]{0:T(128)S(6)} %div.12.s.refs_0_, f32[4,2,1024]{2,1,0:T(2,128)S(1)} %pad_maximum_fusion.4.t, f32[2,2048]{1,0:T(2,128)S(1)} %pad_maximum_fusion.6.p, bf16[2048,256]{1,0:T(8,128)(2,1)} %get-tuple-element.33.w), custom_call_target="tpu_custom_call" | custom-call | tf_op jit(solution)/shard_map/cross_near/pallas_call | solution.py:471
  151.9 6.1 %collective-permute-done.8.refs_3_ = bf16[2048,256]{1,0:T(8,128)(2,1)S(1)} collective-permute-done((bf16[2048,256]{1,0:T(8,128)(2,1)}, bf16[2048,256]{1,0:T(8,128)(2,1)S(1)}, u32[]{:S(2)}, u32[]{:S(2)}) %collective-permute-start.8) | collective-permute-done | bytes 1048608 | tf_op jit(solution)/shard_map/ppermute | solution.py:579
  158.1 3.2 %cross_far.3 = bf16[1024,256]{1,0:T(8,128)(2,1)S(1)} custom-call(f32[1]{0:T(128)S(6)} %div.12.s.refs_0_, f32[1,2,1024]{2,1,0:T(2,128)S(1)} %get-tuple-element.45.refs_1_, f32[2,2048]{1,0:T(2,128)S(1)} %pad_maximum_fusion.5.refs_2_, bf16[2048,256]{1,0:T(8,128)(2,1)S(1)} %collective-permute-done.8.refs_3_, f32[4096,256]{1,0:T(8,128)S(1)} %cross_near.1.refs_4_), custom_call_target="tpu_custom_call" | custom-call | tf_op jit(solution)/shard_map/cross_far/pallas_call | solution.py:471
  161.2 2.9 %collective-permute-start.9 = (bf16[1024,256]{1,0:T(8,128)(2,1)S(1)}, bf16[1024,256]{1,0:T(8,128)(2,1)S(1)}, u32[]{:S(2)}, u32[]{:S(2)}) collective-permute-start(bf16[1024,256]{1,0:T(8,128)(2,1)S(1)} %cross_far.3), channel_id=1, source_target_pairs={{0,4},{1,5},{2,6},{3,7},{4,0},{5,1},{6,2},{7,3},{8,12},{9,13},{10,... | collective-permute-start | bytes 1572872 | tf_op jit(solution)/shard_map/ppermute | solution.py:587
  164.1 3.2 %cross_far.4 = bf16[1024,256]{1,0:T(8,128)(2,1)S(1)} custom-call(f32[1]{0:T(128)S(6)} %div.12.s.refs_0_, f32[1,2,1024]{2,1,0:T(2,128)S(1)} %get-tuple-element.47.refs_1_, f32[2,2048]{1,0:T(2,128)S(1)} %pad_maximum_fusion.5.refs_2_, bf16[2048,256]{1,0:T(8,128)(2,1)S(1)} %collective-permute-done.8.refs_3_, f32[4096,256]{1,0:T(8,128)S(1)} %cross_near.1.refs_4_), custom_call_target="tpu_custom_call" | custom-call | tf_op jit(solution)/shard_map/cross_far/pallas_call | solution.py:471
  167.3 0.7 collective-permute-start.10
  168.0 3.2 %cross_far.5 = bf16[1024,256]{1,0:T(8,128)(2,1)S(1)} custom-call(f32[1]{0:T(128)S(6)} %div.12.s.refs_0_, f32[1,2,1024]{2,1,0:T(2,128)S(1)} %get-tuple-element.48.refs_1_, f32[2,2048]{1,0:T(2,128)S(1)} %pad_maximum_fusion.5.refs_2_, bf16[2048,256]{1,0:T(8,128)(2,1)S(1)} %collective-permute-done.8.refs_3_, f32[4096,256]{1,0:T(8,128)S(1)} %cross_near.1.refs_4_), custom_call_target="tpu_custom_call" | custom-call | tf_op jit(solution)/shard_map/cross_far/pallas_call | solution.py:471
  171.2 2.4 %collective-permute-start.11 = (bf16[1024,256]{1,0:T(8,128)(2,1)S(1)}, bf16[1024,256]{1,0:T(8,128)(2,1)S(1)}, u32[]{:S(2)}, u32[]{:S(2)}) collective-permute-start(bf16[1024,256]{1,0:T(8,128)(2,1)S(1)} %cross_far.5), channel_id=1, source_target_pairs={{0,6},{1,7},{2,0},{3,1},{4,2},{5,3},{6,4},{7,5},{8,14},{9,15},{10,... | collective-permute-start | bytes 1572872 | tf_op jit(solution)/shard_map/ppermute | solution.py:587
  173.6 3.5 %cross_here.1 = f32[1024,256]{1,0:T(8,128)S(1)} custom-call(f32[1]{0:T(128)S(6)} %div.12.s.refs_0_, f32[1,2,1024]{2,1,0:T(2,128)S(1)} %get-tuple-element.46.refs_1_, f32[2,2048]{1,0:T(2,128)S(1)} %pad_maximum_fusion.5.refs_2_, bf16[2048,256]{1,0:T(8,128)(2,1)S(1)} %collective-permute-done.8.refs_3_, f32[4096,256]{1,0:T(8,128)S(1)} %cross_near.1.refs_4_), custom_call_target="tpu_custom_call" | custom-call | tf_op jit(solution)/shard_map/cross_here/pallas_call | solution.py:471
  177.1 10.5 %collective-permute-done.10 = bf16[1024,256]{1,0:T(8,128)(2,1)S(1)} collective-permute-done((bf16[1024,256]{1,0:T(8,128)(2,1)S(1)}, bf16[1024,256]{1,0:T(8,128)(2,1)S(1)}, u32[]{:S(2)}, u32[]{:S(2)}) %collective-permute-start.10) | collective-permute-done | bytes 524320 | tf_op jit(solution)/shard_map/ppermute | solution.py:587
  187.6 1.1 multiply_convert_fusion
  188.7 5.9 %all-to-all-start.1 = ((bf16[16,64,256]{2,1,0:T(8,128)(2,1)}), bf16[16,64,256]{2,1,0:T(8,128)(2,1)S(1)}, u32[]{:S(2)}, u32[]{:S(2)}) async-start(bf16[16,64,256]{2,1,0:T(8,128)(2,1)} %bitcast.18), calls=%async_computation.1 | async-start | bytes 1048576 | tf_op jit(solution)/shard_map/all_to_all | solution.py:591
  194.6 0.7 slice_reduce_fusion
  195.3 10.5 %all-to-all-done.1 = bf16[16,64,256]{2,1,0:T(8,128)(2,1)S(1)} async-done(((bf16[16,64,256]{2,1,0:T(8,128)(2,1)}), bf16[16,64,256]{2,1,0:T(8,128)(2,1)S(1)}, u32[]{:S(2)}, u32[]{:S(2)}) %all-to-all-start.1) | async-done | bytes 524320 | tf_op jit(solution)/shard_map/all_to_all | solution.py:591
  205.7 1.9 gather_fusion.1
  207.7 0.8 convert_element_type.32
  (59 shorter events, 2.0 us)
Async XLA Ops:
  2.1 19.5 %collective-permute-start.3 = (f32[4,4,8,128]{3,2,1,0:T(8,128)S(1)}, f32[4,4,8,128]{3,2,1,0:T(8,128)S(1)}, u32[]{:S(2)}, u32[]{:S(2)}) collective-permute-start(f32[4,4,8,128]{3,2,1,0:T(8,128)S(1)} %pad_maximum_fusion.3), channel_id=1, source_target_pairs={{1,0},{2,1},{3,2},{4,3},{5,4},{6,5},{7,6},{9,8},{10,9},{11,10},{12... | collective-permute-start | bytes 196616 | tf_op jit(solution)/shard_map/ppermute | solution.py:530
  3.4 18.2 %collective-permute-start.2 = (f32[4,4,8,128]{3,2,1,0:T(8,128)S(1)}, f32[4,4,8,128]{3,2,1,0:T(8,128)S(1)}, u32[]{:S(2)}, u32[]{:S(2)}) collective-permute-start(f32[4,4,8,128]{3,2,1,0:T(8,128)S(1)} %pad_maximum_fusion.3), channel_id=1, source_target_pairs={{0,1},{1,2},{2,3},{3,4},{4,5},{5,6},{6,7},{8,9},{9,10},{10,11},{11... | collective-permute-start | bytes 196616 | tf_op jit(solution)/shard_map/ppermute | solution.py:530
  10.9 1.3 copy-start.4
  12.2 7.7 %copy-start.7 = (f32[2,4,4,128]{3,2,1,0:T(4,128)S(1)}, f32[2,4,4,128]{3,2,1,0:T(4,128)}, u32[]{:S(2)}) copy-start(f32[2,4,4,128]{3,2,1,0:T(4,128)} %param.9) | copy-start | bytes 49156
  12.2 7.7 %copy-start.11 = (s32[4]{0:T(128)S(1)}, s32[4]{0:T(128)}, u32[]{:S(2)}) copy-start(s32[4]{0:T(128)} %constant.94.clone) | copy-start | bytes 52
  12.2 9.4 %copy-start.5 = (f32[4,4,128]{2,1,0:T(4,128)S(1)}, f32[4,4,128]{2,1,0:T(4,128)}, u32[]{:S(2)}) copy-start(f32[4,4,128]{2,1,0:T(4,128)} %param.10) | copy-start | bytes 24580
  12.8 8.9 %copy-start.2 = (f32[2,512]{1,0:T(2,128)S(1)}, f32[2,512]{1,0:T(2,128)}, u32[]{:S(2)}) copy-start(f32[2,512]{1,0:T(2,128)} %spots) | copy-start | bytes 12292
  12.8 8.9 %copy-start.3 = (s32[512,1]{0,1:T(1,128)S(1)}, s32[512,1]{0,1:T(1,128)}, u32[]{:S(2)}) copy-start(s32[512,1]{0,1:T(1,128)} %param.13) | copy-start | bytes 6148
  12.9 34.1 %collective-permute-start.1 = (bf16[4,256,256]{2,1,0:T(8,128)(2,1)S(1)}, bf16[4,256,256]{2,1,0:T(8,128)(2,1)}, u32[]{:S(2)}, u32[]{:S(2)}) collective-permute-start(bf16[4,256,256]{2,1,0:T(8,128)(2,1)S(1)} %get-tuple-element.39), channel_id=1, source_target_pairs={{1,0},{2,1},{3,2},{4,3},{5,4},{6,5},{7,6},{9,8},{10,9},{11,10},{12... | collective-permute-start | bytes 1572872 | tf_op jit(solution)/shard_map/ppermute | solution.py:530
  14.2 33.5 %collective-permute-start = (bf16[4,256,256]{2,1,0:T(8,128)(2,1)S(1)}, bf16[4,256,256]{2,1,0:T(8,128)(2,1)}, u32[]{:S(2)}, u32[]{:S(2)}) collective-permute-start(bf16[4,256,256]{2,1,0:T(8,128)(2,1)S(1)} %get-tuple-element.40), channel_id=1, source_target_pairs={{0,1},{1,2},{2,3},{3,4},{4,5},{5,6},{6,7},{8,9},{9,10},{10,11},{11... | collective-permute-start | bytes 1572872 | tf_op jit(solution)/shard_map/ppermute | solution.py:530
  22.7 22.7 %all-to-all-start = ((f32[128,1,128]{2,1,0:T(1,128)}), f32[128,1,128]{2,1,0:T(1,128)S(1)}, u32[]{:S(2)}, u32[]{:S(2)}) async-start(f32[128,1,128]{2,1,0:T(1,128)} %bitcast.7), calls=%async_computation | async-start | bytes 131072 | tf_op jit(solution)/shard_map/all_to_all | solution.py:555
  34.5 10.9 %collective-permute-start.4 = (f32[2,8,8,128]{3,2,1,0:T(8,128)S(1)}, f32[2,8,8,128]{3,2,1,0:T(8,128)}, u32[]{:S(2)}, u32[]{:S(2)}) collective-permute-start(f32[2,8,8,128]{3,2,1,0:T(8,128)S(1)} %get-tuple-element.19), channel_id=1, source_target_pairs={{0,8},{8,16},{16,24},{24,32},{32,40},{40,48},{48,56},{56,64},{64,7... | collective-permute-start | bytes 196616 | tf_op jit(solution)/shard_map/ppermute | solution.py:530
  39.9 7.1 %collective-permute-start.5 = (f32[2,8,8,128]{3,2,1,0:T(8,128)S(1)}, f32[2,8,8,128]{3,2,1,0:T(8,128)S(1)}, u32[]{:S(2)}, u32[]{:S(2)}) collective-permute-start(f32[2,8,8,128]{3,2,1,0:T(8,128)S(1)} %get-tuple-element.20), channel_id=1, source_target_pairs={{8,0},{16,8},{24,16},{32,24},{40,32},{48,40},{56,48},{64,56},{72,6... | collective-permute-start | bytes 196616 | tf_op jit(solution)/shard_map/ppermute | solution.py:530
  47.0 0.6 copy-start.6
  50.7 65.5 %collective-permute-start.7 = (bf16[2,256,1024]{2,1,0:T(8,128)(2,1)}, bf16[2,256,1024]{2,1,0:T(8,128)(2,1)S(1)}, u32[]{:S(2)}, u32[]{:S(2)}) collective-permute-start(bf16[2,256,1024]{2,1,0:T(8,128)(2,1)} %get-tuple-element.37), channel_id=1, source_target_pairs={{8,0},{16,8},{24,16},{32,24},{40,32},{48,40},{56,48},{64,56},{72,6... | collective-permute-start | bytes 3145736 | tf_op jit(solution)/shard_map/ppermute | solution.py:530
  52.6 63.6 %collective-permute-start.6 = (bf16[2,256,1024]{2,1,0:T(8,128)(2,1)}, bf16[2,256,1024]{2,1,0:T(8,128)(2,1)}, u32[]{:S(2)}, u32[]{:S(2)}) collective-permute-start(bf16[2,256,1024]{2,1,0:T(8,128)(2,1)} %get-tuple-element.38), channel_id=1, source_target_pairs={{0,8},{8,16},{16,24},{24,32},{32,40},{40,48},{48,56},{56,64},{64,7... | collective-permute-start | bytes 3145736 | tf_op jit(solution)/shard_map/ppermute | solution.py:530
  58.4 4.3 %copy-start.10 = (f32[4]{0:T(128)S(1)}, f32[4]{0:T(128)}, u32[]{:S(2)}) copy-start(f32[4]{0:T(128)} %get-tuple-element.55) | copy-start | bytes 52
  58.4 6.1 %copy-start.1 = (s32[4,4,256]{2,1,0:T(4,128)S(1)}, s32[4,4,256]{2,1,0:T(4,128)}, u32[]{:S(2)}) copy-start(s32[4,4,256]{2,1,0:T(4,128)} %nb.3) | copy-start | bytes 49156
  116.2 1.6 copy-start
  117.7 17.3 %copy-start.9 = (f32[4]{0:T(128)S(1)}, f32[4]{0:T(128)}, u32[]{:S(2)}) copy-start(f32[4]{0:T(128)} %get-tuple-element.56) | copy-start | bytes 52
  117.7 19.8 %copy-start.8 = (pred[4]{0:T(512)(128)(4,1)S(1)}, pred[4]{0:T(512)(128)(4,1)}, u32[]{:S(2)}) copy-start(pred[4]{0:T(512)(128)(4,1)} %get-tuple-element.35) | copy-start | bytes 16
  134.4 23.6 %collective-permute-start.8 = (bf16[2048,256]{1,0:T(8,128)(2,1)}, bf16[2048,256]{1,0:T(8,128)(2,1)S(1)}, u32[]{:S(2)}, u32[]{:S(2)}) collective-permute-start(bf16[2048,256]{1,0:T(8,128)(2,1)} %get-tuple-element.33.w), channel_id=1, source_target_pairs={{0,1},{1,0},{2,3},{3,2},{4,5},{5,4},{6,7},{7,6},{8,9},{9,8},{10,11... | collective-permute-start | bytes 3145736 | tf_op jit(solution)/shard_map/ppermute | solution.py:579
  161.2 15.9 %collective-permute-start.9 = (bf16[1024,256]{1,0:T(8,128)(2,1)S(1)}, bf16[1024,256]{1,0:T(8,128)(2,1)S(1)}, u32[]{:S(2)}, u32[]{:S(2)}) collective-permute-start(bf16[1024,256]{1,0:T(8,128)(2,1)S(1)} %cross_far.3), channel_id=1, source_target_pairs={{0,4},{1,5},{2,6},{3,7},{4,0},{5,1},{6,2},{7,3},{8,12},{9,13},{10,... | collective-permute-start | bytes 1572872 | tf_op jit(solution)/shard_map/ppermute | solution.py:587
  167.3 20.3 %collective-permute-start.10 = (bf16[1024,256]{1,0:T(8,128)(2,1)S(1)}, bf16[1024,256]{1,0:T(8,128)(2,1)S(1)}, u32[]{:S(2)}, u32[]{:S(2)}) collective-permute-start(bf16[1024,256]{1,0:T(8,128)(2,1)S(1)} %cross_far.4), channel_id=1, source_target_pairs={{0,2},{1,3},{2,4},{3,5},{4,6},{5,7},{6,0},{7,1},{8,10},{9,11},{10,... | collective-permute-start | bytes 1572872 | tf_op jit(solution)/shard_map/ppermute | solution.py:587
  171.2 16.4 %collective-permute-start.11 = (bf16[1024,256]{1,0:T(8,128)(2,1)S(1)}, bf16[1024,256]{1,0:T(8,128)(2,1)S(1)}, u32[]{:S(2)}, u32[]{:S(2)}) collective-permute-start(bf16[1024,256]{1,0:T(8,128)(2,1)S(1)} %cross_far.5), channel_id=1, source_target_pairs={{0,6},{1,7},{2,0},{3,1},{4,2},{5,3},{6,4},{7,5},{8,14},{9,15},{10,... | collective-permute-start | bytes 1572872 | tf_op jit(solution)/shard_map/ppermute | solution.py:587
  188.7 17.1 %all-to-all-start.1 = ((bf16[16,64,256]{2,1,0:T(8,128)(2,1)}), bf16[16,64,256]{2,1,0:T(8,128)(2,1)S(1)}, u32[]{:S(2)}, u32[]{:S(2)}) async-start(bf16[16,64,256]{2,1,0:T(8,128)(2,1)} %bitcast.18), calls=%async_computation.1 | async-start | bytes 1048576 | tf_op jit(solution)/shard_map/all_to_all | solution.py:591

commit v4 on v3

--- a/solution.py
+++ b/solution.py
@@ -317,13 +317,14 @@
     )(first, length, nb, geo)
 
 
-def whiten_kernel(first, nb, north, mid, south, g, w3, own, white, weights, term, tab, acc, lhs):
+def whiten_kernel(first, nb, north, upper, lower, south, g, w3, own, white, weights, term, tab, acc, lhs):
     ci = pl.program_id(0)
 
     @pl.when(ci == 0)
     def _():
         tab[0:2] = north[...]
-        tab[2:6] = mid[...]
+        tab[2:4] = upper[...]
+        tab[4:6] = lower[...]
         tab[6:8] = south[...]
         for wi in range(5):
             for cj, q in ((0, 5), (1, 0), (2, 7), (3, 2)):
@@ -553,7 +554,9 @@
     everyone, slot = sort_targets(target_tile.reshape(1, 512), target_spots)
     everyone = everyone.reshape(128, 1, 128)
     spots = lax.all_to_all(everyone, ("rows", "cols"), split_axis=0, concat_axis=0, tiled=True)
-    first, w, e, north, south, spots = lax.optimization_barrier((first, w, e, north, south, spots))
+    first, w, e, north, south, spots, own = lax.optimization_barrier(
+        (first, w, e, north, south, spots, own)
+    )
     spots = spots.reshape(16, 8, 2, 64).transpose(1, 2, 0, 3).reshape(4, 2, 2, 1024)
     band, half = col // 2, col % 2
     spots = lax.dynamic_index_in_dim(spots, half, 1, keepdims=False)
@@ -570,9 +573,10 @@
     pts2 = jnp.stack([px.reshape(-1), py.reshape(-1)])
 
     geo = jnp.concatenate([north, geo, south], 0)
-    mid = jnp.concatenate([w, mid, e], 2)
-    n, s = sides(mid[:2], mid[2:], "rows")
-    around = [n, mid, s]
+    upper = jnp.concatenate([w[:2], mid[:2], e[:2]], 2)
+    lower = jnp.concatenate([w[2:], mid[2:], e[2:]], 2)
+    n, s = sides(upper, lower, "rows")
+    around = [n, upper, lower, s]
     g, w3 = factor(first, length_scale, neighbours, geo)
     white, weights, term = whiten(first, neighbours, around, g, w3, own)
     scale = jnp.stack([math.sqrt(3.0) / LN2 / length])

time: 209 us -> 203 us (0.971)
  starting transfers between devices: 52.1 us -> 48.7 us
  local copies, waits for them, and re-layouts: 17.6 us -> 14.4 us
    unnamed x25 -> x23, local copies, waits for them, and re-layouts: 4.29 us -> 0.79 us
    ppermute x4, starting transfers between devices: 21.5 us -> 18.1 us  [sides(): lax.ppermute(high, axis, forward)]
  transfers between devices with their start and end apart: 14 -> 14, of which waited for: 5 -> 5; matrix products, arithmetic and copies ran while one was open for 7% -> 7% of each run, Pallas kernels for 37% -> 38%
where the time goes in v4:
time: 203 us
  Pallas kernels  97.2 us (48%)
  starting transfers between devices  48.7 us (24%)
  waiting for transfers between devices  34.1 us (17%)
  local copies, waits for them, and re-layouts  14.4 us (7%)
  other arithmetic  6.51 us (3%)
    pallas_call x1, Pallas kernels, factor(): pl.pallas_call(factor_kernel, out_shape=(jax.ShapeDtypeStruct((16, 128, 2...  51.6 us
    pallas_call x5, Pallas kernels, cross(): pl.pallas_call(kernel, grid=(n,), out_shape=jax.ShapeDtypeStruct((n * TB,...  27.2 us
    ppermute x4, starting transfers between devices, sides(): lax.ppermute(high, axis, forward)  18.1 us
    pallas_call x1, Pallas kernels, whiten(): pl.pallas_call(whiten_kernel, grid=(4,), out_shape=(jax.ShapeDtypeStruct(...  17.4 us
    all_to_all x1, starting transfers between devices, body(): lax.all_to_all(everyone, ('rows', 'cols'), split_axis=0, concat_axis=0, t...  11.7 us
    ppermute x3, waiting for transfers between devices, body(): lax.ppermute(part, 'cols', [(c, (c + 2 * k) % 8) for c in range(8)])  10.8 us
    all_to_all x1, waiting for transfers between devices, body(): lax.all_to_all(predicted.reshape(16, 64, 256), 'rows', split_axis=0, conc...  10.5 us
    ppermute x4, starting transfers between devices, sides(): lax.ppermute(low, axis, backward)  8.04 us
  transfers between devices with their start and end apart: 14, of which 5 were waited for; matrix products, arithmetic and copies ran while one was open for 7% of the time, Pallas kernels for 38%

profile of v4, /device:TPU:1, one launch (start us, length us, event | category | flops | bytes accessed | tf_op | source)
XLA Modules:
  0.0 202.7 jit_solution(3262799943709176812)
XLA Ops:
  0.6 0.7 copy.26
  1.4 0.7 pad_maximum_fusion.4
  2.1 1.3 collective-permute-start.3
  3.4 5.0 %collective-permute-start.2 = (f32[4,4,8,128]{3,2,1,0:T(8,128)S(1)}, f32[4,4,8,128]{3,2,1,0:T(8,128)S(1)}, u32[]{:S(2)}, u32[]{:S(2)}) collective-permute-start(f32[4,4,8,128]{3,2,1,0:T(8,128)S(1)} %pad_maximum_fusion.4), channel_id=1, source_target_pairs={{0,1},{1,2},{2,3},{3,4},{4,5},{5,6},{6,7},{8,9},{9,10},{10,11},{11... | collective-permute-start | bytes 196616 | tf_op jit(solution)/shard_map/ppermute | solution.py:531
  8.4 2.5 %reshape.184 = f32[4,256,512]{2,0,1:T(4,128)S(1)} reshape(f32[4,256,4,128]{3,2,0,1:T(4,128)} %bitcast.33) | data formatting | bytes 4194304 | tf_op jit(solution)/shard_map/reshape | solution.py:550
  10.9 0.6 copy.25
  11.5 1.0 fusion.8
  12.5 1.3 collective-permute-start.1
  13.8 5.7 %collective-permute-start = (bf16[4,256,256]{2,1,0:T(8,128)(2,1)}, bf16[4,256,256]{2,1,0:T(8,128)(2,1)}, u32[]{:S(2)}, u32[]{:S(2)}) collective-permute-start(bf16[4,256,256]{2,1,0:T(8,128)(2,1)} %get-tuple-element.42), channel_id=1, source_target_pairs={{0,1},{1,2},{2,3},{3,4},{4,5},{5,6},{6,7},{8,9},{9,10},{10,11},{11... | collective-permute-start | bytes 1572872 | tf_op jit(solution)/shard_map/ppermute | solution.py:531
  19.5 2.3 %copy.22.own = f32[4,256,512]{2,1,0:T(8,128)S(1)} copy(f32[4,256,512]{2,0,1:T(4,128)} %copy-done.3) | data formatting | bytes 4194304 | tf_op jit(solution)/shard_map/reshape | solution.py:550
  21.8 1.0 fusion.7
  23.1 1.0 sort_targets.1
  24.1 11.7 %all-to-all-start = ((f32[128,1,128]{2,1,0:T(1,128)}), f32[128,1,128]{2,1,0:T(1,128)S(1)}, u32[]{:S(2)}, u32[]{:S(2)}) async-start(f32[128,1,128]{2,1,0:T(1,128)} %bitcast.7), calls=%async_computation | async-start | bytes 131072 | tf_op jit(solution)/shard_map/all_to_all | solution.py:556
  35.8 5.4 %collective-permute-start.4 = (f32[2,8,8,128]{3,2,1,0:T(8,128)S(1)}, f32[2,8,8,128]{3,2,1,0:T(8,128)S(1)}, u32[]{:S(2)}, u32[]{:S(2)}) collective-permute-start(f32[2,8,8,128]{3,2,1,0:T(8,128)S(1)} %get-tuple-element.20), channel_id=1, source_target_pairs={{0,8},{8,16},{16,24},{24,32},{32,40},{40,48},{48,56},{56,64},{64,7... | collective-permute-start | bytes 196616 | tf_op jit(solution)/shard_map/ppermute | solution.py:531
  41.3 1.9 collective-permute-start.5
  43.3 2.3 %all-to-all-done = f32[128,1,128]{2,1,0:T(1,128)S(1)} async-done(((f32[128,1,128]{2,1,0:T(1,128)}), f32[128,1,128]{2,1,0:T(1,128)S(1)}, u32[]{:S(2)}, u32[]{:S(2)}) %all-to-all-start) | async-done | bytes 65568 | tf_op jit(solution)/shard_map/all_to_all | solution.py:556
  45.5 2.8 %collective-permute-done.5 = f32[2,8,8,128]{3,2,1,0:T(8,128)S(1)} collective-permute-done((f32[2,8,8,128]{3,2,1,0:T(8,128)S(1)}, f32[2,8,8,128]{3,2,1,0:T(8,128)S(1)}, u32[]{:S(2)}, u32[]{:S(2)}) %collective-permute-start.5) | collective-permute-done | bytes 65568 | tf_op jit(solution)/shard_map/ppermute | solution.py:531
  48.4 1.3 fusion.9
  49.7 0.1 pad_maximum_fusion.lower
  49.8 1.9 collective-permute-start.6
  51.8 1.1 pad_maximum_fusion.1.upper
  52.9 3.5 %collective-permute-start.7 = (bf16[2,256,1024]{2,1,0:T(8,128)(2,1)}, bf16[2,256,1024]{2,1,0:T(8,128)(2,1)}, u32[]{:S(2)}, u32[]{:S(2)}) collective-permute-start(bf16[2,256,1024]{2,1,0:T(8,128)(2,1)} %pad_maximum_fusion.1.upper), channel_id=1, source_target_pairs={{8,0},{16,8},{24,16},{32,24},{40,32},{48,40},{56,48},{64,56},{72,6... | collective-permute-start | bytes 3145736 | tf_op jit(solution)/shard_map/ppermute | solution.py:531
  56.4 0.5 iota_add_fusion
  57.8 0.7 add.146
  58.5 0.9 pad_maximum_fusion.2.geo
  59.4 51.6 %factor.1 = (bf16[16,128,256]{2,1,0:T(8,128)(2,1)S(1)}, f32[16,128,128]{2,1,0:T(8,128)S(1)}) custom-call(s32[2]{0:T(128)S(1)} %pad_add_fusion.first, f32[1]{0:T(128)S(6)} %copy.27.length, s32[4,4,256]{2,1,0:T(4,128)S(1)} %copy-done, f32[8,8,8,128]{3,2,1,0:T(8,128)S(1)} %pad_maximum_fusion.2.geo), custom_call_target="tpu_custom_call" | custom-call | tf_op jit(solution)/shard_map/factor/pallas_call | solution.py:299
  111.0 17.4 %whiten.1 = (f32[16,128,256]{2,1,0:T(8,128)}, bf16[2048,256]{1,0:T(8,128)(2,1)}, f32[4,8,128]{2,1,0:T(8,128)S(1)}) custom-call(s32[2]{0:T(128)S(1)} %pad_add_fusion.first, s32[4,4,256]{2,1,0:T(4,128)S(1)} %copy-done, bf16[2,256,1024]{2,1,0:T(8,128)(2,1)} %collective-permute-done.6.north, bf16[2,256,1024]{2,1,0:T(8,128)(2,1)} %pad_maximum_fusion.1.upper, ...), custom_call_target="tpu_custom_call" | custom-call | tf_op jit(solution)/shard_map/whiten/pallas_call | solution.py:381
  128.4 0.6 collective-permute-start.8
  129.1 0.5 broadcast.93
  129.6 0.8 reduce.5
  130.4 0.1 reshape.162
  130.8 0.6 gather_fusion
  131.6 14.2 %cross_near.1.refs_4_ = f32[4096,256]{1,0:T(8,128)S(1)} custom-call(f32[1]{0:T(128)S(6)} %div.12.s.refs_0_, f32[4,2,1024]{2,1,0:T(2,128)S(1)} %pad_maximum_fusion.5.t, f32[2,2048]{1,0:T(2,128)S(1)} %pad_maximum_fusion.7.p, bf16[2048,256]{1,0:T(8,128)(2,1)} %get-tuple-element.35.w), custom_call_target="tpu_custom_call" | custom-call | tf_op jit(solution)/shard_map/cross_near/pallas_call | solution.py:472
  145.8 7.7 %collective-permute-done.8.refs_3_ = bf16[2048,256]{1,0:T(8,128)(2,1)S(1)} collective-permute-done((bf16[2048,256]{1,0:T(8,128)(2,1)}, bf16[2048,256]{1,0:T(8,128)(2,1)S(1)}, u32[]{:S(2)}, u32[]{:S(2)}) %collective-permute-start.8) | collective-permute-done | bytes 1048608 | tf_op jit(solution)/shard_map/ppermute | solution.py:583
  153.5 3.2 %cross_far.3 = bf16[1024,256]{1,0:T(8,128)(2,1)S(1)} custom-call(f32[1]{0:T(128)S(6)} %div.12.s.refs_0_, f32[1,2,1024]{2,1,0:T(2,128)S(1)} %get-tuple-element.51.refs_1_, f32[2,2048]{1,0:T(2,128)S(1)} %pad_maximum_fusion.6.refs_2_, bf16[2048,256]{1,0:T(8,128)(2,1)S(1)} %collective-permute-done.8.refs_3_, f32[4096,256]{1,0:T(8,128)S(1)} %cross_near.1.refs_4_), custom_call_target="tpu_custom_call" | custom-call | tf_op jit(solution)/shard_map/cross_far/pallas_call | solution.py:472
  156.7 2.9 %collective-permute-start.9 = (bf16[1024,256]{1,0:T(8,128)(2,1)S(1)}, bf16[1024,256]{1,0:T(8,128)(2,1)S(1)}, u32[]{:S(2)}, u32[]{:S(2)}) collective-permute-start(bf16[1024,256]{1,0:T(8,128)(2,1)S(1)} %cross_far.3), channel_id=1, source_target_pairs={{0,4},{1,5},{2,6},{3,7},{4,0},{5,1},{6,2},{7,3},{8,12},{9,13},{10,... | collective-permute-start | bytes 1572872 | tf_op jit(solution)/shard_map/ppermute | solution.py:591
  159.6 3.2 %cross_far.4 = bf16[1024,256]{1,0:T(8,128)(2,1)S(1)} custom-call(f32[1]{0:T(128)S(6)} %div.12.s.refs_0_, f32[1,2,1024]{2,1,0:T(2,128)S(1)} %get-tuple-element.53.refs_1_, f32[2,2048]{1,0:T(2,128)S(1)} %pad_maximum_fusion.6.refs_2_, bf16[2048,256]{1,0:T(8,128)(2,1)S(1)} %collective-permute-done.8.refs_3_, f32[4096,256]{1,0:T(8,128)S(1)} %cross_near.1.refs_4_), custom_call_target="tpu_custom_call" | custom-call | tf_op jit(solution)/shard_map/cross_far/pallas_call | solution.py:472
  162.7 0.7 collective-permute-start.10
  163.4 3.2 %cross_far.5 = bf16[1024,256]{1,0:T(8,128)(2,1)S(1)} custom-call(f32[1]{0:T(128)S(6)} %div.12.s.refs_0_, f32[1,2,1024]{2,1,0:T(2,128)S(1)} %get-tuple-element.54.refs_1_, f32[2,2048]{1,0:T(2,128)S(1)} %pad_maximum_fusion.6.refs_2_, bf16[2048,256]{1,0:T(8,128)(2,1)S(1)} %collective-permute-done.8.refs_3_, f32[4096,256]{1,0:T(8,128)S(1)} %cross_near.1.refs_4_), custom_call_target="tpu_custom_call" | custom-call | tf_op jit(solution)/shard_map/cross_far/pallas_call | solution.py:472
  166.6 2.4 %collective-permute-start.11 = (bf16[1024,256]{1,0:T(8,128)(2,1)S(1)}, bf16[1024,256]{1,0:T(8,128)(2,1)S(1)}, u32[]{:S(2)}, u32[]{:S(2)}) collective-permute-start(bf16[1024,256]{1,0:T(8,128)(2,1)S(1)} %cross_far.5), channel_id=1, source_target_pairs={{0,6},{1,7},{2,0},{3,1},{4,2},{5,3},{6,4},{7,5},{8,14},{9,15},{10,... | collective-permute-start | bytes 1572872 | tf_op jit(solution)/shard_map/ppermute | solution.py:591
  169.0 3.5 %cross_here.1 = f32[1024,256]{1,0:T(8,128)S(1)} custom-call(f32[1]{0:T(128)S(6)} %div.12.s.refs_0_, f32[1,2,1024]{2,1,0:T(2,128)S(1)} %get-tuple-element.52.refs_1_, f32[2,2048]{1,0:T(2,128)S(1)} %pad_maximum_fusion.6.refs_2_, bf16[2048,256]{1,0:T(8,128)(2,1)S(1)} %collective-permute-done.8.refs_3_, f32[4096,256]{1,0:T(8,128)S(1)} %cross_near.1.refs_4_), custom_call_target="tpu_custom_call" | custom-call | tf_op jit(solution)/shard_map/cross_here/pallas_call | solution.py:472
  172.5 10.8 %collective-permute-done.10 = bf16[1024,256]{1,0:T(8,128)(2,1)S(1)} collective-permute-done((bf16[1024,256]{1,0:T(8,128)(2,1)S(1)}, bf16[1024,256]{1,0:T(8,128)(2,1)S(1)}, u32[]{:S(2)}, u32[]{:S(2)}) %collective-permute-start.10) | collective-permute-done | bytes 524320 | tf_op jit(solution)/shard_map/ppermute | solution.py:591
  183.3 1.1 multiply_convert_fusion
  184.4 4.4 %all-to-all-start.1 = ((bf16[16,64,256]{2,1,0:T(8,128)(2,1)}), bf16[16,64,256]{2,1,0:T(8,128)(2,1)S(1)}, u32[]{:S(2)}, u32[]{:S(2)}) async-start(bf16[16,64,256]{2,1,0:T(8,128)(2,1)} %bitcast.18), calls=%async_computation.1 | async-start | bytes 1048576 | tf_op jit(solution)/shard_map/all_to_all | solution.py:595
  188.8 0.7 slice_reduce_fusion
  189.4 10.5 %all-to-all-done.1 = bf16[16,64,256]{2,1,0:T(8,128)(2,1)S(1)} async-done(((bf16[16,64,256]{2,1,0:T(8,128)(2,1)}), bf16[16,64,256]{2,1,0:T(8,128)(2,1)S(1)}, u32[]{:S(2)}, u32[]{:S(2)}) %all-to-all-start.1) | async-done | bytes 524320 | tf_op jit(solution)/shard_map/all_to_all | solution.py:595
  199.9 1.9 gather_fusion.1
  201.8 0.8 convert_element_type.32
  (59 shorter events, 0.9 us)
Async XLA Ops:
  2.1 20.8 %collective-permute-start.3 = (f32[4,4,8,128]{3,2,1,0:T(8,128)S(1)}, f32[4,4,8,128]{3,2,1,0:T(8,128)S(1)}, u32[]{:S(2)}, u32[]{:S(2)}) collective-permute-start(f32[4,4,8,128]{3,2,1,0:T(8,128)S(1)} %pad_maximum_fusion.4), channel_id=1, source_target_pairs={{1,0},{2,1},{3,2},{4,3},{5,4},{6,5},{7,6},{9,8},{10,9},{11,10},{12... | collective-permute-start | bytes 196616 | tf_op jit(solution)/shard_map/ppermute | solution.py:531
  3.4 19.6 %collective-permute-start.2 = (f32[4,4,8,128]{3,2,1,0:T(8,128)S(1)}, f32[4,4,8,128]{3,2,1,0:T(8,128)S(1)}, u32[]{:S(2)}, u32[]{:S(2)}) collective-permute-start(f32[4,4,8,128]{3,2,1,0:T(8,128)S(1)} %pad_maximum_fusion.4), channel_id=1, source_target_pairs={{0,1},{1,2},{2,3},{3,4},{4,5},{5,6},{6,7},{8,9},{9,10},{10,11},{11... | collective-permute-start | bytes 196616 | tf_op jit(solution)/shard_map/ppermute | solution.py:531
  10.9 1.7 copy-start.3
  10.9 8.6 %copy-start.9 = (f32[2,4,4,128]{3,2,1,0:T(4,128)S(1)}, f32[2,4,4,128]{3,2,1,0:T(4,128)}, u32[]{:S(2)}) copy-start(f32[2,4,4,128]{3,2,1,0:T(4,128)} %param.9) | copy-start | bytes 49156
  12.5 35.8 %collective-permute-start.1 = (bf16[4,256,256]{2,1,0:T(8,128)(2,1)}, bf16[4,256,256]{2,1,0:T(8,128)(2,1)}, u32[]{:S(2)}, u32[]{:S(2)}) collective-permute-start(bf16[4,256,256]{2,1,0:T(8,128)(2,1)} %get-tuple-element.41), channel_id=1, source_target_pairs={{1,0},{2,1},{3,2},{4,3},{5,4},{6,5},{7,6},{9,8},{10,9},{11,10},{12... | collective-permute-start | bytes 1572872 | tf_op jit(solution)/shard_map/ppermute | solution.py:531
  13.8 34.5 %collective-permute-start = (bf16[4,256,256]{2,1,0:T(8,128)(2,1)}, bf16[4,256,256]{2,1,0:T(8,128)(2,1)}, u32[]{:S(2)}, u32[]{:S(2)}) collective-permute-start(bf16[4,256,256]{2,1,0:T(8,128)(2,1)} %get-tuple-element.42), channel_id=1, source_target_pairs={{0,1},{1,2},{2,3},{3,4},{4,5},{5,6},{6,7},{8,9},{9,10},{10,11},{11... | collective-permute-start | bytes 1572872 | tf_op jit(solution)/shard_map/ppermute | solution.py:531
  21.8 1.1 copy-start.10
  21.8 1.2 copy-start.6
  21.8 1.2 copy-start.1
  21.8 1.2 copy-start.2
  24.1 21.4 %all-to-all-start = ((f32[128,1,128]{2,1,0:T(1,128)}), f32[128,1,128]{2,1,0:T(1,128)S(1)}, u32[]{:S(2)}, u32[]{:S(2)}) async-start(f32[128,1,128]{2,1,0:T(1,128)} %bitcast.7), calls=%async_computation | async-start | bytes 131072 | tf_op jit(solution)/shard_map/all_to_all | solution.py:556
  35.8 9.7 %collective-permute-start.4 = (f32[2,8,8,128]{3,2,1,0:T(8,128)S(1)}, f32[2,8,8,128]{3,2,1,0:T(8,128)S(1)}, u32[]{:S(2)}, u32[]{:S(2)}) collective-permute-start(f32[2,8,8,128]{3,2,1,0:T(8,128)S(1)} %get-tuple-element.20), channel_id=1, source_target_pairs={{0,8},{8,16},{16,24},{24,32},{32,40},{40,48},{48,56},{56,64},{64,7... | collective-permute-start | bytes 196616 | tf_op jit(solution)/shard_map/ppermute | solution.py:531
  41.3 7.1 %collective-permute-start.5 = (f32[2,8,8,128]{3,2,1,0:T(8,128)S(1)}, f32[2,8,8,128]{3,2,1,0:T(8,128)S(1)}, u32[]{:S(2)}, u32[]{:S(2)}) collective-permute-start(f32[2,8,8,128]{3,2,1,0:T(8,128)S(1)} %get-tuple-element.21), channel_id=1, source_target_pairs={{8,0},{16,8},{24,16},{32,24},{40,32},{48,40},{56,48},{64,56},{72,6... | collective-permute-start | bytes 196616 | tf_op jit(solution)/shard_map/ppermute | solution.py:531
  45.5 4.2 %copy-start.5 = (bf16[2,256,512]{2,1,0:T(8,128)(2,1)S(1)}, bf16[2,256,512]{2,1,0:T(8,128)(2,1)}, u32[]{:S(2)}) copy-start(bf16[2,256,512]{2,1,0:T(8,128)(2,1)} %get-tuple-element.40) | copy-start | bytes 1572868
  45.5 6.2 %copy-start.4 = (bf16[2,256,512]{2,1,0:T(8,128)(2,1)S(1)}, bf16[2,256,512]{2,1,0:T(8,128)(2,1)}, u32[]{:S(2)}) copy-start(bf16[2,256,512]{2,1,0:T(8,128)(2,1)} %get-tuple-element.39) | copy-start | bytes 1572868
  45.5 4.1 %copy-start.7 = (f32[2,8,8,128]{3,2,1,0:T(8,128)}, f32[2,8,8,128]{3,2,1,0:T(8,128)S(1)}, u32[]{:S(2)}) copy-start(f32[2,8,8,128]{3,2,1,0:T(8,128)S(1)} %collective-permute-done.4) | copy-start | bytes 196612
  48.4 1.3 copy-start.8
  49.7 9.8 %copy-start = (s32[4,4,256]{2,1,0:T(4,128)S(1)}, s32[4,4,256]{2,1,0:T(4,128)}, u32[]{:S(2)}) copy-start(s32[4,4,256]{2,1,0:T(4,128)} %nb.3) | copy-start | bytes 49156
  49.8 61.2 %collective-permute-start.6 = (bf16[2,256,1024]{2,1,0:T(8,128)(2,1)S(1)}, bf16[2,256,1024]{2,1,0:T(8,128)(2,1)}, u32[]{:S(2)}, u32[]{:S(2)}) collective-permute-start(bf16[2,256,1024]{2,1,0:T(8,128)(2,1)S(1)} %pad_maximum_fusion.lower), channel_id=1, source_target_pairs={{0,8},{8,16},{16,24},{24,32},{32,40},{40,48},{48,56},{56,64},{64,7... | collective-permute-start | bytes 3145736 | tf_op jit(solution)/shard_map/ppermute | solution.py:531
  52.9 58.1 %collective-permute-start.7 = (bf16[2,256,1024]{2,1,0:T(8,128)(2,1)}, bf16[2,256,1024]{2,1,0:T(8,128)(2,1)}, u32[]{:S(2)}, u32[]{:S(2)}) collective-permute-start(bf16[2,256,1024]{2,1,0:T(8,128)(2,1)} %pad_maximum_fusion.1.upper), channel_id=1, source_target_pairs={{8,0},{16,8},{24,16},{32,24},{40,32},{48,40},{56,48},{64,56},{72,6... | collective-permute-start | bytes 3145736 | tf_op jit(solution)/shard_map/ppermute | solution.py:531
  128.4 25.1 %collective-permute-start.8 = (bf16[2048,256]{1,0:T(8,128)(2,1)}, bf16[2048,256]{1,0:T(8,128)(2,1)S(1)}, u32[]{:S(2)}, u32[]{:S(2)}) collective-permute-start(bf16[2048,256]{1,0:T(8,128)(2,1)} %get-tuple-element.35.w), channel_id=1, source_target_pairs={{0,1},{1,0},{2,3},{3,2},{4,5},{5,4},{6,7},{7,6},{8,9},{9,8},{10,11... | collective-permute-start | bytes 3145736 | tf_op jit(solution)/shard_map/ppermute | solution.py:583
  156.7 15.9 %collective-permute-start.9 = (bf16[1024,256]{1,0:T(8,128)(2,1)S(1)}, bf16[1024,256]{1,0:T(8,128)(2,1)S(1)}, u32[]{:S(2)}, u32[]{:S(2)}) collective-permute-start(bf16[1024,256]{1,0:T(8,128)(2,1)S(1)} %cross_far.3), channel_id=1, source_target_pairs={{0,4},{1,5},{2,6},{3,7},{4,0},{5,1},{6,2},{7,3},{8,12},{9,13},{10,... | collective-permute-start | bytes 1572872 | tf_op jit(solution)/shard_map/ppermute | solution.py:591
  162.7 20.6 %collective-permute-start.10 = (bf16[1024,256]{1,0:T(8,128)(2,1)S(1)}, bf16[1024,256]{1,0:T(8,128)(2,1)S(1)}, u32[]{:S(2)}, u32[]{:S(2)}) collective-permute-start(bf16[1024,256]{1,0:T(8,128)(2,1)S(1)} %cross_far.4), channel_id=1, source_target_pairs={{0,2},{1,3},{2,4},{3,5},{4,6},{5,7},{6,0},{7,1},{8,10},{9,11},{10,... | collective-permute-start | bytes 1572872 | tf_op jit(solution)/shard_map/ppermute | solution.py:591
  166.6 16.8 %collective-permute-start.11 = (bf16[1024,256]{1,0:T(8,128)(2,1)S(1)}, bf16[1024,256]{1,0:T(8,128)(2,1)S(1)}, u32[]{:S(2)}, u32[]{:S(2)}) collective-permute-start(bf16[1024,256]{1,0:T(8,128)(2,1)S(1)} %cross_far.5), channel_id=1, source_target_pairs={{0,6},{1,7},{2,0},{3,1},{4,2},{5,3},{6,4},{7,5},{8,14},{9,15},{10,... | collective-permute-start | bytes 1572872 | tf_op jit(solution)/shard_map/ppermute | solution.py:591
  184.4 15.5 %all-to-all-start.1 = ((bf16[16,64,256]{2,1,0:T(8,128)(2,1)}), bf16[16,64,256]{2,1,0:T(8,128)(2,1)S(1)}, u32[]{:S(2)}, u32[]{:S(2)}) async-start(bf16[16,64,256]{2,1,0:T(8,128)(2,1)} %bitcast.18), calls=%async_computation.1 | async-start | bytes 1048576 | tf_op jit(solution)/shard_map/all_to_all | solution.py:595

commit v5 on v4

--- a/solution.py
+++ b/solution.py
@@ -560,7 +560,7 @@
     spots = spots.reshape(16, 8, 2, 64).transpose(1, 2, 0, 3).reshape(4, 2, 2, 1024)
     band, half = col // 2, col % 2
     spots = lax.dynamic_index_in_dim(spots, half, 1, keepdims=False)
-    spots = jnp.take(spots, (band + jnp.array([2, 1, 3, 0], jnp.int32)) % 4, axis=0)
+    spots = jnp.take(spots, (band + jnp.array([1, 2, 3, 0], jnp.int32)) % 4, axis=0)
     mid_y = (band * 8 + 4).astype(F32)
     tgt = jnp.stack([spots[:, 0] * 4.0 - 2.0, spots[:, 1] * 32.0 - mid_y], 1)
     tgt = tgt.reshape(4, 2, 1024 // TB, TB).transpose(0, 2, 1, 3).reshape(-1, 2, TB)
@@ -584,7 +584,7 @@
     near = cross(scale, tgt, pts, weights, F32, name="cross_near")
     per = 1024 // TB
     parts = []
-    for i, k in enumerate((2, 1, 3)):
+    for i, k in enumerate((1, 2, 3)):
         part = cross(
             scale, tgt[per * i : per * i + per], pts2, weights2, BF, near, per * i, "cross_far", FAR
         )

time: 203 us -> 208 us (1.025)
  waiting for transfers between devices: 34.1 us -> 37.4 us
    ppermute x3, waiting for transfers between devices: 10.8 us -> 14.2 us  [body(): lax.ppermute(part, 'cols', [(c, (c + 2 * k) % 8) for c in range(8)])]
  transfers between devices with their start and end apart: 14 -> 14, of which waited for: 5 -> 6; matrix products, arithmetic and copies ran while one was open for 7% -> 7% of each run, Pallas kernels for 38% -> 37%
where the time goes in v5:
time: 208 us; the launch traced here: 206 us
  Pallas kernels  97.2 us (47%)
  starting transfers between devices  49 us (24%)
  waiting for transfers between devices  37.4 us (18%)
  local copies, waits for them, and re-layouts  14.4 us (7%)
  other arithmetic  6.51 us (3%)
    pallas_call x1, Pallas kernels, factor(): pl.pallas_call(factor_kernel, out_shape=(jax.ShapeDtypeStruct((16, 128, 2...  51.6 us
    pallas_call x5, Pallas kernels, cross(): pl.pallas_call(kernel, grid=(n,), out_shape=jax.ShapeDtypeStruct((n * TB,...  27.2 us
    ppermute x4, starting transfers between devices, sides(): lax.ppermute(high, axis, forward)  18.1 us
    pallas_call x1, Pallas kernels, whiten(): pl.pallas_call(whiten_kernel, grid=(4,), out_shape=(jax.ShapeDtypeStruct(...  17.4 us
    ppermute x3, waiting for transfers between devices, body(): lax.ppermute(part, 'cols', [(c, (c + 2 * k) % 8) for c in range(8)])  14.2 us
    all_to_all x1, starting transfers between devices, body(): lax.all_to_all(everyone, ('rows', 'cols'), split_axis=0, concat_axis=0, t...  11.7 us
    all_to_all x1, waiting for transfers between devices, body(): lax.all_to_all(predicted.reshape(16, 64, 256), 'rows', split_axis=0, conc...  10.5 us
    ppermute x4, starting transfers between devices, sides(): lax.ppermute(low, axis, backward)  8.04 us
  transfers between devices with their start and end apart: 14, of which 6 were waited for; matrix products, arithmetic and copies ran while one was open for 7% of the time, Pallas kernels for 37%

profile of v5, /device:TPU:1, one launch (start us, length us, event | category | flops | bytes accessed | tf_op | source)
XLA Modules:
  0.0 206.3 jit_solution(13109701924346963740)
XLA Ops:
  0.6 0.7 copy.26
  1.4 0.7 pad_maximum_fusion.4
  2.1 1.3 collective-permute-start.3
  3.4 5.0 %collective-permute-start.2 = (f32[4,4,8,128]{3,2,1,0:T(8,128)S(1)}, f32[4,4,8,128]{3,2,1,0:T(8,128)S(1)}, u32[]{:S(2)}, u32[]{:S(2)}) collective-permute-start(f32[4,4,8,128]{3,2,1,0:T(8,128)S(1)} %pad_maximum_fusion.4), channel_id=1, source_target_pairs={{0,1},{1,2},{2,3},{3,4},{4,5},{5,6},{6,7},{8,9},{9,10},{10,11},{11... | collective-permute-start | bytes 196616 | tf_op jit(solution)/shard_map/ppermute | solution.py:531
  8.4 2.5 %reshape.184 = f32[4,256,512]{2,0,1:T(4,128)S(1)} reshape(f32[4,256,4,128]{3,2,0,1:T(4,128)} %bitcast.33) | data formatting | bytes 4194304 | tf_op jit(solution)/shard_map/reshape | solution.py:550
  10.9 0.6 copy.25
  11.5 1.0 fusion.8
  12.5 1.3 collective-permute-start.1
  13.8 5.7 %collective-permute-start = (bf16[4,256,256]{2,1,0:T(8,128)(2,1)}, bf16[4,256,256]{2,1,0:T(8,128)(2,1)}, u32[]{:S(2)}, u32[]{:S(2)}) collective-permute-start(bf16[4,256,256]{2,1,0:T(8,128)(2,1)} %get-tuple-element.42), channel_id=1, source_target_pairs={{0,1},{1,2},{2,3},{3,4},{4,5},{5,6},{6,7},{8,9},{9,10},{10,11},{11... | collective-permute-start | bytes 1572872 | tf_op jit(solution)/shard_map/ppermute | solution.py:531
  19.5 2.3 %copy.22.own = f32[4,256,512]{2,1,0:T(8,128)S(1)} copy(f32[4,256,512]{2,0,1:T(4,128)} %copy-done.3) | data formatting | bytes 4194304 | tf_op jit(solution)/shard_map/reshape | solution.py:550
  21.8 1.0 fusion.7
  23.1 1.0 sort_targets.1
  24.1 11.7 %all-to-all-start = ((f32[128,1,128]{2,1,0:T(1,128)}), f32[128,1,128]{2,1,0:T(1,128)S(1)}, u32[]{:S(2)}, u32[]{:S(2)}) async-start(f32[128,1,128]{2,1,0:T(1,128)} %bitcast.7), calls=%async_computation | async-start | bytes 131072 | tf_op jit(solution)/shard_map/all_to_all | solution.py:556
  35.8 5.4 %collective-permute-start.4 = (f32[2,8,8,128]{3,2,1,0:T(8,128)S(1)}, f32[2,8,8,128]{3,2,1,0:T(8,128)S(1)}, u32[]{:S(2)}, u32[]{:S(2)}) collective-permute-start(f32[2,8,8,128]{3,2,1,0:T(8,128)S(1)} %get-tuple-element.20), channel_id=1, source_target_pairs={{0,8},{8,16},{16,24},{24,32},{32,40},{40,48},{48,56},{56,64},{64,7... | collective-permute-start | bytes 196616 | tf_op jit(solution)/shard_map/ppermute | solution.py:531
  41.3 1.9 collective-permute-start.5
  43.3 2.3 %all-to-all-done = f32[128,1,128]{2,1,0:T(1,128)S(1)} async-done(((f32[128,1,128]{2,1,0:T(1,128)}), f32[128,1,128]{2,1,0:T(1,128)S(1)}, u32[]{:S(2)}, u32[]{:S(2)}) %all-to-all-start) | async-done | bytes 65568 | tf_op jit(solution)/shard_map/all_to_all | solution.py:556
  45.5 2.8 %collective-permute-done.5 = f32[2,8,8,128]{3,2,1,0:T(8,128)S(1)} collective-permute-done((f32[2,8,8,128]{3,2,1,0:T(8,128)S(1)}, f32[2,8,8,128]{3,2,1,0:T(8,128)S(1)}, u32[]{:S(2)}, u32[]{:S(2)}) %collective-permute-start.5) | collective-permute-done | bytes 65568 | tf_op jit(solution)/shard_map/ppermute | solution.py:531
  48.4 1.3 fusion.9
  49.7 0.1 pad_maximum_fusion.lower
  49.8 1.9 collective-permute-start.6
  51.8 1.1 pad_maximum_fusion.1.upper
  52.9 3.5 %collective-permute-start.7 = (bf16[2,256,1024]{2,1,0:T(8,128)(2,1)}, bf16[2,256,1024]{2,1,0:T(8,128)(2,1)}, u32[]{:S(2)}, u32[]{:S(2)}) collective-permute-start(bf16[2,256,1024]{2,1,0:T(8,128)(2,1)} %pad_maximum_fusion.1.upper), channel_id=1, source_target_pairs={{8,0},{16,8},{24,16},{32,24},{40,32},{48,40},{56,48},{64,56},{72,6... | collective-permute-start | bytes 3145736 | tf_op jit(solution)/shard_map/ppermute | solution.py:531
  56.4 0.5 iota_add_fusion
  57.8 0.7 add.146
  58.5 0.9 pad_maximum_fusion.2.geo
  59.4 51.6 %factor.1 = (bf16[16,128,256]{2,1,0:T(8,128)(2,1)S(1)}, f32[16,128,128]{2,1,0:T(8,128)S(1)}) custom-call(s32[2]{0:T(128)S(1)} %pad_add_fusion.first, f32[1]{0:T(128)S(6)} %copy.27.length, s32[4,4,256]{2,1,0:T(4,128)S(1)} %copy-done, f32[8,8,8,128]{3,2,1,0:T(8,128)S(1)} %pad_maximum_fusion.2.geo), custom_call_target="tpu_custom_call" | custom-call | tf_op jit(solution)/shard_map/factor/pallas_call | solution.py:299
  111.0 17.4 %whiten.1 = (f32[16,128,256]{2,1,0:T(8,128)}, bf16[2048,256]{1,0:T(8,128)(2,1)}, f32[4,8,128]{2,1,0:T(8,128)S(1)}) custom-call(s32[2]{0:T(128)S(1)} %pad_add_fusion.first, s32[4,4,256]{2,1,0:T(4,128)S(1)} %copy-done, bf16[2,256,1024]{2,1,0:T(8,128)(2,1)} %collective-permute-done.6.north, bf16[2,256,1024]{2,1,0:T(8,128)(2,1)} %pad_maximum_fusion.1.upper, ...), custom_call_target="tpu_custom_call" | custom-call | tf_op jit(solution)/shard_map/whiten/pallas_call | solution.py:381
  128.4 0.6 collective-permute-start.8
  129.1 0.5 broadcast.93
  129.6 0.8 reduce.5
  130.8 0.6 gather_fusion
  131.6 14.2 %cross_near.1.refs_4_ = f32[4096,256]{1,0:T(8,128)S(1)} custom-call(f32[1]{0:T(128)S(6)} %div.12.s.refs_0_, f32[4,2,1024]{2,1,0:T(2,128)S(1)} %pad_maximum_fusion.5.t, f32[2,2048]{1,0:T(2,128)S(1)} %pad_maximum_fusion.7.p, bf16[2048,256]{1,0:T(8,128)(2,1)} %get-tuple-element.35.w), custom_call_target="tpu_custom_call" | custom-call | tf_op jit(solution)/shard_map/cross_near/pallas_call | solution.py:472
  145.8 7.7 %collective-permute-done.8.refs_3_ = bf16[2048,256]{1,0:T(8,128)(2,1)S(1)} collective-permute-done((bf16[2048,256]{1,0:T(8,128)(2,1)}, bf16[2048,256]{1,0:T(8,128)(2,1)S(1)}, u32[]{:S(2)}, u32[]{:S(2)}) %collective-permute-start.8) | collective-permute-done | bytes 1048608 | tf_op jit(solution)/shard_map/ppermute | solution.py:583
  153.5 3.2 %cross_far.3 = bf16[1024,256]{1,0:T(8,128)(2,1)S(1)} custom-call(f32[1]{0:T(128)S(6)} %div.12.s.refs_0_, f32[1,2,1024]{2,1,0:T(2,128)S(1)} %get-tuple-element.51.refs_1_, f32[2,2048]{1,0:T(2,128)S(1)} %pad_maximum_fusion.6.refs_2_, bf16[2048,256]{1,0:T(8,128)(2,1)S(1)} %collective-permute-done.8.refs_3_, f32[4096,256]{1,0:T(8,128)S(1)} %cross_near.1.refs_4_), custom_call_target="tpu_custom_call" | custom-call | tf_op jit(solution)/shard_map/cross_far/pallas_call | solution.py:472
  156.7 1.3 collective-permute-start.9
  158.0 3.2 %cross_far.4 = bf16[1024,256]{1,0:T(8,128)(2,1)S(1)} custom-call(f32[1]{0:T(128)S(6)} %div.12.s.refs_0_, f32[1,2,1024]{2,1,0:T(2,128)S(1)} %get-tuple-element.53.refs_1_, f32[2,2048]{1,0:T(2,128)S(1)} %pad_maximum_fusion.6.refs_2_, bf16[2048,256]{1,0:T(8,128)(2,1)S(1)} %collective-permute-done.8.refs_3_, f32[4096,256]{1,0:T(8,128)S(1)} %cross_near.1.refs_4_), custom_call_target="tpu_custom_call" | custom-call | tf_op jit(solution)/shard_map/cross_far/pallas_call | solution.py:472
  161.1 2.9 %collective-permute-start.10 = (bf16[1024,256]{1,0:T(8,128)(2,1)S(1)}, bf16[1024,256]{1,0:T(8,128)(2,1)S(1)}, u32[]{:S(2)}, u32[]{:S(2)}) collective-permute-start(bf16[1024,256]{1,0:T(8,128)(2,1)S(1)} %cross_far.4), channel_id=1, source_target_pairs={{0,4},{1,5},{2,6},{3,7},{4,0},{5,1},{6,2},{7,3},{8,12},{9,13},{10,... | collective-permute-start | bytes 1572872 | tf_op jit(solution)/shard_map/ppermute | solution.py:591
  164.0 3.2 %cross_far.5 = bf16[1024,256]{1,0:T(8,128)(2,1)S(1)} custom-call(f32[1]{0:T(128)S(6)} %div.12.s.refs_0_, f32[1,2,1024]{2,1,0:T(2,128)S(1)} %get-tuple-element.54.refs_1_, f32[2,2048]{1,0:T(2,128)S(1)} %pad_maximum_fusion.6.refs_2_, bf16[2048,256]{1,0:T(8,128)(2,1)S(1)} %collective-permute-done.8.refs_3_, f32[4096,256]{1,0:T(8,128)S(1)} %cross_near.1.refs_4_), custom_call_target="tpu_custom_call" | custom-call | tf_op jit(solution)/shard_map/cross_far/pallas_call | solution.py:472
  167.2 1.2 collective-permute-start.11
  168.4 3.5 %cross_here.1 = f32[1024,256]{1,0:T(8,128)S(1)} custom-call(f32[1]{0:T(128)S(6)} %div.12.s.refs_0_, f32[1,2,1024]{2,1,0:T(2,128)S(1)} %get-tuple-element.52.refs_1_, f32[2,2048]{1,0:T(2,128)S(1)} %pad_maximum_fusion.6.refs_2_, bf16[2048,256]{1,0:T(8,128)(2,1)S(1)} %collective-permute-done.8.refs_3_, f32[4096,256]{1,0:T(8,128)S(1)} %cross_near.1.refs_4_), custom_call_target="tpu_custom_call" | custom-call | tf_op jit(solution)/shard_map/cross_here/pallas_call | solution.py:472
  171.9 11.5 %collective-permute-done.10 = bf16[1024,256]{1,0:T(8,128)(2,1)S(1)} collective-permute-done((bf16[1024,256]{1,0:T(8,128)(2,1)S(1)}, bf16[1024,256]{1,0:T(8,128)(2,1)S(1)}, u32[]{:S(2)}, u32[]{:S(2)}) %collective-permute-start.10) | collective-permute-done | bytes 524320 | tf_op jit(solution)/shard_map/ppermute | solution.py:591
  183.4 2.7 %collective-permute-done.11 = bf16[1024,256]{1,0:T(8,128)(2,1)S(1)} collective-permute-done((bf16[1024,256]{1,0:T(8,128)(2,1)S(1)}, bf16[1024,256]{1,0:T(8,128)(2,1)S(1)}, u32[]{:S(2)}, u32[]{:S(2)}) %collective-permute-start.11) | collective-permute-done | bytes 524320 | tf_op jit(solution)/shard_map/ppermute | solution.py:591
  186.1 1.1 multiply_convert_fusion
  187.1 5.2 %all-to-all-start.1 = ((bf16[16,64,256]{2,1,0:T(8,128)(2,1)}), bf16[16,64,256]{2,1,0:T(8,128)(2,1)S(1)}, u32[]{:S(2)}, u32[]{:S(2)}) async-start(bf16[16,64,256]{2,1,0:T(8,128)(2,1)} %bitcast.18), calls=%async_computation.1 | async-start | bytes 1048576 | tf_op jit(solution)/shard_map/all_to_all | solution.py:595
  192.4 0.7 slice_reduce_fusion
  193.1 10.5 %all-to-all-done.1 = bf16[16,64,256]{2,1,0:T(8,128)(2,1)S(1)} async-done(((bf16[16,64,256]{2,1,0:T(8,128)(2,1)}), bf16[16,64,256]{2,1,0:T(8,128)(2,1)S(1)}, u32[]{:S(2)}, u32[]{:S(2)}) %all-to-all-start.1) | async-done | bytes 524320 | tf_op jit(solution)/shard_map/all_to_all | solution.py:595
  203.5 1.9 gather_fusion.1
  205.5 0.8 convert_element_type.32
  (59 shorter events, 1.0 us)
Async XLA Ops:
  2.1 20.8 %collective-permute-start.3 = (f32[4,4,8,128]{3,2,1,0:T(8,128)S(1)}, f32[4,4,8,128]{3,2,1,0:T(8,128)S(1)}, u32[]{:S(2)}, u32[]{:S(2)}) collective-permute-start(f32[4,4,8,128]{3,2,1,0:T(8,128)S(1)} %pad_maximum_fusion.4), channel_id=1, source_target_pairs={{1,0},{2,1},{3,2},{4,3},{5,4},{6,5},{7,6},{9,8},{10,9},{11,10},{12... | collective-permute-start | bytes 196616 | tf_op jit(solution)/shard_map/ppermute | solution.py:531
  3.4 19.6 %collective-permute-start.2 = (f32[4,4,8,128]{3,2,1,0:T(8,128)S(1)}, f32[4,4,8,128]{3,2,1,0:T(8,128)S(1)}, u32[]{:S(2)}, u32[]{:S(2)}) collective-permute-start(f32[4,4,8,128]{3,2,1,0:T(8,128)S(1)} %pad_maximum_fusion.4), channel_id=1, source_target_pairs={{0,1},{1,2},{2,3},{3,4},{4,5},{5,6},{6,7},{8,9},{9,10},{10,11},{11... | collective-permute-start | bytes 196616 | tf_op jit(solution)/shard_map/ppermute | solution.py:531
  10.9 1.7 copy-start.3
  10.9 8.6 %copy-start.9 = (f32[2,4,4,128]{3,2,1,0:T(4,128)S(1)}, f32[2,4,4,128]{3,2,1,0:T(4,128)}, u32[]{:S(2)}) copy-start(f32[2,4,4,128]{3,2,1,0:T(4,128)} %param.9) | copy-start | bytes 49156
  12.5 35.8 %collective-permute-start.1 = (bf16[4,256,256]{2,1,0:T(8,128)(2,1)}, bf16[4,256,256]{2,1,0:T(8,128)(2,1)}, u32[]{:S(2)}, u32[]{:S(2)}) collective-permute-start(bf16[4,256,256]{2,1,0:T(8,128)(2,1)} %get-tuple-element.41), channel_id=1, source_target_pairs={{1,0},{2,1},{3,2},{4,3},{5,4},{6,5},{7,6},{9,8},{10,9},{11,10},{12... | collective-permute-start | bytes 1572872 | tf_op jit(solution)/shard_map/ppermute | solution.py:531
  13.8 34.5 %collective-permute-start = (bf16[4,256,256]{2,1,0:T(8,128)(2,1)}, bf16[4,256,256]{2,1,0:T(8,128)(2,1)}, u32[]{:S(2)}, u32[]{:S(2)}) collective-permute-start(bf16[4,256,256]{2,1,0:T(8,128)(2,1)} %get-tuple-element.42), channel_id=1, source_target_pairs={{0,1},{1,2},{2,3},{3,4},{4,5},{5,6},{6,7},{8,9},{9,10},{10,11},{11... | collective-permute-start | bytes 1572872 | tf_op jit(solution)/shard_map/ppermute | solution.py:531
  21.8 1.1 copy-start.10
  21.8 1.2 copy-start.6
  21.8 1.2 copy-start.1
  21.8 1.2 copy-start.2
  24.1 21.4 %all-to-all-start = ((f32[128,1,128]{2,1,0:T(1,128)}), f32[128,1,128]{2,1,0:T(1,128)S(1)}, u32[]{:S(2)}, u32[]{:S(2)}) async-start(f32[128,1,128]{2,1,0:T(1,128)} %bitcast.7), calls=%async_computation | async-start | bytes 131072 | tf_op jit(solution)/shard_map/all_to_all | solution.py:556
  35.8 9.7 %collective-permute-start.4 = (f32[2,8,8,128]{3,2,1,0:T(8,128)S(1)}, f32[2,8,8,128]{3,2,1,0:T(8,128)S(1)}, u32[]{:S(2)}, u32[]{:S(2)}) collective-permute-start(f32[2,8,8,128]{3,2,1,0:T(8,128)S(1)} %get-tuple-element.20), channel_id=1, source_target_pairs={{0,8},{8,16},{16,24},{24,32},{32,40},{40,48},{48,56},{56,64},{64,7... | collective-permute-start | bytes 196616 | tf_op jit(solution)/shard_map/ppermute | solution.py:531
  41.3 7.1 %collective-permute-start.5 = (f32[2,8,8,128]{3,2,1,0:T(8,128)S(1)}, f32[2,8,8,128]{3,2,1,0:T(8,128)S(1)}, u32[]{:S(2)}, u32[]{:S(2)}) collective-permute-start(f32[2,8,8,128]{3,2,1,0:T(8,128)S(1)} %get-tuple-element.21), channel_id=1, source_target_pairs={{8,0},{16,8},{24,16},{32,24},{40,32},{48,40},{56,48},{64,56},{72,6... | collective-permute-start | bytes 196616 | tf_op jit(solution)/shard_map/ppermute | solution.py:531
  45.5 4.2 %copy-start.5 = (bf16[2,256,512]{2,1,0:T(8,128)(2,1)S(1)}, bf16[2,256,512]{2,1,0:T(8,128)(2,1)}, u32[]{:S(2)}) copy-start(bf16[2,256,512]{2,1,0:T(8,128)(2,1)} %get-tuple-element.40) | copy-start | bytes 1572868
  45.5 6.2 %copy-start.4 = (bf16[2,256,512]{2,1,0:T(8,128)(2,1)S(1)}, bf16[2,256,512]{2,1,0:T(8,128)(2,1)}, u32[]{:S(2)}) copy-start(bf16[2,256,512]{2,1,0:T(8,128)(2,1)} %get-tuple-element.39) | copy-start | bytes 1572868
  45.5 4.1 %copy-start.7 = (f32[2,8,8,128]{3,2,1,0:T(8,128)}, f32[2,8,8,128]{3,2,1,0:T(8,128)S(1)}, u32[]{:S(2)}) copy-start(f32[2,8,8,128]{3,2,1,0:T(8,128)S(1)} %collective-permute-done.4) | copy-start | bytes 196612
  48.4 1.3 copy-start.8
  49.7 9.8 %copy-start = (s32[4,4,256]{2,1,0:T(4,128)S(1)}, s32[4,4,256]{2,1,0:T(4,128)}, u32[]{:S(2)}) copy-start(s32[4,4,256]{2,1,0:T(4,128)} %nb.3) | copy-start | bytes 49156
  49.8 61.2 %collective-permute-start.6 = (bf16[2,256,1024]{2,1,0:T(8,128)(2,1)S(1)}, bf16[2,256,1024]{2,1,0:T(8,128)(2,1)}, u32[]{:S(2)}, u32[]{:S(2)}) collective-permute-start(bf16[2,256,1024]{2,1,0:T(8,128)(2,1)S(1)} %pad_maximum_fusion.lower), channel_id=1, source_target_pairs={{0,8},{8,16},{16,24},{24,32},{32,40},{40,48},{48,56},{56,64},{64,7... | collective-permute-start | bytes 3145736 | tf_op jit(solution)/shard_map/ppermute | solution.py:531
  52.9 58.1 %collective-permute-start.7 = (bf16[2,256,1024]{2,1,0:T(8,128)(2,1)}, bf16[2,256,1024]{2,1,0:T(8,128)(2,1)}, u32[]{:S(2)}, u32[]{:S(2)}) collective-permute-start(bf16[2,256,1024]{2,1,0:T(8,128)(2,1)} %pad_maximum_fusion.1.upper), channel_id=1, source_target_pairs={{8,0},{16,8},{24,16},{32,24},{40,32},{48,40},{56,48},{64,56},{72,6... | collective-permute-start | bytes 3145736 | tf_op jit(solution)/shard_map/ppermute | solution.py:531
  128.4 25.1 %collective-permute-start.8 = (bf16[2048,256]{1,0:T(8,128)(2,1)}, bf16[2048,256]{1,0:T(8,128)(2,1)S(1)}, u32[]{:S(2)}, u32[]{:S(2)}) collective-permute-start(bf16[2048,256]{1,0:T(8,128)(2,1)} %get-tuple-element.35.w), channel_id=1, source_target_pairs={{0,1},{1,0},{2,3},{3,2},{4,5},{5,4},{6,7},{7,6},{8,9},{9,8},{10,11... | collective-permute-start | bytes 3145736 | tf_op jit(solution)/shard_map/ppermute | solution.py:583
  156.7 15.2 %collective-permute-start.9 = (bf16[1024,256]{1,0:T(8,128)(2,1)S(1)}, bf16[1024,256]{1,0:T(8,128)(2,1)S(1)}, u32[]{:S(2)}, u32[]{:S(2)}) collective-permute-start(bf16[1024,256]{1,0:T(8,128)(2,1)S(1)} %cross_far.3), channel_id=1, source_target_pairs={{0,2},{1,3},{2,4},{3,5},{4,6},{5,7},{6,0},{7,1},{8,10},{9,11},{10,... | collective-permute-start | bytes 1572872 | tf_op jit(solution)/shard_map/ppermute | solution.py:591
  161.1 22.2 %collective-permute-start.10 = (bf16[1024,256]{1,0:T(8,128)(2,1)S(1)}, bf16[1024,256]{1,0:T(8,128)(2,1)S(1)}, u32[]{:S(2)}, u32[]{:S(2)}) collective-permute-start(bf16[1024,256]{1,0:T(8,128)(2,1)S(1)} %cross_far.4), channel_id=1, source_target_pairs={{0,4},{1,5},{2,6},{3,7},{4,0},{5,1},{6,2},{7,3},{8,12},{9,13},{10,... | collective-permute-start | bytes 1572872 | tf_op jit(solution)/shard_map/ppermute | solution.py:591
  167.2 18.9 %collective-permute-start.11 = (bf16[1024,256]{1,0:T(8,128)(2,1)S(1)}, bf16[1024,256]{1,0:T(8,128)(2,1)S(1)}, u32[]{:S(2)}, u32[]{:S(2)}) collective-permute-start(bf16[1024,256]{1,0:T(8,128)(2,1)S(1)} %cross_far.5), channel_id=1, source_target_pairs={{0,6},{1,7},{2,0},{3,1},{4,2},{5,3},{6,4},{7,5},{8,14},{9,15},{10,... | collective-permute-start | bytes 1572872 | tf_op jit(solution)/shard_map/ppermute | solution.py:591
  187.1 16.4 %all-to-all-start.1 = ((bf16[16,64,256]{2,1,0:T(8,128)(2,1)}), bf16[16,64,256]{2,1,0:T(8,128)(2,1)S(1)}, u32[]{:S(2)}, u32[]{:S(2)}) async-start(bf16[16,64,256]{2,1,0:T(8,128)(2,1)} %bitcast.18), calls=%async_computation.1 | async-start | bytes 1048576 | tf_op jit(solution)/shard_map/all_to_all | solution.py:595
